TPU v7x, 256 devices: a whole 4x4x8 slice. The times are simulated.
256 devices in a mesh: ctx: 32 (over x, y, z_lo), tp: 8 (over z_hi, core).
Axes of the slice: x: 4, y: 4, z: 8 (z_hi: 4, z_lo: 2; z = z_hi * 2 + z_lo), core: 2. Of those that a mesh axis runs over, the one named last changes fastest.
Arguments:
- query_rows: bfloat16 [4096, 8192], P('ctx', 'tp'), may hold values from -24 to 24
- key_rows: bfloat16 [4096, 1024], P('ctx', 'tp'), may hold values from -24 to 24
- value_rows: bfloat16 [4096, 1024], P('ctx', 'tp'), may hold values from -6 to 6
- out_grad: bfloat16 [4096, 8192], P(('ctx', 'tp')), may hold values from -6 to 6
- segment_ids: int32 [4096], replicated, may hold values from 0 to 2, as said below
- span_order: int32 [64], replicated, may hold values from 0 to 63, as said below
Outputs:
- attn_out: bfloat16 [4096, 8192], P(('ctx', 'tp'))
- query_grad: bfloat16 [4096, 8192], P('ctx', 'tp')
- key_grad: bfloat16 [4096, 1024], P('ctx', 'tp')
- value_grad: bfloat16 [4096, 1024], P('ctx', 'tp')
Inputs may be any that keep to these rules, and one draw needn't show every extreme that they name: `segment_ids`: never falling: a nonempty prompt labelled 0 from position 0, then a nonempty chosen response labelled 1, then a nonempty rejected response labelled 2. `span_order`: each block number once; entries 2 j and 2 j + 1 sum to 63.
All inputs are finite; a program needn't handle non-finite values.
Results may differ from a plain program's by a relative error of at most 0.033.
Values may be sent and summed in bfloat16 or wider, within the bound.
A program may use at most 64 MiB of HBM per device.

v0:
```python
import math

import jax
import jax.numpy as jnp
from jax import lax
from jax.sharding import PartitionSpec as P

HEAD_DIM = 128
SPAN = 64


def fetch_grad(out_grad):
    return lax.all_to_all(out_grad, "tp", split_axis=1, concat_axis=0, tiled=True)


def spread_output(attn_flat):
    return lax.all_to_all(attn_flat, "tp", split_axis=0, concat_axis=1, tiled=True)


def on_device(query_rows, key_rows, value_rows, out_grad, segment_ids, span_order):
    ctx_size = lax.axis_size("ctx")
    ctx_index = lax.axis_index("ctx")
    local_rows = query_rows.shape[0]
    heads_here = query_rows.shape[1] // HEAD_DIM
    groups_here = key_rows.shape[1] // HEAD_DIM
    ratio = heads_here // groups_here
    total_rows = local_rows * ctx_size
    width = groups_here * HEAD_DIM
    scale = 1.0 / math.sqrt(HEAD_DIM)
    all_rows = jnp.arange(total_rows, dtype=jnp.int32)
    positions = SPAN * jnp.take(span_order, all_rows // SPAN) + all_rows % SPAN
    labels = jnp.take(segment_ids, positions)
    own_start = ctx_index * local_rows
    own_pos = lax.dynamic_slice_in_dim(positions, own_start, local_rows, 0)
    own_label = lax.dynamic_slice_in_dim(labels, own_start, local_rows, 0)
    block = math.gcd(total_rows, 512)
    blocks = total_rows // block
    queries4 = query_rows.reshape(local_rows, groups_here, ratio, HEAD_DIM)
    grad_rows = None
    keys_all, values_all = (
        lax.all_gather(key_rows, "ctx", axis=0, tiled=True),
        lax.all_gather(value_rows, "ctx", axis=0, tiled=True),
    )
    keys_all = keys_all.reshape(total_rows, groups_here, HEAD_DIM)
    values_all = values_all.reshape(total_rows, groups_here, HEAD_DIM)

    def block_inputs(start, size):
        key_block = lax.dynamic_slice_in_dim(keys_all, start, size, 0)
        value_block = lax.dynamic_slice_in_dim(values_all, start, size, 0)
        pos_block = lax.dynamic_slice_in_dim(positions, start, size, 0)
        label_block = lax.dynamic_slice_in_dim(labels, start, size, 0)
        visible = (pos_block[None, :] <= own_pos[:, None]) & (
            (label_block[None, :] == 0) | (label_block[None, :] == own_label[:, None])
        )
        scores = (
            jnp.einsum("rgjd,cgd->gjrc", queries4, key_block, preferred_element_type=jnp.float32)
            * scale
        )
        scores = jnp.where(visible[None, None], scores, -jnp.inf)
        return (scores, visible, key_block, value_block)

    def sum_step(index, carry):
        running, total, summed = carry
        scores, visible, key_block, value_block = block_inputs(
            (index * block).astype(jnp.int32), block
        )
        new_max = jnp.maximum(running, jnp.max(scores, axis=-1, keepdims=True))
        shift = jnp.where(new_max == -jnp.inf, 0.0, new_max)
        factor = jnp.exp(running - shift)
        weights = jnp.where(visible[None, None], jnp.exp(scores - shift), 0.0)
        total = total * factor + jnp.sum(weights, axis=-1, keepdims=True)
        summed = summed * jnp.transpose(factor, (2, 0, 1, 3)) + jnp.einsum(
            "gjrc,cgd->rgjd",
            weights.astype(jnp.bfloat16),
            value_block,
            preferred_element_type=jnp.float32,
        )
        return (new_max, total, summed)

    start_max = jnp.full((groups_here, ratio, local_rows, 1), -jnp.inf, jnp.float32)
    start_total = jnp.zeros((groups_here, ratio, local_rows, 1), jnp.float32)
    start_summed = jnp.zeros((local_rows, groups_here, ratio, HEAD_DIM), jnp.float32)
    row_max, total, summed = lax.fori_loop(
        0, blocks, sum_step, (start_max, start_total, start_summed)
    )
    attn_local = (summed / jnp.transpose(total, (2, 0, 1, 3))).astype(jnp.bfloat16)
    attn_flat = attn_local.reshape(local_rows, heads_here * HEAD_DIM)
    attn_spread = None
    grad_rows = fetch_grad(out_grad)
    grads4 = grad_rows.reshape(local_rows, groups_here, ratio, HEAD_DIM)
    delta = jnp.sum(grads4.astype(jnp.float32) * attn_local.astype(jnp.float32), axis=-1)
    delta = jnp.transpose(delta, (1, 2, 0))[..., None]

    def score_grads(start, size):
        scores, visible, key_block, value_block = block_inputs(start, size)
        weights = jnp.where(visible[None, None], jnp.exp(scores - row_max), 0.0)
        probs = weights / total
        probs_b = probs.astype(jnp.bfloat16)
        dprob = jnp.einsum(
            "rgjd,cgd->gjrc", grads4, value_block, preferred_element_type=jnp.float32
        )
        dscore_b = (probs * (dprob - delta)).astype(jnp.bfloat16)
        return (probs_b, dscore_b, key_block)

    def kv_terms(probs_b, dscore_b, size):
        key_term = (
            jnp.einsum("gjrc,rgjd->cgd", dscore_b, queries4, preferred_element_type=jnp.float32)
            * scale
        )
        value_term = jnp.einsum(
            "gjrc,rgjd->cgd", probs_b, grads4, preferred_element_type=jnp.float32
        )
        return jnp.concatenate(
            [key_term.reshape(size, width), value_term.reshape(size, width)], axis=1
        )

    start_query = jnp.zeros((local_rows, groups_here, ratio, HEAD_DIM), jnp.float32)

    def grad_step(query_acc, index):
        probs_b, dscore_b, key_block = score_grads(index * block, block)
        query_acc = query_acc + jnp.einsum(
            "gjrc,cgd->rgjd", dscore_b, key_block, preferred_element_type=jnp.float32
        )
        return (query_acc, kv_terms(probs_b, dscore_b, block))

    query_acc, term_blocks = lax.scan(grad_step, start_query, jnp.arange(blocks, dtype=jnp.int32))
    terms = term_blocks.reshape(total_rows, 2 * width)
    reduced = lax.psum_scatter(terms, "ctx", scatter_dimension=0, tiled=True)
    key_grad = reduced[:, :width].astype(jnp.bfloat16)
    value_grad = reduced[:, width:].astype(jnp.bfloat16)
    query_grad = (query_acc * scale).astype(jnp.bfloat16).reshape(local_rows, heads_here * HEAD_DIM)
    attn_spread = spread_output(attn_flat)
    return (attn_spread, query_grad, key_grad, value_grad)


def solution(mesh):
    placed = (P("ctx", "tp"), P("ctx", "tp"), P("ctx", "tp"), P(("ctx", "tp"), None), P(), P())
    return jax.shard_map(
        on_device,
        mesh=mesh,
        in_specs=placed,
        out_specs=(P(("ctx", "tp"), None), P("ctx", "tp"), P("ctx", "tp"), P("ctx", "tp")),
        check_vma=False,
    )
```

profile of v0, /device:TPU:16, one launch (start us, length us, event | category | flops | bytes accessed | tf_op | source)
XLA Modules:
  0.0 596.8 jit_solution(17384996602906757508)
XLA Ops:
  7.9 1.7 copy.92
  9.6 8.5 %all-to-all-start.1 = ((bf16[16,8,1024]{2,0,1:T(8,128)(2,1)}), bf16[16,8,1024]{2,0,1:T(8,128)(2,1)S(1)}, u32[]{:S(2)}, u32[]{:S(2)}) async-start(bf16[16,8,1024]{2,0,1:T(8,128)(2,1)} %bitcast.216), calls=%async_computation.1 | async-start | bytes 524288 | tf_op jit(solution)/shard_map/all_to_all | solution.py:13
  23.9 2.1 fusion.62
  25.9 2.1 fusion.63
  28.0 2.1 fusion.64
  30.1 4.4 compare_select_fusion.3
  34.5 35.9 %select_select_fusion = s32[4096]{0:T(1024)S(1)} fusion(pred[4096]{0:T(1024)(128)(4,1)S(1)} %compare_reduce_fusion, pred[4096]{0:T(1024)(128)(4,1)S(1)} %compare_reduce_fusion.1, pred[4096]{0:T(1024)(128)(4,1)S(1)} %compare_reduce_fusion.2, pred[4096]{0:T(1024)(128)(4,1)S(1)} %compare_reduce_fusion.3, pred[4096]{0:T(1024)(128)(4,1)S(1)} %compare_reduce_fusion.4, ...), kind=kLoop, calls=%fused_computation.160 | loop fusion | flops 233472 | bytes 266468 | tf_op jit(solution)/shard_map/jit(_take)/gather | solution.py:31
  70.6 23.0 %gather_fusion = s32[4096]{0:T(1024)S(1)} fusion(s32[4096]{0:T(1024)S(1)} %copy-done, s32[4096]{0:T(1024)S(1)} %broadcast_clamp_fusion), kind=kCustom, calls=%fused_computation | custom fusion | bytes 49152 | tf_op jit(solution)/shard_map/jit(_take)/gather | solution.py:32
  94.5 66.2 %all-gather.3.cloned.1.call-done = bf16[4096,128]{1,0:T(8,128)(2,1)} async-done(((bf16[128,128]{1,0:T(8,128)(2,1)}), bf16[4096,128]{1,0:T(8,128)(2,1)}) %all-gather.3.cloned.1.call-update) | async-done | bytes 1048592 | tf_op jit(solution)/shard_map/all_gather | solution.py:41
  160.6 155.9 %all-gather.5.cloned.1.call-done = bf16[4096,128]{1,0:T(8,128)(2,1)} async-done(((bf16[128,128]{1,0:T(8,128)(2,1)}), bf16[4096,128]{1,0:T(8,128)(2,1)}) %all-gather.5.cloned.1.call-update) | async-done | bytes 1048592 | tf_op jit(solution)/shard_map/all_gather | solution.py:42
  316.5 32.4 %while.31 = (s32[]{:T(128)}, f32[1,8,128,1]{2,1,3,0:T(8,128)S(1)}, f32[1,8,128,1]{2,1,3,0:T(8,128)S(1)}, f32[128,1,8,128]{0,3,2,1:T(8,128)S(1)}, s32[4096]{0:T(1...) while((s32[]{:T(128)}, f32[1,8,128,1]{2,1,3,0:T(8,128)S(1)}, ...), condition=%wide.region_3.4_spmd.clone, body=%wide.region_0.0_spmd.clone.sunk | while | flops 275919360 | bytes 8214751 | solution.py:83
  318.8 1.7 fusion.95
  322.9 1.7 fusion.95
  326.9 1.7 fusion.95
  331.0 1.7 fusion.95
  335.0 1.7 fusion.95
  339.1 1.7 fusion.95
  343.1 1.7 fusion.95
  347.2 1.7 fusion.95
  349.6 63.9 %while.32 = (s32[]{:T(128)}, f32[128,1,8,128]{0,3,2,1:T(8,128)S(1)}, f32[8,512,256]{2,1,0:T(8,128)}, s32[8]{0:T(128)S(1)}, bf16[4096,1,128]{2,0,1:T(8,128)(2,1)}...) while((s32[]{:T(128)}, ...), condition=%wide.region_6.7_spmd.clone, body=%wide.region_5.6_spmd.clone.sunk | while | flops 676528640 | bytes 15755537 | solution.py:126
  359.3 1.6 fusion.106
  414.4 6.3 %all-to-all-start = ((bf16[8,16,1024]{2,1,0:T(8,128)(2,1)}), bf16[8,16,1024]{2,1,0:T(8,128)(2,1)S(1)}, u32[]{:S(2)}, u32[]{:S(2)}) async-start(bf16[8,16,1024]{2,1,0:T(8,128)(2,1)} %all_to_all.26), calls=%async_computation | async-start | bytes 524288 | tf_op jit(solution)/shard_map/all_to_all | solution.py:17
  421.6 11.8 %all-to-all-done = bf16[8,16,1024]{2,1,0:T(8,128)(2,1)S(1)} async-done(((bf16[8,16,1024]{2,1,0:T(8,128)(2,1)}), bf16[8,16,1024]{2,1,0:T(8,128)(2,1)S(1)}, u32[]{:S(2)}, u32[]{:S(2)}) %all-to-all-start) | async-done | bytes 262176 | tf_op jit(solution)/shard_map/all_to_all | solution.py:17
  434.2 154.5 %reduce-scatter.2.cloned.1.call-done = f32[128,256]{1,0:T(8,128)} async-done(((f32[4096,256]{1,0:T(8,128)}), f32[128,256]{1,0:T(8,128)}) %reduce-scatter.2.cloned.1.call-update) | async-done | bytes 131088 | tf_op jit(solution)/shard_map/reduce_scatter | solution.py:128
  (261 shorter events, 87.2 us)
Async XLA Ops:
  7.2 63.4 %copy-start = (s32[4096]{0:T(1024)S(1)}, s32[4096]{0:T(1024)}, u32[]{:S(2)}) copy-start(s32[4096]{0:T(1024)} %param.14) | copy-start | bytes 49156
  7.2 153.4 %all-gather.3.cloned.1.call-start = ((), (), s32[]{:S(2)}) async-start(), calls=%async_computation.3 | async-start | bytes 1081344 | tf_op jit(solution)/shard_map/all_gather | solution.py:41
  9.6 84.6 %all-to-all-start.1 = ((bf16[16,8,1024]{2,0,1:T(8,128)(2,1)}), bf16[16,8,1024]{2,0,1:T(8,128)(2,1)S(1)}, u32[]{:S(2)}, u32[]{:S(2)}) async-start(bf16[16,8,1024]{2,0,1:T(8,128)(2,1)} %bitcast.216), calls=%async_computation.1 | async-start | bytes 524288 | tf_op jit(solution)/shard_map/all_to_all | solution.py:13
  18.1 298.4 %all-gather.5.cloned.1.call-start = ((), (), s32[]{:S(2)}) async-start(), calls=%async_computation.4 | async-start | bytes 1081344 | tf_op jit(solution)/shard_map/all_gather | solution.py:42
  18.8 569.9 %reduce-scatter.2.cloned.1.call-start = ((), (), s32[]{:S(2)}) async-start(), calls=%async_computation.5 | async-start | bytes 4325376 | tf_op jit(solution)/shard_map/reduce_scatter | solution.py:128
  70.6 23.2 %copy-start.1 = (bf16[128,1024]{1,0:T(8,128)(2,1)S(1)}, bf16[128,1024]{1,0:T(8,128)(2,1)}, u32[]{:S(2)}) copy-start(bf16[128,1024]{1,0:T(8,128)(2,1)} %param.10) | copy-start | bytes 786436
  414.4 19.0 %all-to-all-start = ((bf16[8,16,1024]{2,1,0:T(8,128)(2,1)}), bf16[8,16,1024]{2,1,0:T(8,128)(2,1)S(1)}, u32[]{:S(2)}, u32[]{:S(2)}) async-start(bf16[8,16,1024]{2,1,0:T(8,128)(2,1)} %all_to_all.26), calls=%async_computation | async-start | bytes 524288 | tf_op jit(solution)/shard_map/all_to_all | solution.py:17
Sparse Core Ops, SparseCore 0:
  9.8 150.7 all-gather.2
  162.4 154.0 all-gather.4
  413.7 174.9 reduce-scatter.1
where the time goes:
time: 606 us; the launch traced here: 597 us
  waiting for transfers between devices  390 us (64%)
  matrix products  65.5 us (11%)
  other arithmetic  55.3 us (9%)
  local copies, waits for them, and re-layouts  51 us (8%)
  starting transfers between devices  14.9 us (2%)
  between operations  14 us (2%)
  loops' own time  6.3 us (1%)
    all_gather x1, waiting for transfers between devices, on_device(): lax.all_gather(value_rows, 'ctx', axis=0, tiled=True)  156 us
    reduce_scatter x1, waiting for transfers between devices, on_device(): reduced = lax.psum_scatter(terms, 'ctx', scatter_dimension=0, tiled=True)  155 us
    all_gather x1, waiting for transfers between devices, on_device(): lax.all_gather(key_rows, 'ctx', axis=0, tiled=True)  66.2 us
    gather x59, other arithmetic, on_device(): positions = SPAN * jnp.take(span_order, all_rows // SPAN) + all_rows % SPAN  43.7 us
    dot_general x16, matrix products, block_inputs(): jnp.einsum('rgjd,cgd->gjrc', queries4, key_block, preferred_element_type=...  23.6 us
    gather x1, local copies, waits for them, and re-layouts, on_device(): labels = jnp.take(segment_ids, positions)  23 us
    dot_general x8, matrix products, sum_step(): jnp.einsum('gjrc,cgd->rgjd', weights.astype(jnp.bfloat16), value_block, p...  13.2 us
  transfers between devices with their start and end apart: 5, of which 4 were waited for; matrix products, arithmetic and copies ran while one was open for 13% of the time, Pallas kernels for 0%

commit v1 on v0

--- a/solution.py
+++ b/solution.py
@@ -1,12 +1,116 @@
+import functools
 import math
 
 import jax
 import jax.numpy as jnp
 from jax import lax
+from jax.experimental import pallas as pl
+from jax.experimental.pallas import tpu as pltpu
 from jax.sharding import PartitionSpec as P
 
 HEAD_DIM = 128
 SPAN = 64
+MESH = pl.DeviceIdType.MESH
+
+
+def greet_all(n, me):
+    barrier = pltpu.get_barrier_semaphore()
+
+    def greet(i, c):
+        peer = lax.rem(me + i, n)
+        pl.semaphore_signal(barrier, inc=1, device_id={"ctx": peer}, device_id_type=MESH)
+        return c
+
+    lax.fori_loop(1, n, greet, 0)
+    pl.semaphore_wait(barrier, n - 1)
+
+
+def gather_kernel(n, src_ref, out_ref, send_sem, recv_sem):
+    me = lax.axis_index("ctx")
+    greet_all(n, me)
+
+    def copy_to(peer):
+        return pltpu.make_async_remote_copy(
+            src_ref, out_ref.at[me], send_sem.at[peer], recv_sem.at[me],
+            device_id={"ctx": peer}, device_id_type=MESH)
+
+    def copy_from(src):
+        return pltpu.make_async_remote_copy(
+            src_ref, out_ref.at[src], send_sem.at[src], recv_sem.at[src],
+            device_id={"ctx": src}, device_id_type=MESH)
+
+    def send(i, c):
+        copy_to(lax.rem(me + i, n)).start()
+        return c
+
+    lax.fori_loop(1, n, send, 0)
+    out_ref[me] = src_ref[...]
+
+    def wait(i, c):
+        copy_to(lax.rem(me + i, n)).wait_send()
+        copy_from(lax.rem(me + n - i, n)).wait_recv()
+        return c
+
+    lax.fori_loop(1, n, wait, 0)
+
+
+def ctx_gather(block, n):
+    rows, width = block.shape
+    return pl.pallas_call(
+        functools.partial(gather_kernel, n),
+        out_shape=jax.ShapeDtypeStruct((n, rows, width), block.dtype),
+        in_specs=[pl.BlockSpec(memory_space=pltpu.VMEM)],
+        out_specs=pl.BlockSpec(memory_space=pltpu.VMEM),
+        scratch_shapes=[pltpu.SemaphoreType.DMA((n,)), pltpu.SemaphoreType.DMA((n,))],
+        compiler_params=pltpu.CompilerParams(collective_id=0, has_side_effects=True),
+    )(block)
+
+
+def scatter_kernel(n, terms_ref, out_ref, held, send_sem, recv_sem):
+    me = lax.axis_index("ctx")
+    greet_all(n, me)
+
+    def copy_to(peer):
+        return pltpu.make_async_remote_copy(
+            terms_ref.at[peer], held.at[me], send_sem.at[peer], recv_sem.at[me],
+            device_id={"ctx": peer}, device_id_type=MESH)
+
+    def copy_from(src):
+        return pltpu.make_async_remote_copy(
+            terms_ref.at[src], held.at[src], send_sem.at[src], recv_sem.at[src],
+            device_id={"ctx": src}, device_id_type=MESH)
+
+    def send(i, c):
+        copy_to(lax.rem(me + i, n)).start()
+        return c
+
+    lax.fori_loop(1, n, send, 0)
+    out_ref[...] = terms_ref[me].astype(jnp.float32)
+
+    def wait(i, c):
+        copy_to(lax.rem(me + i, n)).wait_send()
+        src = lax.rem(me + n - i, n)
+        copy_from(src).wait_recv()
+        out_ref[...] += held[src].astype(jnp.float32)
+        return c
+
+    lax.fori_loop(1, n, wait, 0)
+
+
+def ctx_reduce_scatter(terms, n):
+    _, rows, width = terms.shape
+    return pl.pallas_call(
+        functools.partial(scatter_kernel, n),
+        out_shape=jax.ShapeDtypeStruct((rows, width), jnp.float32),
+        in_specs=[pl.BlockSpec(memory_space=pltpu.VMEM)],
+        out_specs=pl.BlockSpec(memory_space=pltpu.VMEM),
+        scratch_shapes=[
+            pltpu.VMEM(terms.shape, terms.dtype),
+            pltpu.SemaphoreType.DMA((n,)),
+            pltpu.SemaphoreType.DMA((n,)),
+        ],
+        compiler_params=pltpu.CompilerParams(collective_id=1, has_side_effects=True),
+    )(terms)
 
 
 def fetch_grad(out_grad):
@@ -27,9 +131,11 @@
     total_rows = local_rows * ctx_size
     width = groups_here * HEAD_DIM
     scale = 1.0 / math.sqrt(HEAD_DIM)
-    all_rows = jnp.arange(total_rows, dtype=jnp.int32)
-    positions = SPAN * jnp.take(span_order, all_rows // SPAN) + all_rows % SPAN
-    labels = jnp.take(segment_ids, positions)
+    offsets = jnp.arange(SPAN, dtype=jnp.int32)
+    positions = (SPAN * span_order[:, None] + offsets[None, :]).reshape(total_rows)
+    prompt_end = jnp.sum((segment_ids == 0).astype(jnp.int32))
+    chosen_end = jnp.sum((segment_ids <= 1).astype(jnp.int32))
+    labels = (positions >= prompt_end).astype(jnp.int32) + (positions >= chosen_end).astype(jnp.int32)
     own_start = ctx_index * local_rows
     own_pos = lax.dynamic_slice_in_dim(positions, own_start, local_rows, 0)
     own_label = lax.dynamic_slice_in_dim(labels, own_start, local_rows, 0)
@@ -37,10 +143,9 @@
     blocks = total_rows // block
     queries4 = query_rows.reshape(local_rows, groups_here, ratio, HEAD_DIM)
     grad_rows = None
-    keys_all, values_all = (
-        lax.all_gather(key_rows, "ctx", axis=0, tiled=True),
-        lax.all_gather(value_rows, "ctx", axis=0, tiled=True),
-    )
+    kv_all = ctx_gather(jnp.concatenate([key_rows, value_rows], axis=1), ctx_size)
+    keys_all = kv_all[:, :, :width].reshape(total_rows, width)
+    values_all = kv_all[:, :, width:].reshape(total_rows, width)
     keys_all = keys_all.reshape(total_rows, groups_here, HEAD_DIM)
     values_all = values_all.reshape(total_rows, groups_here, HEAD_DIM)
 
@@ -124,8 +229,8 @@
         return (query_acc, kv_terms(probs_b, dscore_b, block))
 
     query_acc, term_blocks = lax.scan(grad_step, start_query, jnp.arange(blocks, dtype=jnp.int32))
-    terms = term_blocks.reshape(total_rows, 2 * width)
-    reduced = lax.psum_scatter(terms, "ctx", scatter_dimension=0, tiled=True)
+    terms = term_blocks.reshape(ctx_size, local_rows, 2 * width)
+    reduced = ctx_reduce_scatter(terms, ctx_size)
     key_grad = reduced[:, :width].astype(jnp.bfloat16)
     value_grad = reduced[:, width:].astype(jnp.bfloat16)
     query_grad = (query_acc * scale).astype(jnp.bfloat16).reshape(local_rows, heads_here * HEAD_DIM)

time: 606 us -> 227 us (0.37); the launches traced: 597 us -> 225 us
  waiting for transfers between devices: 390 us -> 0.01 us
  Pallas kernels: 0 us -> 122 us
  other arithmetic: 55.3 us -> 15.5 us
  local copies, waits for them, and re-layouts: 51 us -> 23.8 us
  matrix products: 65.5 us -> 43.7 us
  between operations: 14 us -> 0.79 us
    all_gather x2 -> x0, waiting for transfers between devices: 222 us -> none  [the longest x1 156 us: on_device(): lax.all_gather(value_rows, 'ctx', axis=0, tiled=True)]
    reduce_scatter x1 -> x0, waiting for transfers between devices: 155 us -> none  [on_device(): reduced = lax.psum_scatter(terms, 'ctx', scatter_dimension=0, tiled=True)]
    pallas_call x0 -> x2, Pallas kernels: none -> 122 us  [the longest x1 82.1 us: ctx_reduce_scatter(): pl.pallas_call(functools.partial(scatter_kernel, n), out_shape=jax.ShapeD...]
    gather x60 -> x0, other arithmetic: 43.7 us -> none  [the longest x59 43.7 us: on_device(): positions = SPAN * jnp.take(span_order, all_rows // SPAN) + all_rows % SPAN]
    gather x5 -> x0, local copies, waits for them, and re-layouts: 30.8 us -> none  [the longest x1 23 us: on_device(): labels = jnp.take(segment_ids, positions)]
    dot_general x16, matrix products: 23.6 us -> 9 us  [block_inputs(): jnp.einsum('rgjd,cgd->gjrc', queries4, key_block, preferred_element_type=...]
    all_to_all x1, waiting for transfers between devices: 11.8 us -> 0.01 us  [spread_output(): lax.all_to_all(attn_flat, 'tp', split_axis=0, concat_axis=1, tiled=True)]
    dot_general x8, matrix products: 10.5 us -> 3.25 us  [grad_step(): jnp.einsum('gjrc,cgd->rgjd', dscore_b, key_block, preferred_element_type=...]
  transfers between devices with their start and end apart: 5 -> 2, of which waited for: 4 -> 0; matrix products, arithmetic and copies ran while one was open for 13% -> 35% of each run, Pallas kernels for 0% -> 54%
where the time goes in v1:
time: 227 us; the launch traced here: 225 us
  Pallas kernels  122 us (54%)
  matrix products  43.7 us (19%)
  local copies, waits for them, and re-layouts  23.8 us (10%)
  other arithmetic  15.5 us (7%)
  starting transfers between devices  12.6 us (6%)
  loops' own time  6.32 us (3%)
    pallas_call x1, Pallas kernels, ctx_reduce_scatter(): pl.pallas_call(functools.partial(scatter_kernel, n), out_shape=jax.ShapeD...  82.1 us
    pallas_call x1, Pallas kernels, ctx_gather(): pl.pallas_call(functools.partial(gather_kernel, n), out_shape=jax.ShapeDt...  39.7 us
    dot_general x8, matrix products, sum_step(): jnp.einsum('gjrc,cgd->rgjd', weights.astype(jnp.bfloat16), value_block, p...  13.2 us
    dot_general x8, matrix products, score_grads(): jnp.einsum('rgjd,cgd->gjrc', grads4, value_block, preferred_element_type=...  10.7 us
    dot_general x16, matrix products, block_inputs(): jnp.einsum('rgjd,cgd->gjrc', queries4, key_block, preferred_element_type=...  9 us
    all_to_all x1, starting transfers between devices, fetch_grad(): lax.all_to_all(out_grad, 'tp', split_axis=1, concat_axis=0, tiled=True)  8.47 us
    dynamic_update_slice x16, local copies, waits for them, and re-layouts, on_device(): lax.scan(grad_step, start_query, jnp.arange(blocks, dtype=jnp.int32))  8.25 us
    another operation x1, loops' own time, on_device(): lax.scan(grad_step, start_query, jnp.arange(blocks, dtype=jnp.int32))  5.75 us
  transfers between devices with their start and end apart: 2, of which 0 were waited for; matrix products, arithmetic and copies ran while one was open for 35% of the time, Pallas kernels for 54%

profile of v1, /device:TPU:16, one launch (start us, length us, event | category | flops | bytes accessed | tf_op | source)
XLA Modules:
  0.0 224.5 jit_solution(10380588177707358474)
XLA Ops:
  0.7 1.7 copy.92
  2.3 8.5 %all-to-all-start.1 = ((bf16[16,8,1024]{2,0,1:T(8,128)(2,1)}), bf16[16,8,1024]{2,0,1:T(8,128)(2,1)S(1)}, u32[]{:S(2)}, u32[]{:S(2)}) async-start(bf16[16,8,1024]{2,0,1:T(8,128)(2,1)} %bitcast.149), calls=%async_computation.1 | async-start | bytes 524288 | tf_op jit(solution)/shard_map/all_to_all | solution.py:117
  11.5 1.4 convert_reduce_fusion.1
  16.4 39.7 %shard_map.93 = bf16[32,128,256]{2,1,0:T(8,128)(2,1)} custom-call(bf16[128,256]{1,0:T(8,128)(2,1)} %pad_maximum_fusion.src_ref), custom_call_target="tpu_custom_call" | custom-call | tf_op jit(solution)/shard_map/pallas_call | solution.py:59
  56.1 2.8 %fusion.48 = (bf16[32,128,128]{2,1,0:T(8,128)(2,1)}, bf16[32,128,128]{2,1,0:T(8,128)(2,1)S(1)}) fusion(bf16[32,128,256]{2,1,0:T(8,128)(2,1)} %shard_map.93), kind=kLoop, calls=%fused_computation.77 | loop fusion | bytes 4194304 | tf_op jit(solution)/shard_map/slice | solution.py:148
  58.9 25.1 %while.31 = (s32[]{:T(128)}, f32[1,8,128,1]{2,1,3,0:T(8,128)S(1)}, f32[1,8,128,1]{2,1,3,0:T(8,128)S(1)}, f32[128,1,8,128]{0,3,2,1:T(8,128)S(1)}, s32[4096]{0:T(1...) while((s32[]{:T(128)}, f32[1,8,128,1]{2,1,3,0:T(8,128)S(1)}, ...), condition=%wide.region_5.6_spmd.clone, body=%wide.region_2.5_spmd.clone.sunk | while | flops 275919360 | bytes 8214751 | solution.py:188
  60.3 1.7 fusion.79
  63.4 1.7 fusion.79
  66.6 1.7 fusion.79
  69.7 1.7 fusion.79
  72.9 1.7 fusion.79
  76.0 1.7 fusion.79
  79.1 1.7 fusion.79
  82.3 1.7 fusion.79
  85.9 4.1 %all-to-all-start = ((bf16[8,16,1024]{2,1,0:T(8,128)(2,1)}), bf16[8,16,1024]{2,1,0:T(8,128)(2,1)S(1)}, u32[]{:S(2)}, u32[]{:S(2)}) async-start(bf16[8,16,1024]{2,1,0:T(8,128)(2,1)} %all_to_all.26), calls=%async_computation | async-start | bytes 524288 | tf_op jit(solution)/shard_map/all_to_all | solution.py:121
  90.0 49.3 %while.32 = (s32[]{:T(128)}, f32[128,1,8,128]{0,3,2,1:T(8,128)S(1)}, f32[8,512,256]{2,1,0:T(8,128)}, s32[8]{0:T(128)S(1)}, bf16[4096,1,128]{2,0,1:T(8,128)(2,1)S...) while((s32[]{:T(128)}, ...), condition=%wide.region_8.9_spmd.clone, body=%wide.region_7.8_spmd.clone.sunk | while | flops 676528640 | bytes 15755537 | solution.py:231
  92.8 1.3 fusion.91
  99.0 1.3 fusion.91
  105.1 1.3 fusion.91
  111.3 1.3 fusion.91
  117.5 1.3 fusion.91
  123.6 1.3 fusion.91
  135.9 1.3 fusion.91
  139.2 82.1 %shard_map.94 = f32[128,256]{1,0:T(8,128)} custom-call(f32[32,128,256]{2,1,0:T(8,128)} %bitcast.217), custom_call_target="tpu_custom_call" | custom-call | tf_op jit(solution)/shard_map/pallas_call | solution.py:102
  (194 shorter events, 54.7 us)
Async XLA Ops:
  0.6 15.1 %copy-start = (bf16[128,128]{1,0:T(8,128)(2,1)S(1)}, bf16[128,128]{1,0:T(8,128)(2,1)}, u32[]{:S(2)}) copy-start(bf16[128,128]{1,0:T(8,128)(2,1)} %param.12) | copy-start | bytes 98308
  0.6 15.1 %copy-start.1 = (bf16[128,128]{1,0:T(8,128)(2,1)S(1)}, bf16[128,128]{1,0:T(8,128)(2,1)}, u32[]{:S(2)}) copy-start(bf16[128,128]{1,0:T(8,128)(2,1)} %param.11) | copy-start | bytes 98308
  2.3 82.0 %all-to-all-start.1 = ((bf16[16,8,1024]{2,0,1:T(8,128)(2,1)}), bf16[16,8,1024]{2,0,1:T(8,128)(2,1)S(1)}, u32[]{:S(2)}, u32[]{:S(2)}) async-start(bf16[16,8,1024]{2,0,1:T(8,128)(2,1)} %bitcast.149), calls=%async_computation.1 | async-start | bytes 524288 | tf_op jit(solution)/shard_map/all_to_all | solution.py:117
  85.9 137.9 %all-to-all-start = ((bf16[8,16,1024]{2,1,0:T(8,128)(2,1)}), bf16[8,16,1024]{2,1,0:T(8,128)(2,1)S(1)}, u32[]{:S(2)}, u32[]{:S(2)}) async-start(bf16[8,16,1024]{2,1,0:T(8,128)(2,1)} %all_to_all.26), calls=%async_computation | async-start | bytes 524288 | tf_op jit(solution)/shard_map/all_to_all | solution.py:121

commit v2 on v1

--- a/solution.py
+++ b/solution.py
@@ -230,7 +230,7 @@
 
     query_acc, term_blocks = lax.scan(grad_step, start_query, jnp.arange(blocks, dtype=jnp.int32))
     terms = term_blocks.reshape(ctx_size, local_rows, 2 * width)
-    reduced = ctx_reduce_scatter(terms, ctx_size)
+    reduced = ctx_reduce_scatter(terms.astype(jnp.bfloat16), ctx_size)
     key_grad = reduced[:, :width].astype(jnp.bfloat16)
     value_grad = reduced[:, width:].astype(jnp.bfloat16)
     query_grad = (query_acc * scale).astype(jnp.bfloat16).reshape(local_rows, heads_here * HEAD_DIM)

time: 227 us -> 192 us (0.85)
  Pallas kernels: 122 us -> 78.5 us
  matrix products: 43.7 us -> 29.2 us
  other arithmetic: 15.5 us -> 28.1 us
  local copies, waits for them, and re-layouts: 23.8 us -> 33.7 us
    pallas_call x1, Pallas kernels: 82.1 us -> 38.8 us  [ctx_reduce_scatter(): pl.pallas_call(functools.partial(scatter_kernel, n), out_shape=jax.ShapeD...]
    dynamic_update_slice x16 -> x0, local copies, waits for them, and re-layouts: 8.25 us -> none  [on_device(): lax.scan(grad_step, start_query, jnp.arange(blocks, dtype=jnp.int32))]
    dot_general x8, matrix products: 13.2 us -> 5.88 us  [sum_step(): jnp.einsum('gjrc,cgd->rgjd', weights.astype(jnp.bfloat16), value_block, p...]
    dot_general x8, matrix products: 10.7 us -> 3.41 us  [score_grads(): jnp.einsum('rgjd,cgd->gjrc', grads4, value_block, preferred_element_type=...]
    while x8 -> x40, local copies, waits for them, and re-layouts: 0.02 us -> 6.37 us
    dynamic_update_slice x0 -> x8, other arithmetic: none -> 5.75 us  [on_device(): lax.scan(grad_step, start_query, jnp.arange(blocks, dtype=jnp.int32))]
    dynamic_slice x16, local copies, waits for them, and re-layouts: 1.24 us -> 6.72 us  [block_inputs(): pos_block = lax.dynamic_slice_in_dim(positions, start, size, 0)]
    eq x16, other arithmetic: 1.24 us -> 6.72 us  [block_inputs(): label_block[None, :] == 0]
  transfers between devices with their start and end apart: 2 -> 2, of which waited for: 0 -> 0; matrix products, arithmetic and copies ran while one was open for 35% -> 41% of each run, Pallas kernels for 54% -> 42%
where the time goes in v2:
time: 192 us; the launch traced here: 189 us
  Pallas kernels  78.5 us (41%)
  local copies, waits for them, and re-layouts  33.7 us (18%)
  matrix products  29.2 us (15%)
  other arithmetic  28.1 us (15%)
  starting transfers between devices  12.6 us (7%)
  loops' own time  6.2 us (3%)
    pallas_call x1, Pallas kernels, ctx_gather(): pl.pallas_call(functools.partial(gather_kernel, n), out_shape=jax.ShapeDt...  39.7 us
    pallas_call x1, Pallas kernels, ctx_reduce_scatter(): pl.pallas_call(functools.partial(scatter_kernel, n), out_shape=jax.ShapeD...  38.8 us
    dot_general x16, matrix products, block_inputs(): jnp.einsum('rgjd,cgd->gjrc', queries4, key_block, preferred_element_type=...  9 us
    all_to_all x1, starting transfers between devices, fetch_grad(): lax.all_to_all(out_grad, 'tp', split_axis=1, concat_axis=0, tiled=True)  8.47 us
    dynamic_slice x16, local copies, waits for them, and re-layouts, block_inputs(): pos_block = lax.dynamic_slice_in_dim(positions, start, size, 0)  6.72 us
    eq x16, other arithmetic, block_inputs(): label_block[None, :] == 0  6.72 us
    while x40, local copies, waits for them, and re-layouts  6.37 us
    dot_general x8, matrix products, sum_step(): jnp.einsum('gjrc,cgd->rgjd', weights.astype(jnp.bfloat16), value_block, p...  5.88 us
  transfers between devices with their start and end apart: 2, of which 0 were waited for; matrix products, arithmetic and copies ran while one was open for 41% of the time, Pallas kernels for 42%

profile of v2, /device:TPU:16, one launch (start us, length us, event | category | flops | bytes accessed | tf_op | source)
XLA Modules:
  0.0 189.0 jit_solution(14707618852682935026)
XLA Ops:
  0.7 1.7 copy.89
  2.3 8.5 %all-to-all-start.1 = ((bf16[16,8,1024]{2,0,1:T(8,128)(2,1)}), bf16[16,8,1024]{2,0,1:T(8,128)(2,1)S(1)}, u32[]{:S(2)}, u32[]{:S(2)}) async-start(bf16[16,8,1024]{2,0,1:T(8,128)(2,1)} %bitcast.151), calls=%async_computation.1 | async-start | bytes 524288 | tf_op jit(solution)/shard_map/all_to_all | solution.py:117
  11.5 1.4 convert_reduce_fusion.1
  13.1 1.3 convert_add_fusion
  14.5 1.1 copy.64
  16.4 39.7 %shard_map.93 = bf16[32,128,256]{2,1,0:T(8,128)(2,1)} custom-call(bf16[128,256]{1,0:T(8,128)(2,1)} %pad_maximum_fusion.src_ref), custom_call_target="tpu_custom_call" | custom-call | tf_op jit(solution)/shard_map/pallas_call | solution.py:59
  56.1 1.8 fusion.49
  57.9 24.1 %while.31 = (s32[]{:T(128)}, f32[1,8,128,1]{2,1,3,0:T(8,128)S(1)}, f32[1,8,128,1]{2,1,3,0:T(8,128)S(1)}, f32[128,1,8,128]{0,3,2,1:T(8,128)}, s32[4096]{0:T(1024)...) while((s32[]{:T(128)}, f32[1,8,128,1]{2,1,3,0:T(8,128)S(1)}, ...), condition=%wide.region_5.6_spmd.clone, body=%wide.region_2.5_spmd.clone.sunk | while | flops 275919360 | bytes 12409111 | solution.py:188
  82.6 2.1 %copy.68 = f32[128,1,8,128]{3,2,0,1:T(8,128)} copy(f32[128,1,8,128]{0,3,2,1:T(8,128)} %get-tuple-element.268) | data formatting | bytes 1048576 | tf_op jit(solution)/shard_map/while | solution.py:188
  85.0 2.0 %multiply_reduce_fusion = (f32[128,8]{1,0:T(8,128)S(1)}, bf16[128,1,8,128]{3,2,0,1:T(8,128)(2,1)}) fusion(bf16[128,1,8,128]{3,2,0,1:T(8,128)(2,1)S(1)} %bitcast.222, f32[128,1,8,128]{3,2,0,1:T(8,128)} %copy.68, f32[128,8]{1,0:T(8,128)S(1)} %copy.67), kind=kLoop, calls=%fused_computation.68 | loop fusion | flops 785408 | bytes 1056768 | tf_op jit(solution)/shard_map/reduce_sum | solution.py:196
  87.0 1.8 all_to_all.26
  88.8 4.1 %all-to-all-start = ((bf16[8,16,1024]{2,1,0:T(8,128)(2,1)}), bf16[8,16,1024]{2,1,0:T(8,128)(2,1)S(1)}, u32[]{:S(2)}, u32[]{:S(2)}) async-start(bf16[8,16,1024]{2,1,0:T(8,128)(2,1)} %all_to_all.26), calls=%async_computation | async-start | bytes 524288 | tf_op jit(solution)/shard_map/all_to_all | solution.py:121
  92.9 50.1 %while.32 = (s32[]{:T(128)}, f32[128,1,8,128]{0,3,2,1:T(8,128)S(1)}, bf16[8,512,256]{1,2,0:T(8,128)(2,1)}, s32[8]{0:T(128)S(1)}, bf16[4096,1,128]{2,0,1:T(8,128)...) while((s32[]{:T(128)}, ...), condition=%wide.region_8.9_spmd.clone, body=%wide.region_7.8_spmd.clone.sunk | while | flops 676987392 | bytes 12871953 | solution.py:231
  94.2 0.8 dynamic_slice.104
  100.5 0.8 dynamic_slice.104
  106.7 0.8 dynamic_slice.104
  113.0 0.8 dynamic_slice.104
  119.2 0.8 dynamic_slice.104
  125.5 0.8 dynamic_slice.104
  131.8 0.8 dynamic_slice.104
  143.1 3.9 %copy.74 = bf16[8,512,256]{2,1,0:T(8,128)(2,1)} copy(bf16[8,512,256]{1,2,0:T(8,128)(2,1)} %get-tuple-element.272) | data formatting | bytes 4194304 | tf_op jit(solution)/shard_map/convert_element_type | solution.py:233
  147.0 38.8 %shard_map.94 = f32[128,256]{1,0:T(8,128)} custom-call(bf16[32,128,256]{2,1,0:T(8,128)(2,1)} %bitcast.218), custom_call_target="tpu_custom_call" | custom-call | tf_op jit(solution)/shard_map/pallas_call | solution.py:102
  185.8 0.9 convert.4
  186.8 0.8 copy.82
  (215 shorter events, 66.9 us)
Async XLA Ops:
  0.6 15.1 %copy-start.4 = (bf16[128,128]{1,0:T(8,128)(2,1)S(1)}, bf16[128,128]{1,0:T(8,128)(2,1)}, u32[]{:S(2)}) copy-start(bf16[128,128]{1,0:T(8,128)(2,1)} %param.12) | copy-start | bytes 98308
  0.6 15.1 %copy-start.5 = (bf16[128,128]{1,0:T(8,128)(2,1)S(1)}, bf16[128,128]{1,0:T(8,128)(2,1)}, u32[]{:S(2)}) copy-start(bf16[128,128]{1,0:T(8,128)(2,1)} %param.11) | copy-start | bytes 98308
  2.3 82.4 %all-to-all-start.1 = ((bf16[16,8,1024]{2,0,1:T(8,128)(2,1)}), bf16[16,8,1024]{2,0,1:T(8,128)(2,1)S(1)}, u32[]{:S(2)}, u32[]{:S(2)}) async-start(bf16[16,8,1024]{2,0,1:T(8,128)(2,1)} %bitcast.151), calls=%async_computation.1 | async-start | bytes 524288 | tf_op jit(solution)/shard_map/all_to_all | solution.py:117
  58.3 1.0 copy-start
  60.1 0.8 copy-start.1
  61.4 1.0 copy-start
  63.1 0.8 copy-start.1
  64.4 1.0 copy-start
  66.1 0.8 copy-start.1
  67.4 1.0 copy-start
  69.2 0.8 copy-start.1
  70.4 1.0 copy-start
  72.2 0.8 copy-start.1
  73.4 1.0 copy-start
  75.2 0.8 copy-start.1
  76.4 1.0 copy-start
  78.2 0.8 copy-start.1
  79.4 1.0 copy-start
  81.2 0.8 copy-start.1
  82.0 0.6 copy-start.2
  82.6 2.1 %copy-start.3 = (s32[4096]{0:T(1024)}, s32[4096]{0:T(1024)S(1)}, u32[]{:S(2)}) copy-start(s32[4096]{0:T(1024)S(1)} %get-tuple-element.797) | copy-start | bytes 49156
  88.8 99.5 %all-to-all-start = ((bf16[8,16,1024]{2,1,0:T(8,128)(2,1)}), bf16[8,16,1024]{2,1,0:T(8,128)(2,1)S(1)}, u32[]{:S(2)}, u32[]{:S(2)}) async-start(bf16[8,16,1024]{2,1,0:T(8,128)(2,1)} %all_to_all.26), calls=%async_computation | async-start | bytes 524288 | tf_op jit(solution)/shard_map/all_to_all | solution.py:121

commit v3 on v2

v3 whole, which is shorter than its diff:
```python
import functools
import math

import jax
import jax.numpy as jnp
from jax import lax
from jax.experimental import pallas as pl
from jax.experimental.pallas import tpu as pltpu
from jax.sharding import PartitionSpec as P

HEAD_DIM = 128
SPAN = 64
MESH = pl.DeviceIdType.MESH


def greet_all(n, me):
    barrier = pltpu.get_barrier_semaphore()

    def greet(i, c):
        peer = lax.rem(me + i, n)
        pl.semaphore_signal(barrier, inc=1, device_id={"ctx": peer}, device_id_type=MESH)
        return c

    lax.fori_loop(1, n, greet, 0)
    pl.semaphore_wait(barrier, n - 1)


def gather_kernel(n, src_ref, out_ref, send_sem, recv_sem):
    me = lax.axis_index("ctx")
    greet_all(n, me)

    def copy_to(peer):
        return pltpu.make_async_remote_copy(
            src_ref, out_ref.at[me], send_sem.at[peer], recv_sem.at[me],
            device_id={"ctx": peer}, device_id_type=MESH)

    def copy_from(src):
        return pltpu.make_async_remote_copy(
            src_ref, out_ref.at[src], send_sem.at[src], recv_sem.at[src],
            device_id={"ctx": src}, device_id_type=MESH)

    def send(i, c):
        copy_to(lax.rem(me + i, n)).start()
        return c

    lax.fori_loop(1, n, send, 0)
    out_ref[me] = src_ref[...]

    def wait(i, c):
        copy_to(lax.rem(me + i, n)).wait_send()
        copy_from(lax.rem(me + n - i, n)).wait_recv()
        return c

    lax.fori_loop(1, n, wait, 0)


def ctx_gather(block, n):
    rows, width = block.shape
    return pl.pallas_call(
        functools.partial(gather_kernel, n),
        out_shape=jax.ShapeDtypeStruct((n, rows, width), block.dtype),
        in_specs=[pl.BlockSpec(memory_space=pltpu.VMEM)],
        out_specs=pl.BlockSpec(memory_space=pltpu.VMEM),
        scratch_shapes=[pltpu.SemaphoreType.DMA((n,)), pltpu.SemaphoreType.DMA((n,))],
        compiler_params=pltpu.CompilerParams(collective_id=0, has_side_effects=True),
    )(block)


def scatter_kernel(n, terms_ref, out_ref, held, send_sem, recv_sem):
    me = lax.axis_index("ctx")
    greet_all(n, me)

    def copy_to(peer):
        return pltpu.make_async_remote_copy(
            terms_ref.at[peer], held.at[me], send_sem.at[peer], recv_sem.at[me],
            device_id={"ctx": peer}, device_id_type=MESH)

    def copy_from(src):
        return pltpu.make_async_remote_copy(
            terms_ref.at[src], held.at[src], send_sem.at[src], recv_sem.at[src],
            device_id={"ctx": src}, device_id_type=MESH)

    def send(i, c):
        copy_to(lax.rem(me + i, n)).start()
        return c

    lax.fori_loop(1, n, send, 0)
    out_ref[...] = terms_ref[me].astype(jnp.float32)

    def wait(i, c):
        copy_to(lax.rem(me + i, n)).wait_send()
        src = lax.rem(me + n - i, n)
        copy_from(src).wait_recv()
        out_ref[...] += held[src].astype(jnp.float32)
        return c

    lax.fori_loop(1, n, wait, 0)


def ctx_reduce_scatter(terms, n):
    _, rows, width = terms.shape
    return pl.pallas_call(
        functools.partial(scatter_kernel, n),
        out_shape=jax.ShapeDtypeStruct((rows, width), jnp.float32),
        in_specs=[pl.BlockSpec(memory_space=pltpu.VMEM)],
        out_specs=pl.BlockSpec(memory_space=pltpu.VMEM),
        scratch_shapes=[
            pltpu.VMEM(terms.shape, terms.dtype),
            pltpu.SemaphoreType.DMA((n,)),
            pltpu.SemaphoreType.DMA((n,)),
        ],
        compiler_params=pltpu.CompilerParams(collective_id=1, has_side_effects=True),
    )(terms)


def fetch_grad(out_grad):
    return lax.all_to_all(out_grad, "tp", split_axis=1, concat_axis=0, tiled=True)


def spread_output(attn_flat):
    return lax.all_to_all(attn_flat, "tp", split_axis=0, concat_axis=1, tiled=True)


KEY_BLOCK = 512
NT_DIMS = (((1,), (1,)), ((), ()))
TN_DIMS = (((0,), (0,)), ((), ()))


def stack_heads(ref):
    heads = ref.shape[1] // HEAD_DIM
    return jnp.concatenate([ref[:, h * HEAD_DIM:(h + 1) * HEAD_DIM] for h in range(heads)], axis=0)


def unstack_heads(ref, value):
    rows = ref.shape[0]
    for h in range(ref.shape[1] // HEAD_DIM):
        ref[:, h * HEAD_DIM:(h + 1) * HEAD_DIM] = value[h * rows:(h + 1) * rows]


def key_block(kv_ref, cpos_ref, clab_ref, rpos, rlab, kb):
    start = pl.multiple_of(kb * KEY_BLOCK, KEY_BLOCK)
    keys = kv_ref[pl.ds(start, KEY_BLOCK), :HEAD_DIM]
    values = kv_ref[pl.ds(start, KEY_BLOCK), HEAD_DIM:]
    cpos = cpos_ref[:, pl.ds(start, KEY_BLOCK)]
    clab = clab_ref[:, pl.ds(start, KEY_BLOCK)]
    visible = (cpos <= rpos) & ((clab == 0) | (clab == rlab))
    return start, keys, values, visible


def fwd_kernel(q_ref, kv_ref, rpos_ref, rlab_ref, cpos_ref, clab_ref, o_ref, m_ref, l_ref, acc_sc):
    scale = 1.0 / math.sqrt(HEAD_DIM)
    queries = stack_heads(q_ref)
    rpos = rpos_ref[...]
    rlab = rlab_ref[...]
    m_ref[...] = jnp.full(m_ref.shape, -jnp.inf, jnp.float32)
    l_ref[...] = jnp.zeros(l_ref.shape, jnp.float32)
    acc_sc[...] = jnp.zeros(acc_sc.shape, jnp.float32)

    def body(kb, c):
        _, keys, values, visible = key_block(kv_ref, cpos_ref, clab_ref, rpos, rlab, kb)
        scores = lax.dot_general(queries, keys, NT_DIMS, preferred_element_type=jnp.float32) * scale
        scores = jnp.where(visible, scores, -jnp.inf)
        running = m_ref[...]
        new_max = jnp.maximum(running, jnp.max(scores, axis=-1, keepdims=True))
        shift = jnp.where(new_max == -jnp.inf, 0.0, new_max)
        factor = jnp.exp(running - shift)
        weights = jnp.where(visible, jnp.exp(scores - shift), 0.0)
        l_ref[...] = l_ref[...] * factor + jnp.sum(weights, axis=-1, keepdims=True)
        acc_sc[...] = acc_sc[...] * factor + jnp.dot(
            weights.astype(jnp.bfloat16), values, preferred_element_type=jnp.float32)
        m_ref[...] = new_max
        return c

    lax.fori_loop(0, kv_ref.shape[0] // KEY_BLOCK, body, 0)
    unstack_heads(o_ref, (acc_sc[...] / l_ref[...]).astype(o_ref.dtype))


def bwd_kernel(q_ref, g_ref, o_ref, kv_ref, rpos_ref, rlab_ref, cpos_ref, clab_ref, m_ref, l_ref,
               dq_ref, terms_ref, dq_sc):
    scale = 1.0 / math.sqrt(HEAD_DIM)
    queries = stack_heads(q_ref)
    grads = stack_heads(g_ref)
    outs = stack_heads(o_ref)
    delta = jnp.sum(grads.astype(jnp.float32) * outs.astype(jnp.float32), axis=-1, keepdims=True)
    rpos = rpos_ref[...]
    rlab = rlab_ref[...]
    row_max = m_ref[...]
    inv_total = 1.0 / l_ref[...]
    dq_sc[...] = jnp.zeros(dq_sc.shape, jnp.float32)

    def body(kb, c):
        start, keys, values, visible = key_block(kv_ref, cpos_ref, clab_ref, rpos, rlab, kb)
        scores = lax.dot_general(queries, keys, NT_DIMS, preferred_element_type=jnp.float32) * scale
        probs = jnp.where(visible, jnp.exp(scores - row_max), 0.0) * inv_total
        dprob = lax.dot_general(grads, values, NT_DIMS, preferred_element_type=jnp.float32)
        dscore_b = (probs * (dprob - delta)).astype(jnp.bfloat16)
        probs_b = probs.astype(jnp.bfloat16)
        dq_sc[...] += jnp.dot(dscore_b, keys, preferred_element_type=jnp.float32)
        key_term = lax.dot_general(dscore_b, queries, TN_DIMS, preferred_element_type=jnp.float32) * scale
        value_term = lax.dot_general(probs_b, grads, TN_DIMS, preferred_element_type=jnp.float32)
        terms_ref[pl.ds(start, KEY_BLOCK), :HEAD_DIM] = key_term.astype(terms_ref.dtype)
        terms_ref[pl.ds(start, KEY_BLOCK), HEAD_DIM:] = value_term.astype(terms_ref.dtype)
        return c

    lax.fori_loop(0, kv_ref.shape[0] // KEY_BLOCK, body, 0)
    unstack_heads(dq_ref, (dq_sc[...] * scale).astype(dq_ref.dtype))


def vmem_specs(n):
    return [pl.BlockSpec(memory_space=pltpu.VMEM)] * n


def attention_fwd(q, kv, rpos, rlab, cpos, clab):
    stacked = rpos.shape[0]
    return pl.pallas_call(
        fwd_kernel,
        out_shape=(
            jax.ShapeDtypeStruct(q.shape, jnp.bfloat16),
            jax.ShapeDtypeStruct((stacked, 1), jnp.float32),
            jax.ShapeDtypeStruct((stacked, 1), jnp.float32),
        ),
        in_specs=vmem_specs(6),
        out_specs=tuple(vmem_specs(3)),
        scratch_shapes=[pltpu.VMEM((stacked, HEAD_DIM), jnp.float32)],
    )(q, kv, rpos, rlab, cpos, clab)


def attention_bwd(q, g, o, kv, rpos, rlab, cpos, clab, m, l):
    stacked = rpos.shape[0]
    return pl.pallas_call(
        bwd_kernel,
        out_shape=(
            jax.ShapeDtypeStruct(q.shape, jnp.bfloat16),
            jax.ShapeDtypeStruct(kv.shape, jnp.bfloat16),
        ),
        in_specs=vmem_specs(10),
        out_specs=tuple(vmem_specs(2)),
        scratch_shapes=[pltpu.VMEM((stacked, HEAD_DIM), jnp.float32)],
    )(q, g, o, kv, rpos, rlab, cpos, clab, m, l)


def on_device(query_rows, key_rows, value_rows, out_grad, segment_ids, span_order):
    ctx_size = lax.axis_size("ctx")
    ctx_index = lax.axis_index("ctx")
    local_rows = query_rows.shape[0]
    heads_here = query_rows.shape[1] // HEAD_DIM
    total_rows = local_rows * ctx_size
    offsets = jnp.arange(SPAN, dtype=jnp.int32)
    positions = (SPAN * span_order[:, None] + offsets[None, :]).reshape(total_rows)
    prompt_end = jnp.sum((segment_ids == 0).astype(jnp.int32))
    chosen_end = jnp.sum((segment_ids <= 1).astype(jnp.int32))
    labels = (positions >= prompt_end).astype(jnp.int32) + (positions >= chosen_end).astype(jnp.int32)
    own_pos = lax.dynamic_slice_in_dim(positions, ctx_index * local_rows, local_rows, 0)
    own_label = lax.dynamic_slice_in_dim(labels, ctx_index * local_rows, local_rows, 0)
    rpos = jnp.tile(own_pos, heads_here)[:, None]
    rlab = jnp.tile(own_label, heads_here)[:, None]
    cpos = positions[None, :]
    clab = labels[None, :]
    kv_all = ctx_gather(jnp.concatenate([key_rows, value_rows], axis=1), ctx_size)
    kv_all = kv_all.reshape(total_rows, kv_all.shape[2])
    attn_local, row_max, total = attention_fwd(query_rows, kv_all, rpos, rlab, cpos, clab)
    grad_rows = fetch_grad(out_grad)
    query_grad, terms = attention_bwd(
        query_rows, grad_rows, attn_local, kv_all, rpos, rlab, cpos, clab, row_max, total)
    reduced = ctx_reduce_scatter(terms.reshape(ctx_size, local_rows, terms.shape[1]), ctx_size)
    key_grad = reduced[:, :HEAD_DIM].astype(jnp.bfloat16)
    value_grad = reduced[:, HEAD_DIM:].astype(jnp.bfloat16)
    attn_spread = spread_output(attn_local)
    return (attn_spread, query_grad, key_grad, value_grad)


def solution(mesh):
    placed = (P("ctx", "tp"), P("ctx", "tp"), P("ctx", "tp"), P(("ctx", "tp"), None), P(), P())
    return jax.shard_map(
        on_device,
        mesh=mesh,
        in_specs=placed,
        out_specs=(P(("ctx", "tp"), None), P("ctx", "tp"), P("ctx", "tp"), P("ctx", "tp")),
        check_vma=False,
    )
```

time: 192 us -> 147 us (0.77)
  Pallas kernels: 78.5 us -> 120 us
  matrix products: 29.2 us -> 0 us
  local copies, waits for them, and re-layouts: 33.7 us -> 5.29 us
  other arithmetic: 28.1 us -> 7.04 us
  loops' own time: 6.2 us -> 0 us
    pallas_call x0 -> x2, Pallas kernels: none -> 41.8 us  [the longest x1 22.2 us: attention_bwd(): pl.pallas_call(bwd_kernel, out_shape=(jax.ShapeDtypeStruct(q.shape, jnp.b...]
    dot_general x56 -> x0, matrix products: 29.2 us -> none  [the longest x16 9 us: block_inputs(): jnp.einsum('rgjd,cgd->gjrc', queries4, key_block, preferred_element_type=...]
    dynamic_slice x26 -> x0, local copies, waits for them, and re-layouts: 11.5 us -> none  [the longest x16 6.72 us: block_inputs(): pos_block = lax.dynamic_slice_in_dim(positions, start, size, 0)]
    while x41 -> x0, local copies, waits for them, and re-layouts: 8.42 us -> none
    eq x16 -> x0, other arithmetic: 6.72 us -> none  [block_inputs(): label_block[None, :] == 0]
    another operation x2 -> x0, loops' own time: 6.2 us -> none  [the longest x1 5.63 us: on_device(): lax.scan(grad_step, start_query, jnp.arange(blocks, dtype=jnp.int32))]
    reduce_sum x9 -> x0, other arithmetic: 6.04 us -> none  [the longest x8 4.08 us: sum_step(): total = total * factor + jnp.sum(weights, axis=-1, keepdims=True)]
    dynamic_update_slice x8 -> x0, other arithmetic: 5.75 us -> none  [on_device(): lax.scan(grad_step, start_query, jnp.arange(blocks, dtype=jnp.int32))]
  transfers between devices with their start and end apart: 2 -> 2, of which waited for: 0 -> 0; matrix products, arithmetic and copies ran while one was open for 41% -> 7% of each run, Pallas kernels for 42% -> 83%
where the time goes in v3:
time: 147 us; the launch traced here: 146 us
  Pallas kernels  120 us (82%)
  starting transfers between devices  12.4 us (8%)
  other arithmetic  7.04 us (5%)
  local copies, waits for them, and re-layouts  5.29 us (4%)
    pallas_call x1, Pallas kernels, ctx_gather(): pl.pallas_call(functools.partial(gather_kernel, n), out_shape=jax.ShapeDt...  39.9 us
    pallas_call x1, Pallas kernels, ctx_reduce_scatter(): pl.pallas_call(functools.partial(scatter_kernel, n), out_shape=jax.ShapeD...  38.5 us
    pallas_call x1, Pallas kernels, attention_bwd(): pl.pallas_call(bwd_kernel, out_shape=(jax.ShapeDtypeStruct(q.shape, jnp.b...  22.2 us
    pallas_call x1, Pallas kernels, attention_fwd(): pl.pallas_call(fwd_kernel, out_shape=(jax.ShapeDtypeStruct(q.shape, jnp.b...  19.7 us
    all_to_all x1, starting transfers between devices, fetch_grad(): lax.all_to_all(out_grad, 'tp', split_axis=1, concat_axis=0, tiled=True)  8.47 us
    all_to_all x1, starting transfers between devices, spread_output(): lax.all_to_all(attn_flat, 'tp', split_axis=0, concat_axis=1, tiled=True)  3.91 us
    add x2, other arithmetic, on_device(): (positions >= prompt_end).astype(jnp.int32)  3.33 us
  transfers between devices with their start and end apart: 2, of which 0 were waited for; matrix products, arithmetic and copies ran while one was open for 7% of the time, Pallas kernels for 83%

profile of v3, /device:TPU:16, one launch (start us, length us, event | category | flops | bytes accessed | tf_op | source)
XLA Modules:
  0.0 145.6 jit_solution(8093040359881969616)
XLA Ops:
  0.6 0.0 copy-start.2
  0.7 1.7 %copy.21 = bf16[2,8,8,1024]{3,2,0,1:T(8,128)(2,1)} copy(bf16[2,8,8,1024]{3,2,1,0:T(8,128)(2,1)} %bitcast.21) | data formatting | bytes 524288 | tf_op jit(solution)/shard_map/all_to_all | solution.py:117
  2.3 8.5 %all-to-all-start.1 = ((bf16[16,8,1024]{2,0,1:T(8,128)(2,1)}), bf16[16,8,1024]{2,0,1:T(8,128)(2,1)S(1)}, u32[]{:S(2)}, u32[]{:S(2)}) async-start(bf16[16,8,1024]{2,0,1:T(8,128)(2,1)} %bitcast.14), calls=%async_computation.1 | async-start | bytes 524288 | tf_op jit(solution)/shard_map/all_to_all | solution.py:117
  10.8 0.7 broadcast_multiply_fusion
  11.5 0.1 iota_add_fusion
  11.5 0.1 add.53.cpos_ref
  11.6 0.0 copy-start.1
  11.6 0.1 add.50
  11.7 1.4 convert_reduce_fusion.1
  13.1 1.4 fusion.1
  14.5 1.0 copy.12.rpos_ref
  15.6 1.0 copy.13.rlab_ref
  16.6 0.6 pad_maximum_fusion.src_ref
  17.2 39.9 %shard_map.93 = bf16[32,128,256]{2,1,0:T(8,128)(2,1)} custom-call(bf16[128,256]{1,0:T(8,128)(2,1)} %pad_maximum_fusion.src_ref), custom_call_target="tpu_custom_call" | custom-call | tf_op jit(solution)/shard_map/pallas_call | solution.py:59
  57.2 1.9 %fusion.clab_ref = s32[1,4096]{1,0:T(1,128)} fusion(s32[1,4096]{1,0:T(1,128)S(1)} %add.53.cpos_ref, s32[]{:T(128)} %get-tuple-element.15, s32[]{:T(128)} %get-tuple-element.14), kind=kLoop, calls=%fused_computation.5 | loop fusion | flops 20480 | bytes 32776 | tf_op jit(solution)/shard_map/add | solution.py:252
  59.1 19.7 %shard_map.94 = (bf16[128,1024]{1,0:T(8,128)(2,1)}, f32[1024,1]{1,0:T(8,128)}, f32[1024,1]{1,0:T(8,128)}) custom-call(bf16[128,1024]{1,0:T(8,128)(2,1)} %q_ref.3, bf16[4096,256]{1,0:T(8,128)(2,1)} %bitcast.15, s32[1024,1]{1,0:T(8,128)} %copy.12.rpos_ref, s32[1024,1]{1,0:T(8,128)} %copy.13.rlab_ref, s32[1,4096]{1,0:T(1,128)} %copy-done.1, s32[1,4096]{1,0:T(1,128)} %fusion.clab_ref), custom_call_target="tpu_custom_call" | custom-call | tf_op jit(solution)/shard_map/pallas_call | solution.py:215
  78.8 0.0 all-to-all-done.1
  78.8 3.9 %all-to-all-start = ((bf16[8,16,1024]{2,1,0:T(8,128)(2,1)}), bf16[8,16,1024]{2,1,0:T(8,128)(2,1)S(1)}, u32[]{:S(2)}, u32[]{:S(2)}) async-start(bf16[8,16,1024]{2,1,0:T(8,128)(2,1)} %bitcast.19), calls=%async_computation | async-start | bytes 524288 | tf_op jit(solution)/shard_map/all_to_all | solution.py:121
  82.7 22.2 %shard_map.95 = (bf16[128,1024]{1,0:T(8,128)(2,1)}, bf16[4096,256]{1,0:T(8,128)(2,1)}) custom-call(bf16[128,1024]{1,0:T(8,128)(2,1)} %q_ref.3, bf16[128,1024]{1,0:T(8,128)(2,1)} %bitcast.18, bf16[128,1024]{1,0:T(8,128)(2,1)} %get-tuple-element.9.o_ref, bf16[4096,256]{1,0:T(8,128)(2,1)} %bitcast.16, s32[1024,1]{1,0:T(8,128)} %copy.12.rpos_ref, ...), custom_call_target="tpu_custom_call" | custom-call | tf_op jit(solution)/shard_map/pallas_call | solution.py:230
  104.9 38.5 %shard_map.96 = f32[128,256]{1,0:T(8,128)} custom-call(bf16[32,128,256]{2,1,0:T(8,128)(2,1)} %bitcast.17), custom_call_target="tpu_custom_call" | custom-call | tf_op jit(solution)/shard_map/pallas_call | solution.py:102
  143.4 0.9 convert.4
  144.3 0.6 fusion.2
  144.9 0.0 all-to-all-done
  144.9 0.7 copy.19
  (8 shorter events, 0.0 us)
Async XLA Ops:
  0.6 16.0 %copy-start.2 = (bf16[128,128]{1,0:T(8,128)(2,1)S(1)}, bf16[128,128]{1,0:T(8,128)(2,1)}, u32[]{:S(2)}) copy-start(bf16[128,128]{1,0:T(8,128)(2,1)} %param.8) | copy-start | bytes 98308
  0.6 16.0 %copy-start.3 = (bf16[128,128]{1,0:T(8,128)(2,1)S(1)}, bf16[128,128]{1,0:T(8,128)(2,1)}, u32[]{:S(2)}) copy-start(bf16[128,128]{1,0:T(8,128)(2,1)} %param.7) | copy-start | bytes 98308
  2.3 76.4 %all-to-all-start.1 = ((bf16[16,8,1024]{2,0,1:T(8,128)(2,1)}), bf16[16,8,1024]{2,0,1:T(8,128)(2,1)S(1)}, u32[]{:S(2)}, u32[]{:S(2)}) async-start(bf16[16,8,1024]{2,0,1:T(8,128)(2,1)} %bitcast.14), calls=%async_computation.1 | async-start | bytes 524288 | tf_op jit(solution)/shard_map/all_to_all | solution.py:117
  11.6 47.5 %copy-start.1 = (s32[1,4096]{1,0:T(1,128)}, s32[1,4096]{1,0:T(1,128)S(1)}, u32[]{:S(2)}) copy-start(s32[1,4096]{1,0:T(1,128)S(1)} %add.53.cpos_ref) | copy-start | bytes 49156
  78.8 3.9 %copy-start = (bf16[16,8,1024]{2,0,1:T(8,128)(2,1)}, bf16[16,8,1024]{2,0,1:T(8,128)(2,1)S(1)}, u32[]{:S(2)}) copy-start(bf16[16,8,1024]{2,0,1:T(8,128)(2,1)S(1)} %all-to-all-done.1) | copy-start | bytes 786436
  78.8 66.1 %all-to-all-start = ((bf16[8,16,1024]{2,1,0:T(8,128)(2,1)}), bf16[8,16,1024]{2,1,0:T(8,128)(2,1)S(1)}, u32[]{:S(2)}, u32[]{:S(2)}) async-start(bf16[8,16,1024]{2,1,0:T(8,128)(2,1)} %bitcast.19), calls=%async_computation | async-start | bytes 524288 | tf_op jit(solution)/shard_map/all_to_all | solution.py:121

commit v4 on v3

--- a/solution.py
+++ b/solution.py
@@ -236,6 +236,191 @@
         in_specs=vmem_specs(10),
         out_specs=tuple(vmem_specs(2)),
         scratch_shapes=[pltpu.VMEM((stacked, HEAD_DIM), jnp.float32)],
+    )(q, g, o, kv, rpos, rlab, cpos, clab, m, l)
+
+
+def fwd_step(queries, keys, values, visible, m_sc, l_sc, acc_sc):
+    scale = 1.0 / math.sqrt(HEAD_DIM)
+    scores = lax.dot_general(queries, keys, NT_DIMS, preferred_element_type=jnp.float32) * scale
+    scores = jnp.where(visible, scores, -jnp.inf)
+    running = m_sc[...]
+    new_max = jnp.maximum(running, jnp.max(scores, axis=-1, keepdims=True))
+    shift = jnp.where(new_max == -jnp.inf, 0.0, new_max)
+    factor = jnp.exp(running - shift)
+    weights = jnp.where(visible, jnp.exp(scores - shift), 0.0)
+    l_sc[...] = l_sc[...] * factor + jnp.sum(weights, axis=-1, keepdims=True)
+    acc_sc[...] = acc_sc[...] * factor + jnp.dot(
+        weights.astype(jnp.bfloat16), values, preferred_element_type=jnp.float32)
+    m_sc[...] = new_max
+
+
+def column_visible(cpos_ref, clab_ref, block, rpos, rlab):
+    cpos = cpos_ref[pl.ds(block, 1), :]
+    clab = clab_ref[pl.ds(block, 1), :]
+    return (cpos <= rpos) & ((clab == 0) | (clab == rlab))
+
+
+def gather_fwd_kernel(n, kv_src, q_ref, rpos_ref, rlab_ref, cpos_ref, clab_ref,
+                      kv_out, o_ref, m_ref, l_ref, acc_sc, send_sem, recv_sem):
+    me = lax.axis_index("ctx")
+    greet_all(n, me)
+
+    def copy_to(peer):
+        return pltpu.make_async_remote_copy(
+            kv_src, kv_out.at[me], send_sem.at[peer], recv_sem.at[me],
+            device_id={"ctx": peer}, device_id_type=MESH)
+
+    def copy_from(src):
+        return pltpu.make_async_remote_copy(
+            kv_src, kv_out.at[src], send_sem.at[src], recv_sem.at[src],
+            device_id={"ctx": src}, device_id_type=MESH)
+
+    def send(i, c):
+        copy_to(lax.rem(me + i, n)).start()
+        return c
+
+    lax.fori_loop(1, n, send, 0)
+    own = kv_src[...]
+    kv_out[me] = own
+    queries = stack_heads(q_ref)
+    rpos = rpos_ref[...]
+    rlab = rlab_ref[...]
+    m_ref[...] = jnp.full(m_ref.shape, -jnp.inf, jnp.float32)
+    l_ref[...] = jnp.zeros(l_ref.shape, jnp.float32)
+    acc_sc[...] = jnp.zeros(acc_sc.shape, jnp.float32)
+    fwd_step(queries, own[:, :HEAD_DIM], own[:, HEAD_DIM:],
+             column_visible(cpos_ref, clab_ref, me, rpos, rlab), m_ref, l_ref, acc_sc)
+
+    def arrive(i, c):
+        src = lax.rem(me + n - i, n)
+        copy_from(src).wait_recv()
+        block = kv_out[src]
+        fwd_step(queries, block[:, :HEAD_DIM], block[:, HEAD_DIM:],
+                 column_visible(cpos_ref, clab_ref, src, rpos, rlab), m_ref, l_ref, acc_sc)
+        return c
+
+    lax.fori_loop(1, n, arrive, 0)
+    unstack_heads(o_ref, (acc_sc[...] / l_ref[...]).astype(o_ref.dtype))
+
+    def drain(i, c):
+        copy_to(lax.rem(me + i, n)).wait_send()
+        return c
+
+    lax.fori_loop(1, n, drain, 0)
+
+
+def gather_fwd(kv_local, q, rpos, rlab, cpos, clab, n):
+    rows, width = kv_local.shape
+    stacked = rpos.shape[0]
+    return pl.pallas_call(
+        functools.partial(gather_fwd_kernel, n),
+        out_shape=(
+            jax.ShapeDtypeStruct((n, rows, width), kv_local.dtype),
+            jax.ShapeDtypeStruct(q.shape, jnp.bfloat16),
+            jax.ShapeDtypeStruct((stacked, 1), jnp.float32),
+            jax.ShapeDtypeStruct((stacked, 1), jnp.float32),
+        ),
+        in_specs=vmem_specs(6),
+        out_specs=tuple(vmem_specs(4)),
+        scratch_shapes=[
+            pltpu.VMEM((stacked, HEAD_DIM), jnp.float32),
+            pltpu.SemaphoreType.DMA((n,)),
+            pltpu.SemaphoreType.DMA((n,)),
+        ],
+        compiler_params=pltpu.CompilerParams(collective_id=0, has_side_effects=True),
+    )(kv_local, q, rpos, rlab, cpos, clab)
+
+
+def bwd_scatter_kernel(n, q_ref, g_ref, o_ref, kv_ref, rpos_ref, rlab_ref, cpos_ref, clab_ref,
+                       m_ref, l_ref, dq_ref, red_ref, terms_sc, held, dq_sc, send_sem, recv_sem):
+    me = lax.axis_index("ctx")
+    greet_all(n, me)
+    scale = 1.0 / math.sqrt(HEAD_DIM)
+    queries = stack_heads(q_ref)
+    grads = stack_heads(g_ref)
+    outs = stack_heads(o_ref)
+    delta = jnp.sum(grads.astype(jnp.float32) * outs.astype(jnp.float32), axis=-1, keepdims=True)
+    rpos = rpos_ref[...]
+    rlab = rlab_ref[...]
+    row_max = m_ref[...]
+    inv_total = 1.0 / l_ref[...]
+    dq_sc[...] = jnp.zeros(dq_sc.shape, jnp.float32)
+
+    def copy_to(peer):
+        return pltpu.make_async_remote_copy(
+            terms_sc.at[peer], held.at[me], send_sem.at[peer], recv_sem.at[me],
+            device_id={"ctx": peer}, device_id_type=MESH)
+
+    def copy_from(src):
+        return pltpu.make_async_remote_copy(
+            terms_sc.at[src], held.at[src], send_sem.at[src], recv_sem.at[src],
+            device_id={"ctx": src}, device_id_type=MESH)
+
+    def block_terms(p):
+        block = kv_ref[p]
+        keys = block[:, :HEAD_DIM]
+        values = block[:, HEAD_DIM:]
+        visible = column_visible(cpos_ref, clab_ref, p, rpos, rlab)
+        scores = lax.dot_general(queries, keys, NT_DIMS, preferred_element_type=jnp.float32) * scale
+        probs = jnp.where(visible, jnp.exp(scores - row_max), 0.0) * inv_total
+        dprob = lax.dot_general(grads, values, NT_DIMS, preferred_element_type=jnp.float32)
+        dscore_b = (probs * (dprob - delta)).astype(jnp.bfloat16)
+        probs_b = probs.astype(jnp.bfloat16)
+        dq_sc[...] += jnp.dot(dscore_b, keys, preferred_element_type=jnp.float32)
+        key_term = lax.dot_general(dscore_b, queries, TN_DIMS, preferred_element_type=jnp.float32) * scale
+        value_term = lax.dot_general(probs_b, grads, TN_DIMS, preferred_element_type=jnp.float32)
+        return jnp.concatenate([key_term, value_term], axis=1)
+
+    red_ref[...] = block_terms(me)
+
+    def step(i, c):
+        peer = lax.rem(me + i, n)
+        terms_sc[peer] = block_terms(peer).astype(terms_sc.dtype)
+
+        @pl.when(i >= 2)
+        def _():
+            copy_to(lax.rem(me + i - 1, n)).start()
+
+        return c
+
+    lax.fori_loop(1, n, step, 0)
+    copy_to(lax.rem(me + n - 1, n)).start()
+    unstack_heads(dq_ref, (dq_sc[...] * scale).astype(dq_ref.dtype))
+
+    def arrive(i, c):
+        src = lax.rem(me + n - i, n)
+        copy_from(src).wait_recv()
+        red_ref[...] += held[src].astype(jnp.float32)
+        return c
+
+    lax.fori_loop(1, n, arrive, 0)
+
+    def drain(i, c):
+        copy_to(lax.rem(me + i, n)).wait_send()
+        return c
+
+    lax.fori_loop(1, n, drain, 0)
+
+
+def bwd_scatter(q, g, o, kv, rpos, rlab, cpos, clab, m, l, n):
+    _, rows, width = kv.shape
+    stacked = rpos.shape[0]
+    return pl.pallas_call(
+        functools.partial(bwd_scatter_kernel, n),
+        out_shape=(
+            jax.ShapeDtypeStruct(q.shape, jnp.bfloat16),
+            jax.ShapeDtypeStruct((rows, width), jnp.float32),
+        ),
+        in_specs=vmem_specs(10),
+        out_specs=tuple(vmem_specs(2)),
+        scratch_shapes=[
+            pltpu.VMEM(kv.shape, jnp.bfloat16),
+            pltpu.VMEM(kv.shape, jnp.bfloat16),
+            pltpu.VMEM((stacked, HEAD_DIM), jnp.float32),
+            pltpu.SemaphoreType.DMA((n,)),
+            pltpu.SemaphoreType.DMA((n,)),
+        ],
+        compiler_params=pltpu.CompilerParams(collective_id=1, has_side_effects=True),
     )(q, g, o, kv, rpos, rlab, cpos, clab, m, l)
 
 
@@ -254,15 +439,14 @@
     own_label = lax.dynamic_slice_in_dim(labels, ctx_index * local_rows, local_rows, 0)
     rpos = jnp.tile(own_pos, heads_here)[:, None]
     rlab = jnp.tile(own_label, heads_here)[:, None]
-    cpos = positions[None, :]
-    clab = labels[None, :]
-    kv_all = ctx_gather(jnp.concatenate([key_rows, value_rows], axis=1), ctx_size)
-    kv_all = kv_all.reshape(total_rows, kv_all.shape[2])
-    attn_local, row_max, total = attention_fwd(query_rows, kv_all, rpos, rlab, cpos, clab)
+    cpos = positions.reshape(ctx_size, local_rows)
+    clab = labels.reshape(ctx_size, local_rows)
+    kv_local = jnp.concatenate([key_rows, value_rows], axis=1)
+    kv_all, attn_local, row_max, total = gather_fwd(
+        kv_local, query_rows, rpos, rlab, cpos, clab, ctx_size)
     grad_rows = fetch_grad(out_grad)
-    query_grad, terms = attention_bwd(
-        query_rows, grad_rows, attn_local, kv_all, rpos, rlab, cpos, clab, row_max, total)
-    reduced = ctx_reduce_scatter(terms.reshape(ctx_size, local_rows, terms.shape[1]), ctx_size)
+    query_grad, reduced = bwd_scatter(
+        query_rows, grad_rows, attn_local, kv_all, rpos, rlab, cpos, clab, row_max, total, ctx_size)
     key_grad = reduced[:, :HEAD_DIM].astype(jnp.bfloat16)
     value_grad = reduced[:, HEAD_DIM:].astype(jnp.bfloat16)
     attn_spread = spread_output(attn_local)

time: 147 us -> 158 us (1.075)
  starting transfers between devices: 12.4 us -> 17.3 us
  Pallas kernels: 120 us -> 124 us
  local copies, waits for them, and re-layouts: 5.29 us -> 7.22 us
    all_to_all x1, starting transfers between devices: 3.91 us -> 8.82 us  [spread_output(): lax.all_to_all(attn_flat, 'tp', split_axis=0, concat_axis=1, tiled=True)]
    pallas_call x4 -> x2, Pallas kernels: 120 us -> 124 us  [the longest x1 74.1 us: gather_fwd(): pl.pallas_call(functools.partial(gather_fwd_kernel, n), out_shape=(jax.Sh...]
    unnamed x8 -> x7, local copies, waits for them, and re-layouts: 0.02 us -> 1.68 us
  transfers between devices with their start and end apart: 2 -> 2, of which waited for: 0 -> 0; matrix products, arithmetic and copies ran while one was open for 7% -> 5% of each run, Pallas kernels for 83% -> 79%
where the time goes in v4:
time: 158 us; the launch traced here: 156 us
  Pallas kernels  124 us (78%)
  starting transfers between devices  17.3 us (11%)
  local copies, waits for them, and re-layouts  7.22 us (5%)
  other arithmetic  6.89 us (4%)
    pallas_call x1, Pallas kernels, gather_fwd(): pl.pallas_call(functools.partial(gather_fwd_kernel, n), out_shape=(jax.Sh...  74.1 us
    pallas_call x1, Pallas kernels, bwd_scatter(): pl.pallas_call(functools.partial(bwd_scatter_kernel, n), out_shape=(jax.S...  50.1 us
    all_to_all x1, starting transfers between devices, spread_output(): lax.all_to_all(attn_flat, 'tp', split_axis=0, concat_axis=1, tiled=True)  8.82 us
    all_to_all x1, starting transfers between devices, fetch_grad(): lax.all_to_all(out_grad, 'tp', split_axis=1, concat_axis=0, tiled=True)  8.47 us
    add x2, other arithmetic, on_device(): (positions >= prompt_end).astype(jnp.int32)  3.17 us
  transfers between devices with their start and end apart: 2, of which 0 were waited for; matrix products, arithmetic and copies ran while one was open for 5% of the time, Pallas kernels for 79%

profile of v4, /device:TPU:16, one launch (start us, length us, event | category | flops | bytes accessed | tf_op | source)
XLA Modules:
  0.0 156.3 jit_solution(4409216046793100953)
XLA Ops:
  0.7 1.7 %copy.21 = bf16[2,8,8,1024]{3,2,0,1:T(8,128)(2,1)} copy(bf16[2,8,8,1024]{3,2,1,0:T(8,128)(2,1)} %bitcast.16) | data formatting | bytes 524288 | tf_op jit(solution)/shard_map/all_to_all | solution.py:117
  2.3 8.5 %all-to-all-start.1 = ((bf16[16,8,1024]{2,0,1:T(8,128)(2,1)}), bf16[16,8,1024]{2,0,1:T(8,128)(2,1)S(1)}, u32[]{:S(2)}, u32[]{:S(2)}) async-start(bf16[16,8,1024]{2,0,1:T(8,128)(2,1)} %bitcast.12), calls=%async_computation.1 | async-start | bytes 524288 | tf_op jit(solution)/shard_map/all_to_all | solution.py:117
  10.8 0.7 broadcast_multiply_fusion
  11.5 0.1 iota_add_fusion
  11.5 1.4 convert_reduce_fusion.1
  13.0 0.1 add.49
  13.1 0.1 add.53
  13.2 0.1 add.50
  13.3 0.1 add.51
  13.3 0.1 add.46
  13.4 1.3 fusion
  14.7 1.0 copy.12.rpos_ref
  15.8 1.0 copy.13.rlab_ref
  16.8 0.6 pad_maximum_fusion.kv_src
  17.5 1.9 %convert_add_fusion = (s32[32,128]{1,0:T(8,128)}, s32[32,128]{1,0:T(8,128)}) fusion(s32[]{:T(128)} %get-tuple-element.17, s32[]{:T(128)} %get-tuple-element.16, s32[32,128]{1,0:T(8,128)S(1)} %add.51, s32[128]{0:T(128)S(1)} %add.53), kind=kLoop, calls=%fused_computation.3 | loop fusion | flops 24576 | bytes 49672 | tf_op jit(solution)/shard_map/add | solution.py:437
  19.3 74.1 %shard_map.93 = (bf16[32,128,256]{2,1,0:T(8,128)(2,1)}, bf16[128,1024]{1,0:T(8,128)(2,1)}, f32[1024,1]{1,0:T(8,128)}, f32[1024,1]{1,0:T(8,128)}) custom-call(bf16[128,256]{1,0:T(8,128)(2,1)} %pad_maximum_fusion.kv_src, bf16[128,1024]{1,0:T(8,128)(2,1)} %q_ref.3, s32[1024,1]{1,0:T(8,128)} %copy.12.rpos_ref, s32[1024,1]{1,0:T(8,128)} %copy.13.rlab_ref, ...), custom_call_target="tpu_custom_call" | custom-call | tf_op jit(solution)/shard_map/pallas_call | solution.py:315
  93.5 0.0 copy-start
  93.5 8.8 %all-to-all-start = ((bf16[8,16,1024]{2,1,0:T(8,128)(2,1)}), bf16[8,16,1024]{2,1,0:T(8,128)(2,1)S(1)}, u32[]{:S(2)}, u32[]{:S(2)}) async-start(bf16[8,16,1024]{2,1,0:T(8,128)(2,1)} %bitcast.14), calls=%async_computation | async-start | bytes 524288 | tf_op jit(solution)/shard_map/all_to_all | solution.py:121
  102.3 50.1 %shard_map.94 = (bf16[128,1024]{1,0:T(8,128)(2,1)}, f32[128,256]{1,0:T(8,128)}) custom-call(bf16[128,1024]{1,0:T(8,128)(2,1)} %q_ref.3, bf16[128,1024]{1,0:T(8,128)(2,1)} %bitcast.13, bf16[128,1024]{1,0:T(8,128)(2,1)} %get-tuple-element.10.o_ref, bf16[32,128,256]{2,1,0:T(8,128)(2,1)} %get-tuple-element.11.kv_ref, s32[1024,1]{1,0:T(8,128)} %copy.12.rpos_ref, ...), custom_call_target="tpu_custom_call" | custom-call | tf_op jit(solution)/shard_map/pallas_call | solution.py:408
  152.4 0.0 all-to-all-done
  152.4 0.7 copy.19
  153.1 0.9 convert.4
  154.0 0.6 fusion.1
  154.6 1.7 %copy.23 = bf16[128,1024]{1,0:T(8,128)(2,1)} copy(bf16[128,1024]{1,0:T(8,128)(2,1)} %get-tuple-element.29) | data formatting | bytes 524288
  (9 shorter events, 0.0 us)
Async XLA Ops:
  0.6 16.2 %copy-start.1 = (bf16[128,128]{1,0:T(8,128)(2,1)S(1)}, bf16[128,128]{1,0:T(8,128)(2,1)}, u32[]{:S(2)}) copy-start(bf16[128,128]{1,0:T(8,128)(2,1)} %param.8) | copy-start | bytes 98308
  0.6 16.2 %copy-start.2 = (bf16[128,128]{1,0:T(8,128)(2,1)S(1)}, bf16[128,128]{1,0:T(8,128)(2,1)}, u32[]{:S(2)}) copy-start(bf16[128,128]{1,0:T(8,128)(2,1)} %param.7) | copy-start | bytes 98308
  2.3 91.1 %all-to-all-start.1 = ((bf16[16,8,1024]{2,0,1:T(8,128)(2,1)}), bf16[16,8,1024]{2,0,1:T(8,128)(2,1)S(1)}, u32[]{:S(2)}, u32[]{:S(2)}) async-start(bf16[16,8,1024]{2,0,1:T(8,128)(2,1)} %bitcast.12), calls=%async_computation.1 | async-start | bytes 524288 | tf_op jit(solution)/shard_map/all_to_all | solution.py:117
  93.5 8.8 %copy-start = (bf16[16,8,1024]{2,0,1:T(8,128)(2,1)}, bf16[16,8,1024]{2,0,1:T(8,128)(2,1)S(1)}, u32[]{:S(2)}) copy-start(bf16[16,8,1024]{2,0,1:T(8,128)(2,1)S(1)} %all-to-all-done.1) | copy-start | bytes 786436
  93.5 58.9 %all-to-all-start = ((bf16[8,16,1024]{2,1,0:T(8,128)(2,1)}), bf16[8,16,1024]{2,1,0:T(8,128)(2,1)S(1)}, u32[]{:S(2)}, u32[]{:S(2)}) async-start(bf16[8,16,1024]{2,1,0:T(8,128)(2,1)} %bitcast.14), calls=%async_computation | async-start | bytes 524288 | tf_op jit(solution)/shard_map/all_to_all | solution.py:121

commit v5 on v4

--- a/solution.py
+++ b/solution.py
@@ -122,6 +122,7 @@
 
 
 KEY_BLOCK = 512
+SEND_WINDOW = 6
 NT_DIMS = (((1,), (1,)), ((), ()))
 TN_DIMS = (((0,), (0,)), ((), ()))
 
@@ -275,11 +276,13 @@
             kv_src, kv_out.at[src], send_sem.at[src], recv_sem.at[src],
             device_id={"ctx": src}, device_id_type=MESH)
 
+    window = min(SEND_WINDOW, n - 1)
+
     def send(i, c):
         copy_to(lax.rem(me + i, n)).start()
         return c
 
-    lax.fori_loop(1, n, send, 0)
+    lax.fori_loop(1, window + 1, send, 0)
     own = kv_src[...]
     kv_out[me] = own
     queries = stack_heads(q_ref)
@@ -297,6 +300,12 @@
         block = kv_out[src]
         fwd_step(queries, block[:, :HEAD_DIM], block[:, HEAD_DIM:],
                  column_visible(cpos_ref, clab_ref, src, rpos, rlab), m_ref, l_ref, acc_sc)
+
+        @pl.when(i + window <= n - 1)
+        def _():
+            copy_to(lax.rem(me + i, n)).wait_send()
+            copy_to(lax.rem(me + i + window, n)).start()
+
         return c
 
     lax.fori_loop(1, n, arrive, 0)
@@ -306,7 +315,7 @@
         copy_to(lax.rem(me + i, n)).wait_send()
         return c
 
-    lax.fori_loop(1, n, drain, 0)
+    lax.fori_loop(n - window, n, drain, 0)
 
 
 def gather_fwd(kv_local, q, rpos, rlab, cpos, clab, n):

time: 158 us -> 147 us (0.930)
  the two profiles are of different devices: /device:TPU:16 before, /device:TPU:26 now
where the time goes in v5:
time: 147 us
  Pallas kernels  118 us (80%)
  starting transfers between devices  14.2 us (10%)
  local copies, waits for them, and re-layouts  7.22 us (5%)
  other arithmetic  6.89 us (5%)
    pallas_call x1, Pallas kernels, gather_fwd(): pl.pallas_call(functools.partial(gather_fwd_kernel, n), out_shape=(jax.Sh...  69 us
    pallas_call x1, Pallas kernels, bwd_scatter(): pl.pallas_call(functools.partial(bwd_scatter_kernel, n), out_shape=(jax.S...  48.9 us
    all_to_all x1, starting transfers between devices, fetch_grad(): lax.all_to_all(out_grad, 'tp', split_axis=1, concat_axis=0, tiled=True)  8.47 us
    all_to_all x1, starting transfers between devices, spread_output(): lax.all_to_all(attn_flat, 'tp', split_axis=0, concat_axis=1, tiled=True)  5.7 us
    add x2, other arithmetic, on_device(): (positions >= prompt_end).astype(jnp.int32)  3.17 us
  transfers between devices with their start and end apart: 2, of which 0 were waited for; matrix products, arithmetic and copies ran while one was open for 6% of the time, Pallas kernels for 80%

profile of v5, /device:TPU:26, one launch (start us, length us, event | category | flops | bytes accessed | tf_op | source)
XLA Modules:
  0.0 147.0 jit_solution(11317032675177965044)
XLA Ops:
  0.7 1.7 %copy.21 = bf16[2,8,8,1024]{3,2,0,1:T(8,128)(2,1)} copy(bf16[2,8,8,1024]{3,2,1,0:T(8,128)(2,1)} %bitcast.16) | data formatting | bytes 524288 | tf_op jit(solution)/shard_map/all_to_all | solution.py:117
  2.3 8.5 %all-to-all-start.1 = ((bf16[16,8,1024]{2,0,1:T(8,128)(2,1)}), bf16[16,8,1024]{2,0,1:T(8,128)(2,1)S(1)}, u32[]{:S(2)}, u32[]{:S(2)}) async-start(bf16[16,8,1024]{2,0,1:T(8,128)(2,1)} %bitcast.12), calls=%async_computation.1 | async-start | bytes 524288 | tf_op jit(solution)/shard_map/all_to_all | solution.py:117
  10.8 0.7 broadcast_multiply_fusion
  11.5 0.1 iota_add_fusion
  11.5 1.4 convert_reduce_fusion.1
  13.0 0.1 add.49
  13.1 0.1 add.53
  13.2 0.1 add.50
  13.3 0.1 add.51
  13.3 0.1 add.46
  13.4 1.3 fusion
  14.7 1.0 copy.12.rpos_ref
  15.8 1.0 copy.13.rlab_ref
  16.8 0.6 pad_maximum_fusion.kv_src
  17.5 1.9 %convert_add_fusion = (s32[32,128]{1,0:T(8,128)}, s32[32,128]{1,0:T(8,128)}) fusion(s32[]{:T(128)} %get-tuple-element.17, s32[]{:T(128)} %get-tuple-element.16, s32[32,128]{1,0:T(8,128)S(1)} %add.51, s32[128]{0:T(128)S(1)} %add.53), kind=kLoop, calls=%fused_computation.3 | loop fusion | flops 24576 | bytes 49672 | tf_op jit(solution)/shard_map/add | solution.py:446
  19.3 69.0 %shard_map.93 = (bf16[32,128,256]{2,1,0:T(8,128)(2,1)}, bf16[128,1024]{1,0:T(8,128)(2,1)}, f32[1024,1]{1,0:T(8,128)}, f32[1024,1]{1,0:T(8,128)}) custom-call(bf16[128,256]{1,0:T(8,128)(2,1)} %pad_maximum_fusion.kv_src, bf16[128,1024]{1,0:T(8,128)(2,1)} %q_ref.3, s32[1024,1]{1,0:T(8,128)} %copy.12.rpos_ref, s32[1024,1]{1,0:T(8,128)} %copy.13.rlab_ref, ...), custom_call_target="tpu_custom_call" | custom-call | tf_op jit(solution)/shard_map/pallas_call | solution.py:324
  88.3 0.0 all-to-all-done.1
  88.4 0.0 copy-start
  88.4 5.7 %all-to-all-start = ((bf16[8,16,1024]{2,1,0:T(8,128)(2,1)}), bf16[8,16,1024]{2,1,0:T(8,128)(2,1)S(1)}, u32[]{:S(2)}, u32[]{:S(2)}) async-start(bf16[8,16,1024]{2,1,0:T(8,128)(2,1)} %bitcast.14), calls=%async_computation | async-start | bytes 524288 | tf_op jit(solution)/shard_map/all_to_all | solution.py:121
  94.1 48.9 %shard_map.94 = (bf16[128,1024]{1,0:T(8,128)(2,1)}, f32[128,256]{1,0:T(8,128)}) custom-call(bf16[128,1024]{1,0:T(8,128)(2,1)} %q_ref.3, bf16[128,1024]{1,0:T(8,128)(2,1)} %bitcast.13, bf16[128,1024]{1,0:T(8,128)(2,1)} %get-tuple-element.10.o_ref, bf16[32,128,256]{2,1,0:T(8,128)(2,1)} %get-tuple-element.11.kv_ref, s32[1024,1]{1,0:T(8,128)} %copy.12.rpos_ref, ...), custom_call_target="tpu_custom_call" | custom-call | tf_op jit(solution)/shard_map/pallas_call | solution.py:417
  143.0 0.7 copy.19
  143.7 0.9 convert.4
  144.7 0.6 fusion.1
  145.3 1.7 %copy.23 = bf16[128,1024]{1,0:T(8,128)(2,1)} copy(bf16[128,1024]{1,0:T(8,128)(2,1)} %get-tuple-element.29) | data formatting | bytes 524288
  (9 shorter events, 0.0 us)
Async XLA Ops:
  0.6 16.2 %copy-start.1 = (bf16[128,128]{1,0:T(8,128)(2,1)S(1)}, bf16[128,128]{1,0:T(8,128)(2,1)}, u32[]{:S(2)}) copy-start(bf16[128,128]{1,0:T(8,128)(2,1)} %param.8) | copy-start | bytes 98308
  0.6 16.2 %copy-start.2 = (bf16[128,128]{1,0:T(8,128)(2,1)S(1)}, bf16[128,128]{1,0:T(8,128)(2,1)}, u32[]{:S(2)}) copy-start(bf16[128,128]{1,0:T(8,128)(2,1)} %param.7) | copy-start | bytes 98308
  2.3 86.0 %all-to-all-start.1 = ((bf16[16,8,1024]{2,0,1:T(8,128)(2,1)}), bf16[16,8,1024]{2,0,1:T(8,128)(2,1)S(1)}, u32[]{:S(2)}, u32[]{:S(2)}) async-start(bf16[16,8,1024]{2,0,1:T(8,128)(2,1)} %bitcast.12), calls=%async_computation.1 | async-start | bytes 524288 | tf_op jit(solution)/shard_map/all_to_all | solution.py:117
  88.4 5.7 %copy-start = (bf16[16,8,1024]{2,0,1:T(8,128)(2,1)}, bf16[16,8,1024]{2,0,1:T(8,128)(2,1)S(1)}, u32[]{:S(2)}) copy-start(bf16[16,8,1024]{2,0,1:T(8,128)(2,1)S(1)} %all-to-all-done.1) | copy-start | bytes 786436
  88.4 54.6 %all-to-all-start = ((bf16[8,16,1024]{2,1,0:T(8,128)(2,1)}), bf16[8,16,1024]{2,1,0:T(8,128)(2,1)S(1)}, u32[]{:S(2)}, u32[]{:S(2)}) async-start(bf16[8,16,1024]{2,1,0:T(8,128)(2,1)} %bitcast.14), calls=%async_computation | async-start | bytes 524288 | tf_op jit(solution)/shard_map/all_to_all | solution.py:121

commit v6 on v5

--- a/solution.py
+++ b/solution.py
@@ -123,6 +123,7 @@
 
 KEY_BLOCK = 512
 SEND_WINDOW = 6
+ARRIVAL_GROUP = 4
 NT_DIMS = (((1,), (1,)), ((), ()))
 TN_DIMS = (((0,), (0,)), ((), ()))
 
@@ -276,39 +277,51 @@
             kv_src, kv_out.at[src], send_sem.at[src], recv_sem.at[src],
             device_id={"ctx": src}, device_id_type=MESH)
 
-    window = min(SEND_WINDOW, n - 1)
+    group = math.gcd(n, ARRIVAL_GROUP)
+    window = min(max(SEND_WINDOW, group), n - 1)
 
     def send(i, c):
         copy_to(lax.rem(me + i, n)).start()
         return c
 
     lax.fori_loop(1, window + 1, send, 0)
-    own = kv_src[...]
-    kv_out[me] = own
+    kv_out[me] = kv_src[...]
     queries = stack_heads(q_ref)
     rpos = rpos_ref[...]
     rlab = rlab_ref[...]
     m_ref[...] = jnp.full(m_ref.shape, -jnp.inf, jnp.float32)
     l_ref[...] = jnp.zeros(l_ref.shape, jnp.float32)
     acc_sc[...] = jnp.zeros(acc_sc.shape, jnp.float32)
-    fwd_step(queries, own[:, :HEAD_DIM], own[:, HEAD_DIM:],
-             column_visible(cpos_ref, clab_ref, me, rpos, rlab), m_ref, l_ref, acc_sc)
-
-    def arrive(i, c):
-        src = lax.rem(me + n - i, n)
-        copy_from(src).wait_recv()
-        block = kv_out[src]
-        fwd_step(queries, block[:, :HEAD_DIM], block[:, HEAD_DIM:],
-                 column_visible(cpos_ref, clab_ref, src, rpos, rlab), m_ref, l_ref, acc_sc)
-
-        @pl.when(i + window <= n - 1)
-        def _():
-            copy_to(lax.rem(me + i, n)).wait_send()
-            copy_to(lax.rem(me + i + window, n)).start()
-
-        return c
-
-    lax.fori_loop(1, n, arrive, 0)
+
+    def arrive(j, c):
+        blocks, cposs, clabs = [], [], []
+        for t in range(group):
+            i = j * group + t
+            src = lax.rem(me + n - i, n)
+
+            @pl.when(i > 0)
+            def _():
+                copy_from(src).wait_recv()
+
+            blocks.append(kv_out[src])
+            cposs.append(cpos_ref[pl.ds(src, 1), :])
+            clabs.append(clab_ref[pl.ds(src, 1), :])
+        block = jnp.concatenate(blocks, axis=0)
+        cpos = jnp.concatenate(cposs, axis=1)
+        clab = jnp.concatenate(clabs, axis=1)
+        visible = (cpos <= rpos) & ((clab == 0) | (clab == rlab))
+        fwd_step(queries, block[:, :HEAD_DIM], block[:, HEAD_DIM:], visible, m_ref, l_ref, acc_sc)
+        for t in range(group):
+            i = j * group + t
+
+            @pl.when((i > 0) & (i + window <= n - 1))
+            def _():
+                copy_to(lax.rem(me + i, n)).wait_send()
+                copy_to(lax.rem(me + i + window, n)).start()
+
+        return c
+
+    lax.fori_loop(0, n // group, arrive, 0)
     unstack_heads(o_ref, (acc_sc[...] / l_ref[...]).astype(o_ref.dtype))
 
     def drain(i, c):

time: 147 us -> 152 us (1.034)
  the two profiles are of different devices: /device:TPU:26 before, /device:TPU:16 now
where the time goes in v6:
time: 152 us; the launch traced here: 150 us
  Pallas kernels  119 us (78%)
  starting transfers between devices  15.9 us (10%)
  local copies, waits for them, and re-layouts  7.22 us (5%)
  other arithmetic  6.89 us (5%)
    pallas_call x1, Pallas kernels, gather_fwd(): pl.pallas_call(functools.partial(gather_fwd_kernel, n), out_shape=(jax.Sh...  68.3 us
    pallas_call x1, Pallas kernels, bwd_scatter(): pl.pallas_call(functools.partial(bwd_scatter_kernel, n), out_shape=(jax.S...  51.1 us
    all_to_all x1, starting transfers between devices, fetch_grad(): lax.all_to_all(out_grad, 'tp', split_axis=1, concat_axis=0, tiled=True)  8.47 us
    all_to_all x1, starting transfers between devices, spread_output(): lax.all_to_all(attn_flat, 'tp', split_axis=0, concat_axis=1, tiled=True)  7.41 us
    add x2, other arithmetic, on_device(): (positions >= prompt_end).astype(jnp.int32)  3.17 us
  transfers between devices with their start and end apart: 2, of which 0 were waited for; matrix products, arithmetic and copies ran while one was open for 6% of the time, Pallas kernels for 80%

profile of v6, /device:TPU:16, one launch (start us, length us, event | category | flops | bytes accessed | tf_op | source)
XLA Modules:
  0.0 150.1 jit_solution(316152381945951329)
XLA Ops:
  0.7 1.7 %copy.21 = bf16[2,8,8,1024]{3,2,0,1:T(8,128)(2,1)} copy(bf16[2,8,8,1024]{3,2,1,0:T(8,128)(2,1)} %bitcast.16) | data formatting | bytes 524288 | tf_op jit(solution)/shard_map/all_to_all | solution.py:117
  2.3 8.5 %all-to-all-start.1 = ((bf16[16,8,1024]{2,0,1:T(8,128)(2,1)}), bf16[16,8,1024]{2,0,1:T(8,128)(2,1)S(1)}, u32[]{:S(2)}, u32[]{:S(2)}) async-start(bf16[16,8,1024]{2,0,1:T(8,128)(2,1)} %bitcast.12), calls=%async_computation.1 | async-start | bytes 524288 | tf_op jit(solution)/shard_map/all_to_all | solution.py:117
  10.8 0.7 broadcast_multiply_fusion
  11.5 0.1 iota_add_fusion
  11.5 1.4 convert_reduce_fusion.1
  13.0 0.1 add.49
  13.1 0.1 add.53
  13.2 0.1 add.50
  13.3 0.1 add.51
  13.3 0.1 add.46
  13.4 1.3 fusion
  14.7 1.0 copy.12.rpos_ref
  15.8 1.0 copy.13.rlab_ref
  16.8 0.6 pad_maximum_fusion.kv_src
  17.5 1.9 %convert_add_fusion = (s32[32,128]{1,0:T(8,128)}, s32[32,128]{1,0:T(8,128)}) fusion(s32[]{:T(128)} %get-tuple-element.17, s32[]{:T(128)} %get-tuple-element.16, s32[32,128]{1,0:T(8,128)S(1)} %add.51, s32[128]{0:T(128)S(1)} %add.53), kind=kLoop, calls=%fused_computation.3 | loop fusion | flops 24576 | bytes 49672 | tf_op jit(solution)/shard_map/add | solution.py:459
  19.3 68.3 %shard_map.93 = (bf16[32,128,256]{2,1,0:T(8,128)(2,1)}, bf16[128,1024]{1,0:T(8,128)(2,1)}, f32[1024,1]{1,0:T(8,128)}, f32[1024,1]{1,0:T(8,128)}) custom-call(bf16[128,256]{1,0:T(8,128)(2,1)} %pad_maximum_fusion.kv_src, bf16[128,1024]{1,0:T(8,128)(2,1)} %q_ref.3, s32[1024,1]{1,0:T(8,128)} %copy.12.rpos_ref, s32[1024,1]{1,0:T(8,128)} %copy.13.rlab_ref, ...), custom_call_target="tpu_custom_call" | custom-call | tf_op jit(solution)/shard_map/pallas_call | solution.py:337
  87.7 0.0 copy-start
  87.7 7.4 %all-to-all-start = ((bf16[8,16,1024]{2,1,0:T(8,128)(2,1)}), bf16[8,16,1024]{2,1,0:T(8,128)(2,1)S(1)}, u32[]{:S(2)}, u32[]{:S(2)}) async-start(bf16[8,16,1024]{2,1,0:T(8,128)(2,1)} %bitcast.14), calls=%async_computation | async-start | bytes 524288 | tf_op jit(solution)/shard_map/all_to_all | solution.py:121
  95.1 51.1 %shard_map.94 = (bf16[128,1024]{1,0:T(8,128)(2,1)}, f32[128,256]{1,0:T(8,128)}) custom-call(bf16[128,1024]{1,0:T(8,128)(2,1)} %q_ref.3, bf16[128,1024]{1,0:T(8,128)(2,1)} %bitcast.13, bf16[128,1024]{1,0:T(8,128)(2,1)} %get-tuple-element.10.o_ref, bf16[32,128,256]{2,1,0:T(8,128)(2,1)} %get-tuple-element.11.kv_ref, s32[1024,1]{1,0:T(8,128)} %copy.12.rpos_ref, ...), custom_call_target="tpu_custom_call" | custom-call | tf_op jit(solution)/shard_map/pallas_call | solution.py:430
  146.2 0.0 all-to-all-done
  146.2 0.7 copy.19
  146.9 0.9 convert.4
  147.8 0.6 fusion.1
  148.5 1.7 %copy.23 = bf16[128,1024]{1,0:T(8,128)(2,1)} copy(bf16[128,1024]{1,0:T(8,128)(2,1)} %get-tuple-element.29) | data formatting | bytes 524288
  (9 shorter events, 0.0 us)
Async XLA Ops:
  0.6 16.2 %copy-start.1 = (bf16[128,128]{1,0:T(8,128)(2,1)S(1)}, bf16[128,128]{1,0:T(8,128)(2,1)}, u32[]{:S(2)}) copy-start(bf16[128,128]{1,0:T(8,128)(2,1)} %param.8) | copy-start | bytes 98308
  0.6 16.2 %copy-start.2 = (bf16[128,128]{1,0:T(8,128)(2,1)S(1)}, bf16[128,128]{1,0:T(8,128)(2,1)}, u32[]{:S(2)}) copy-start(bf16[128,128]{1,0:T(8,128)(2,1)} %param.7) | copy-start | bytes 98308
  2.3 85.3 %all-to-all-start.1 = ((bf16[16,8,1024]{2,0,1:T(8,128)(2,1)}), bf16[16,8,1024]{2,0,1:T(8,128)(2,1)S(1)}, u32[]{:S(2)}, u32[]{:S(2)}) async-start(bf16[16,8,1024]{2,0,1:T(8,128)(2,1)} %bitcast.12), calls=%async_computation.1 | async-start | bytes 524288 | tf_op jit(solution)/shard_map/all_to_all | solution.py:117
  87.7 7.4 %copy-start = (bf16[16,8,1024]{2,0,1:T(8,128)(2,1)}, bf16[16,8,1024]{2,0,1:T(8,128)(2,1)S(1)}, u32[]{:S(2)}) copy-start(bf16[16,8,1024]{2,0,1:T(8,128)(2,1)S(1)} %all-to-all-done.1) | copy-start | bytes 786436
  87.7 58.5 %all-to-all-start = ((bf16[8,16,1024]{2,1,0:T(8,128)(2,1)}), bf16[8,16,1024]{2,1,0:T(8,128)(2,1)S(1)}, u32[]{:S(2)}, u32[]{:S(2)}) async-start(bf16[8,16,1024]{2,1,0:T(8,128)(2,1)} %bitcast.14), calls=%async_computation | async-start | bytes 524288 | tf_op jit(solution)/shard_map/all_to_all | solution.py:121

commit v7 on v4

--- a/solution.py
+++ b/solution.py
@@ -64,53 +64,6 @@
         scratch_shapes=[pltpu.SemaphoreType.DMA((n,)), pltpu.SemaphoreType.DMA((n,))],
         compiler_params=pltpu.CompilerParams(collective_id=0, has_side_effects=True),
     )(block)
-
-
-def scatter_kernel(n, terms_ref, out_ref, held, send_sem, recv_sem):
-    me = lax.axis_index("ctx")
-    greet_all(n, me)
-
-    def copy_to(peer):
-        return pltpu.make_async_remote_copy(
-            terms_ref.at[peer], held.at[me], send_sem.at[peer], recv_sem.at[me],
-            device_id={"ctx": peer}, device_id_type=MESH)
-
-    def copy_from(src):
-        return pltpu.make_async_remote_copy(
-            terms_ref.at[src], held.at[src], send_sem.at[src], recv_sem.at[src],
-            device_id={"ctx": src}, device_id_type=MESH)
-
-    def send(i, c):
-        copy_to(lax.rem(me + i, n)).start()
-        return c
-
-    lax.fori_loop(1, n, send, 0)
-    out_ref[...] = terms_ref[me].astype(jnp.float32)
-
-    def wait(i, c):
-        copy_to(lax.rem(me + i, n)).wait_send()
-        src = lax.rem(me + n - i, n)
-        copy_from(src).wait_recv()
-        out_ref[...] += held[src].astype(jnp.float32)
-        return c
-
-    lax.fori_loop(1, n, wait, 0)
-
-
-def ctx_reduce_scatter(terms, n):
-    _, rows, width = terms.shape
-    return pl.pallas_call(
-        functools.partial(scatter_kernel, n),
-        out_shape=jax.ShapeDtypeStruct((rows, width), jnp.float32),
-        in_specs=[pl.BlockSpec(memory_space=pltpu.VMEM)],
-        out_specs=pl.BlockSpec(memory_space=pltpu.VMEM),
-        scratch_shapes=[
-            pltpu.VMEM(terms.shape, terms.dtype),
-            pltpu.SemaphoreType.DMA((n,)),
-            pltpu.SemaphoreType.DMA((n,)),
-        ],
-        compiler_params=pltpu.CompilerParams(collective_id=1, has_side_effects=True),
-    )(terms)
 
 
 def fetch_grad(out_grad):
@@ -175,37 +128,6 @@
     unstack_heads(o_ref, (acc_sc[...] / l_ref[...]).astype(o_ref.dtype))
 
 
-def bwd_kernel(q_ref, g_ref, o_ref, kv_ref, rpos_ref, rlab_ref, cpos_ref, clab_ref, m_ref, l_ref,
-               dq_ref, terms_ref, dq_sc):
-    scale = 1.0 / math.sqrt(HEAD_DIM)
-    queries = stack_heads(q_ref)
-    grads = stack_heads(g_ref)
-    outs = stack_heads(o_ref)
-    delta = jnp.sum(grads.astype(jnp.float32) * outs.astype(jnp.float32), axis=-1, keepdims=True)
-    rpos = rpos_ref[...]
-    rlab = rlab_ref[...]
-    row_max = m_ref[...]
-    inv_total = 1.0 / l_ref[...]
-    dq_sc[...] = jnp.zeros(dq_sc.shape, jnp.float32)
-
-    def body(kb, c):
-        start, keys, values, visible = key_block(kv_ref, cpos_ref, clab_ref, rpos, rlab, kb)
-        scores = lax.dot_general(queries, keys, NT_DIMS, preferred_element_type=jnp.float32) * scale
-        probs = jnp.where(visible, jnp.exp(scores - row_max), 0.0) * inv_total
-        dprob = lax.dot_general(grads, values, NT_DIMS, preferred_element_type=jnp.float32)
-        dscore_b = (probs * (dprob - delta)).astype(jnp.bfloat16)
-        probs_b = probs.astype(jnp.bfloat16)
-        dq_sc[...] += jnp.dot(dscore_b, keys, preferred_element_type=jnp.float32)
-        key_term = lax.dot_general(dscore_b, queries, TN_DIMS, preferred_element_type=jnp.float32) * scale
-        value_term = lax.dot_general(probs_b, grads, TN_DIMS, preferred_element_type=jnp.float32)
-        terms_ref[pl.ds(start, KEY_BLOCK), :HEAD_DIM] = key_term.astype(terms_ref.dtype)
-        terms_ref[pl.ds(start, KEY_BLOCK), HEAD_DIM:] = value_term.astype(terms_ref.dtype)
-        return c
-
-    lax.fori_loop(0, kv_ref.shape[0] // KEY_BLOCK, body, 0)
-    unstack_heads(dq_ref, (dq_sc[...] * scale).astype(dq_ref.dtype))
-
-
 def vmem_specs(n):
     return [pl.BlockSpec(memory_space=pltpu.VMEM)] * n
 
@@ -225,20 +147,6 @@
     )(q, kv, rpos, rlab, cpos, clab)
 
 
-def attention_bwd(q, g, o, kv, rpos, rlab, cpos, clab, m, l):
-    stacked = rpos.shape[0]
-    return pl.pallas_call(
-        bwd_kernel,
-        out_shape=(
-            jax.ShapeDtypeStruct(q.shape, jnp.bfloat16),
-            jax.ShapeDtypeStruct(kv.shape, jnp.bfloat16),
-        ),
-        in_specs=vmem_specs(10),
-        out_specs=tuple(vmem_specs(2)),
-        scratch_shapes=[pltpu.VMEM((stacked, HEAD_DIM), jnp.float32)],
-    )(q, g, o, kv, rpos, rlab, cpos, clab, m, l)
-
-
 def fwd_step(queries, keys, values, visible, m_sc, l_sc, acc_sc):
     scale = 1.0 / math.sqrt(HEAD_DIM)
     scores = lax.dot_general(queries, keys, NT_DIMS, preferred_element_type=jnp.float32) * scale
@@ -258,77 +166,6 @@
     cpos = cpos_ref[pl.ds(block, 1), :]
     clab = clab_ref[pl.ds(block, 1), :]
     return (cpos <= rpos) & ((clab == 0) | (clab == rlab))
-
-
-def gather_fwd_kernel(n, kv_src, q_ref, rpos_ref, rlab_ref, cpos_ref, clab_ref,
-                      kv_out, o_ref, m_ref, l_ref, acc_sc, send_sem, recv_sem):
-    me = lax.axis_index("ctx")
-    greet_all(n, me)
-
-    def copy_to(peer):
-        return pltpu.make_async_remote_copy(
-            kv_src, kv_out.at[me], send_sem.at[peer], recv_sem.at[me],
-            device_id={"ctx": peer}, device_id_type=MESH)
-
-    def copy_from(src):
-        return pltpu.make_async_remote_copy(
-            kv_src, kv_out.at[src], send_sem.at[src], recv_sem.at[src],
-            device_id={"ctx": src}, device_id_type=MESH)
-
-    def send(i, c):
-        copy_to(lax.rem(me + i, n)).start()
-        return c
-
-    lax.fori_loop(1, n, send, 0)
-    own = kv_src[...]
-    kv_out[me] = own
-    queries = stack_heads(q_ref)
-    rpos = rpos_ref[...]
-    rlab = rlab_ref[...]
-    m_ref[...] = jnp.full(m_ref.shape, -jnp.inf, jnp.float32)
-    l_ref[...] = jnp.zeros(l_ref.shape, jnp.float32)
-    acc_sc[...] = jnp.zeros(acc_sc.shape, jnp.float32)
-    fwd_step(queries, own[:, :HEAD_DIM], own[:, HEAD_DIM:],
-             column_visible(cpos_ref, clab_ref, me, rpos, rlab), m_ref, l_ref, acc_sc)
-
-    def arrive(i, c):
-        src = lax.rem(me + n - i, n)
-        copy_from(src).wait_recv()
-        block = kv_out[src]
-        fwd_step(queries, block[:, :HEAD_DIM], block[:, HEAD_DIM:],
-                 column_visible(cpos_ref, clab_ref, src, rpos, rlab), m_ref, l_ref, acc_sc)
-        return c
-
-    lax.fori_loop(1, n, arrive, 0)
-    unstack_heads(o_ref, (acc_sc[...] / l_ref[...]).astype(o_ref.dtype))
-
-    def drain(i, c):
-        copy_to(lax.rem(me + i, n)).wait_send()
-        return c
-
-    lax.fori_loop(1, n, drain, 0)
-
-
-def gather_fwd(kv_local, q, rpos, rlab, cpos, clab, n):
-    rows, width = kv_local.shape
-    stacked = rpos.shape[0]
-    return pl.pallas_call(
-        functools.partial(gather_fwd_kernel, n),
-        out_shape=(
-            jax.ShapeDtypeStruct((n, rows, width), kv_local.dtype),
-            jax.ShapeDtypeStruct(q.shape, jnp.bfloat16),
-            jax.ShapeDtypeStruct((stacked, 1), jnp.float32),
-            jax.ShapeDtypeStruct((stacked, 1), jnp.float32),
-        ),
-        in_specs=vmem_specs(6),
-        out_specs=tuple(vmem_specs(4)),
-        scratch_shapes=[
-            pltpu.VMEM((stacked, HEAD_DIM), jnp.float32),
-            pltpu.SemaphoreType.DMA((n,)),
-            pltpu.SemaphoreType.DMA((n,)),
-        ],
-        compiler_params=pltpu.CompilerParams(collective_id=0, has_side_effects=True),
-    )(kv_local, q, rpos, rlab, cpos, clab)
 
 
 def bwd_scatter_kernel(n, q_ref, g_ref, o_ref, kv_ref, rpos_ref, rlab_ref, cpos_ref, clab_ref,
@@ -442,8 +279,10 @@
     cpos = positions.reshape(ctx_size, local_rows)
     clab = labels.reshape(ctx_size, local_rows)
     kv_local = jnp.concatenate([key_rows, value_rows], axis=1)
-    kv_all, attn_local, row_max, total = gather_fwd(
-        kv_local, query_rows, rpos, rlab, cpos, clab, ctx_size)
+    kv_all = ctx_gather(kv_local, ctx_size)
+    attn_local, row_max, total = attention_fwd(
+        query_rows, kv_all.reshape(total_rows, kv_all.shape[2]), rpos, rlab,
+        positions[None, :], labels[None, :])
     grad_rows = fetch_grad(out_grad)
     query_grad, reduced = bwd_scatter(
         query_rows, grad_rows, attn_local, kv_all, rpos, rlab, cpos, clab, row_max, total, ctx_size)

time: 158 us -> 137 us (0.87)
  Pallas kernels: 124 us -> 106 us
  starting transfers between devices: 17.3 us -> 12.4 us
  other arithmetic: 6.89 us -> 8.5 us
    pallas_call x1 -> x2, Pallas kernels: 74.1 us -> 59.6 us  [the longest x1 39.9 us: ctx_gather(): pl.pallas_call(functools.partial(gather_kernel, n), out_shape=jax.ShapeDt...]
    all_to_all x1, starting transfers between devices: 8.82 us -> 3.91 us  [spread_output(): lax.all_to_all(attn_flat, 'tp', split_axis=0, concat_axis=1, tiled=True)]
    pallas_call x1, Pallas kernels: 50.1 us -> 46.4 us  [bwd_scatter(): pl.pallas_call(functools.partial(bwd_scatter_kernel, n), out_shape=(jax.S...]
    add x2 -> x3, other arithmetic: 3.17 us -> 4.85 us  [on_device(): (positions >= prompt_end).astype(jnp.int32)]
  transfers between devices with their start and end apart: 2 -> 2, of which waited for: 0 -> 0; matrix products, arithmetic and copies ran while one was open for 5% -> 8% of each run, Pallas kernels for 79% -> 79%
where the time goes in v7:
time: 137 us; the launch traced here: 135 us
  Pallas kernels  106 us (77%)
  starting transfers between devices  12.4 us (9%)
  other arithmetic  8.5 us (6%)
  local copies, waits for them, and re-layouts  7.33 us (5%)
    pallas_call x1, Pallas kernels, bwd_scatter(): pl.pallas_call(functools.partial(bwd_scatter_kernel, n), out_shape=(jax.S...  46.4 us
    pallas_call x1, Pallas kernels, ctx_gather(): pl.pallas_call(functools.partial(gather_kernel, n), out_shape=jax.ShapeDt...  39.9 us
    pallas_call x1, Pallas kernels, attention_fwd(): pl.pallas_call(fwd_kernel, out_shape=(jax.ShapeDtypeStruct(q.shape, jnp.b...  19.7 us
    all_to_all x1, starting transfers between devices, fetch_grad(): lax.all_to_all(out_grad, 'tp', split_axis=1, concat_axis=0, tiled=True)  8.47 us
    add x3, other arithmetic, on_device(): (positions >= prompt_end).astype(jnp.int32)  4.85 us
    all_to_all x1, starting transfers between devices, spread_output(): lax.all_to_all(attn_flat, 'tp', split_axis=0, concat_axis=1, tiled=True)  3.91 us
  transfers between devices with their start and end apart: 2, of which 0 were waited for; matrix products, arithmetic and copies ran while one was open for 8% of the time, Pallas kernels for 79%

profile of v7, /device:TPU:16, one launch (start us, length us, event | category | flops | bytes accessed | tf_op | source)
XLA Modules:
  0.0 134.9 jit_solution(8262910217551570926)
XLA Ops:
  0.7 1.7 %copy.21 = bf16[2,8,8,1024]{3,2,0,1:T(8,128)(2,1)} copy(bf16[2,8,8,1024]{3,2,1,0:T(8,128)(2,1)} %bitcast.18) | data formatting | bytes 524288 | tf_op jit(solution)/shard_map/all_to_all | solution.py:70
  2.3 8.5 %all-to-all-start.1 = ((bf16[16,8,1024]{2,0,1:T(8,128)(2,1)}), bf16[16,8,1024]{2,0,1:T(8,128)(2,1)S(1)}, u32[]{:S(2)}, u32[]{:S(2)}) async-start(bf16[16,8,1024]{2,0,1:T(8,128)(2,1)} %bitcast.13), calls=%async_computation.1 | async-start | bytes 524288 | tf_op jit(solution)/shard_map/all_to_all | solution.py:70
  10.8 0.7 broadcast_multiply_fusion
  11.5 0.1 iota_add_fusion
  11.5 0.1 add.72.cpos_ref
  11.7 1.4 %convert_reduce_fusion.1 = (s32[]{:T(128)}, s32[]{:T(128)}) fusion(s32[4096]{0:T(1024)} %param.10), kind=kLoop, calls=%fused_computation.8 | loop fusion | flops 24574 | bytes 16392 | tf_op jit(solution)/shard_map/reduce_sum | solution.py:272
  13.1 1.3 fusion.1
  14.3 1.0 copy.12.rpos_ref
  15.4 1.0 copy.13.rlab_ref
  16.4 0.6 pad_maximum_fusion.src_ref
  17.1 39.9 %shard_map.93.kv_ref = bf16[32,128,256]{2,1,0:T(8,128)(2,1)} custom-call(bf16[128,256]{1,0:T(8,128)(2,1)} %pad_maximum_fusion.src_ref), custom_call_target="tpu_custom_call" | custom-call | tf_op jit(solution)/shard_map/pallas_call | solution.py:59
  57.0 1.8 %fusion.clab_ref = s32[1,4096]{1,0:T(1,128)} fusion(s32[1,4096]{1,0:T(1,128)S(1)} %add.72.cpos_ref, s32[]{:T(128)} %get-tuple-element.15, s32[]{:T(128)} %get-tuple-element.14), kind=kLoop, calls=%fused_computation.5 | loop fusion | flops 20480 | bytes 32776 | tf_op jit(solution)/shard_map/add | solution.py:274
  58.8 19.7 %shard_map.94 = (bf16[128,1024]{1,0:T(8,128)(2,1)}, f32[1024,1]{1,0:T(8,128)}, f32[1024,1]{1,0:T(8,128)}) custom-call(bf16[128,1024]{1,0:T(8,128)(2,1)} %q_ref.3, bf16[4096,256]{1,0:T(8,128)(2,1)} %bitcast.14, s32[1024,1]{1,0:T(8,128)} %copy.12.rpos_ref, s32[1024,1]{1,0:T(8,128)} %copy.13.rlab_ref, s32[1,4096]{1,0:T(1,128)} %copy-done.1, s32[1,4096]{1,0:T(1,128)} %fusion.clab_ref), custom_call_target="tpu_custom_call" | custom-call | tf_op jit(solution)/shard_map/pallas_call | solution.py:137
  78.5 3.9 %all-to-all-start = ((bf16[8,16,1024]{2,1,0:T(8,128)(2,1)}), bf16[8,16,1024]{2,1,0:T(8,128)(2,1)S(1)}, u32[]{:S(2)}, u32[]{:S(2)}) async-start(bf16[8,16,1024]{2,1,0:T(8,128)(2,1)} %bitcast.16), calls=%async_computation | async-start | bytes 524288 | tf_op jit(solution)/shard_map/all_to_all | solution.py:74
  82.4 0.1 add.74
  82.5 0.1 add.78
  82.6 0.1 add.75
  82.7 0.1 add.76
  82.8 1.8 %convert_add_fusion = (s32[32,128]{1,0:T(8,128)}, s32[32,128]{1,0:T(8,128)}) fusion(s32[]{:T(128)} %get-tuple-element.15, s32[]{:T(128)} %get-tuple-element.14, s32[32,128]{1,0:T(8,128)S(1)} %add.76, s32[128]{0:T(128)S(1)} %add.78), kind=kLoop, calls=%fused_computation.6 | loop fusion | flops 24576 | bytes 49672 | tf_op jit(solution)/shard_map/add | solution.py:274
  84.6 46.4 %shard_map.95 = (bf16[128,1024]{1,0:T(8,128)(2,1)}, f32[128,256]{1,0:T(8,128)}) custom-call(bf16[128,1024]{1,0:T(8,128)(2,1)} %q_ref.3, bf16[128,1024]{1,0:T(8,128)(2,1)} %bitcast.15, bf16[128,1024]{1,0:T(8,128)(2,1)} %get-tuple-element.9.o_ref, bf16[32,128,256]{2,1,0:T(8,128)(2,1)} %shard_map.93.kv_ref, s32[1024,1]{1,0:T(8,128)} %copy.12.rpos_ref, ...), custom_call_target="tpu_custom_call" | custom-call | tf_op jit(solution)/shard_map/pallas_call | solution.py:245
  131.0 0.7 copy.19
  131.7 0.9 convert.4
  132.6 0.6 fusion.2
  133.3 1.7 %copy.23 = bf16[128,1024]{1,0:T(8,128)(2,1)} copy(bf16[128,1024]{1,0:T(8,128)(2,1)} %get-tuple-element.27) | data formatting | bytes 524288
  (14 shorter events, 0.1 us)
Async XLA Ops:
  0.6 15.8 %copy-start.2 = (bf16[128,128]{1,0:T(8,128)(2,1)S(1)}, bf16[128,128]{1,0:T(8,128)(2,1)}, u32[]{:S(2)}) copy-start(bf16[128,128]{1,0:T(8,128)(2,1)} %param.8) | copy-start | bytes 98308
  0.6 15.8 %copy-start.3 = (bf16[128,128]{1,0:T(8,128)(2,1)S(1)}, bf16[128,128]{1,0:T(8,128)(2,1)}, u32[]{:S(2)}) copy-start(bf16[128,128]{1,0:T(8,128)(2,1)} %param.7) | copy-start | bytes 98308
  2.3 76.1 %all-to-all-start.1 = ((bf16[16,8,1024]{2,0,1:T(8,128)(2,1)}), bf16[16,8,1024]{2,0,1:T(8,128)(2,1)S(1)}, u32[]{:S(2)}, u32[]{:S(2)}) async-start(bf16[16,8,1024]{2,0,1:T(8,128)(2,1)} %bitcast.13), calls=%async_computation.1 | async-start | bytes 524288 | tf_op jit(solution)/shard_map/all_to_all | solution.py:70
  11.6 47.2 %copy-start.1 = (s32[1,4096]{1,0:T(1,128)}, s32[1,4096]{1,0:T(1,128)S(1)}, u32[]{:S(2)}) copy-start(s32[1,4096]{1,0:T(1,128)S(1)} %add.72.cpos_ref) | copy-start | bytes 49156
  78.5 6.1 %copy-start = (bf16[16,8,1024]{2,0,1:T(8,128)(2,1)}, bf16[16,8,1024]{2,0,1:T(8,128)(2,1)S(1)}, u32[]{:S(2)}) copy-start(bf16[16,8,1024]{2,0,1:T(8,128)(2,1)S(1)} %all-to-all-done.1) | copy-start | bytes 786436
  78.5 52.5 %all-to-all-start = ((bf16[8,16,1024]{2,1,0:T(8,128)(2,1)}), bf16[8,16,1024]{2,1,0:T(8,128)(2,1)S(1)}, u32[]{:S(2)}, u32[]{:S(2)}) async-start(bf16[8,16,1024]{2,1,0:T(8,128)(2,1)} %bitcast.16), calls=%async_computation | async-start | bytes 524288 | tf_op jit(solution)/shard_map/all_to_all | solution.py:74

commit v8 on v7

--- a/solution.py
+++ b/solution.py
@@ -13,7 +13,7 @@
 MESH = pl.DeviceIdType.MESH
 
 
-def greet_all(n, me):
+def greet_all(n, me, t=1, mt=None):
     barrier = pltpu.get_barrier_semaphore()
 
     def greet(i, c):
@@ -21,13 +21,61 @@
         pl.semaphore_signal(barrier, inc=1, device_id={"ctx": peer}, device_id_type=MESH)
         return c
 
+    def greet_tp(i, c):
+        peer = lax.rem(mt + i, t)
+        pl.semaphore_signal(barrier, inc=1, device_id={"tp": peer}, device_id_type=MESH)
+        return c
+
     lax.fori_loop(1, n, greet, 0)
-    pl.semaphore_wait(barrier, n - 1)
-
-
-def gather_kernel(n, src_ref, out_ref, send_sem, recv_sem):
+    if t > 1:
+        lax.fori_loop(1, t, greet_tp, 0)
+    pl.semaphore_wait(barrier, n - 1 + t - 1)
+
+
+def tp_exchange(t, mt, src_of, dst_of, send_sem, recv_sem):
+    def copy_to(peer):
+        return pltpu.make_async_remote_copy(
+            src_of(peer), dst_of(mt), send_sem.at[peer], recv_sem.at[mt],
+            device_id={"tp": peer}, device_id_type=MESH)
+
+    def copy_from(src):
+        return pltpu.make_async_remote_copy(
+            src_of(mt), dst_of(src), send_sem.at[src], recv_sem.at[src],
+            device_id={"tp": src}, device_id_type=MESH)
+
+    def start():
+        def send(i, c):
+            copy_to(lax.rem(mt + i, t)).start()
+            return c
+
+        lax.fori_loop(1, t, send, 0)
+
+    def finish():
+        def wait(i, c):
+            copy_to(lax.rem(mt + i, t)).wait_send()
+            copy_from(lax.rem(mt + t - i, t)).wait_recv()
+            return c
+
+        lax.fori_loop(1, t, wait, 0)
+
+    return start, finish
+
+
+def gather_kernel(n, t, src_ref, og_ref, out_ref, grad_ref, send_sem, recv_sem, gsend_sem, grecv_sem):
     me = lax.axis_index("ctx")
-    greet_all(n, me)
+    mt = lax.axis_index("tp")
+    greet_all(n, me, t, mt)
+    rows = og_ref.shape[0]
+    cols = grad_ref.shape[1]
+
+    def grad_src(p):
+        return og_ref.at[:, pl.ds(pl.multiple_of(p * cols, cols), cols)]
+
+    def grad_dst(p):
+        return grad_ref.at[pl.ds(pl.multiple_of(p * rows, rows), rows), :]
+
+    grad_start, grad_finish = tp_exchange(t, mt, grad_src, grad_dst, gsend_sem, grecv_sem)
+    grad_start()
 
     def copy_to(peer):
         return pltpu.make_async_remote_copy(
@@ -45,6 +93,8 @@
 
     lax.fori_loop(1, n, send, 0)
     out_ref[me] = src_ref[...]
+    grad_ref[pl.ds(pl.multiple_of(mt * rows, rows), rows), :] = og_ref[
+        :, pl.ds(pl.multiple_of(mt * cols, cols), cols)]
 
     def wait(i, c):
         copy_to(lax.rem(me + i, n)).wait_send()
@@ -52,26 +102,24 @@
         return c
 
     lax.fori_loop(1, n, wait, 0)
-
-
-def ctx_gather(block, n):
+    grad_finish()
+
+
+def ctx_gather(block, out_grad, n, t):
     rows, width = block.shape
+    grad_shape = (out_grad.shape[0] * t, out_grad.shape[1] // t)
     return pl.pallas_call(
-        functools.partial(gather_kernel, n),
-        out_shape=jax.ShapeDtypeStruct((n, rows, width), block.dtype),
-        in_specs=[pl.BlockSpec(memory_space=pltpu.VMEM)],
-        out_specs=pl.BlockSpec(memory_space=pltpu.VMEM),
-        scratch_shapes=[pltpu.SemaphoreType.DMA((n,)), pltpu.SemaphoreType.DMA((n,))],
+        functools.partial(gather_kernel, n, t),
+        out_shape=(
+            jax.ShapeDtypeStruct((n, rows, width), block.dtype),
+            jax.ShapeDtypeStruct(grad_shape, out_grad.dtype),
+        ),
+        in_specs=[pl.BlockSpec(memory_space=pltpu.VMEM)] * 2,
+        out_specs=(pl.BlockSpec(memory_space=pltpu.VMEM),) * 2,
+        scratch_shapes=[pltpu.SemaphoreType.DMA((n,)), pltpu.SemaphoreType.DMA((n,)),
+                        pltpu.SemaphoreType.DMA((t,)), pltpu.SemaphoreType.DMA((t,))],
         compiler_params=pltpu.CompilerParams(collective_id=0, has_side_effects=True),
-    )(block)
-
-
-def fetch_grad(out_grad):
-    return lax.all_to_all(out_grad, "tp", split_axis=1, concat_axis=0, tiled=True)
-
-
-def spread_output(attn_flat):
-    return lax.all_to_all(attn_flat, "tp", split_axis=0, concat_axis=1, tiled=True)
+    )(block, out_grad)
 
 
 KEY_BLOCK = 512
@@ -147,31 +195,31 @@
     )(q, kv, rpos, rlab, cpos, clab)
 
 
-def fwd_step(queries, keys, values, visible, m_sc, l_sc, acc_sc):
-    scale = 1.0 / math.sqrt(HEAD_DIM)
-    scores = lax.dot_general(queries, keys, NT_DIMS, preferred_element_type=jnp.float32) * scale
-    scores = jnp.where(visible, scores, -jnp.inf)
-    running = m_sc[...]
-    new_max = jnp.maximum(running, jnp.max(scores, axis=-1, keepdims=True))
-    shift = jnp.where(new_max == -jnp.inf, 0.0, new_max)
-    factor = jnp.exp(running - shift)
-    weights = jnp.where(visible, jnp.exp(scores - shift), 0.0)
-    l_sc[...] = l_sc[...] * factor + jnp.sum(weights, axis=-1, keepdims=True)
-    acc_sc[...] = acc_sc[...] * factor + jnp.dot(
-        weights.astype(jnp.bfloat16), values, preferred_element_type=jnp.float32)
-    m_sc[...] = new_max
-
-
 def column_visible(cpos_ref, clab_ref, block, rpos, rlab):
     cpos = cpos_ref[pl.ds(block, 1), :]
     clab = clab_ref[pl.ds(block, 1), :]
     return (cpos <= rpos) & ((clab == 0) | (clab == rlab))
 
 
-def bwd_scatter_kernel(n, q_ref, g_ref, o_ref, kv_ref, rpos_ref, rlab_ref, cpos_ref, clab_ref,
-                       m_ref, l_ref, dq_ref, red_ref, terms_sc, held, dq_sc, send_sem, recv_sem):
+def bwd_scatter_kernel(n, t, q_ref, g_ref, o_ref, kv_ref, rpos_ref, rlab_ref, cpos_ref, clab_ref,
+                       m_ref, l_ref, dq_ref, red_ref, spread_ref, terms_sc, held, dq_sc, send_sem, recv_sem,
+                       osend_sem, orecv_sem):
     me = lax.axis_index("ctx")
-    greet_all(n, me)
+    mt = lax.axis_index("tp")
+    greet_all(n, me, t, mt)
+    rows = spread_ref.shape[0]
+    cols = o_ref.shape[1]
+
+    def out_src(p):
+        return o_ref.at[pl.ds(pl.multiple_of(p * rows, rows), rows), :]
+
+    def out_dst(p):
+        return spread_ref.at[:, pl.ds(pl.multiple_of(p * cols, cols), cols)]
+
+    out_start, out_finish = tp_exchange(t, mt, out_src, out_dst, osend_sem, orecv_sem)
+    out_start()
+    spread_ref[:, pl.ds(pl.multiple_of(mt * cols, cols), cols)] = o_ref[
+        pl.ds(pl.multiple_of(mt * rows, rows), rows), :]
     scale = 1.0 / math.sqrt(HEAD_DIM)
     queries = stack_heads(q_ref)
     grads = stack_heads(g_ref)
@@ -237,25 +285,29 @@
         return c
 
     lax.fori_loop(1, n, drain, 0)
-
-
-def bwd_scatter(q, g, o, kv, rpos, rlab, cpos, clab, m, l, n):
+    out_finish()
+
+
+def bwd_scatter(q, g, o, kv, rpos, rlab, cpos, clab, m, l, n, t):
     _, rows, width = kv.shape
     stacked = rpos.shape[0]
     return pl.pallas_call(
-        functools.partial(bwd_scatter_kernel, n),
+        functools.partial(bwd_scatter_kernel, n, t),
         out_shape=(
             jax.ShapeDtypeStruct(q.shape, jnp.bfloat16),
             jax.ShapeDtypeStruct((rows, width), jnp.float32),
+            jax.ShapeDtypeStruct((o.shape[0] // t, o.shape[1] * t), o.dtype),
         ),
         in_specs=vmem_specs(10),
-        out_specs=tuple(vmem_specs(2)),
+        out_specs=tuple(vmem_specs(3)),
         scratch_shapes=[
             pltpu.VMEM(kv.shape, jnp.bfloat16),
             pltpu.VMEM(kv.shape, jnp.bfloat16),
             pltpu.VMEM((stacked, HEAD_DIM), jnp.float32),
             pltpu.SemaphoreType.DMA((n,)),
             pltpu.SemaphoreType.DMA((n,)),
+            pltpu.SemaphoreType.DMA((t,)),
+            pltpu.SemaphoreType.DMA((t,)),
         ],
         compiler_params=pltpu.CompilerParams(collective_id=1, has_side_effects=True),
     )(q, g, o, kv, rpos, rlab, cpos, clab, m, l)
@@ -279,16 +331,16 @@
     cpos = positions.reshape(ctx_size, local_rows)
     clab = labels.reshape(ctx_size, local_rows)
     kv_local = jnp.concatenate([key_rows, value_rows], axis=1)
-    kv_all = ctx_gather(kv_local, ctx_size)
+    tp_size = lax.axis_size("tp")
+    kv_all, grad_rows = ctx_gather(kv_local, out_grad, ctx_size, tp_size)
     attn_local, row_max, total = attention_fwd(
         query_rows, kv_all.reshape(total_rows, kv_all.shape[2]), rpos, rlab,
         positions[None, :], labels[None, :])
-    grad_rows = fetch_grad(out_grad)
-    query_grad, reduced = bwd_scatter(
-        query_rows, grad_rows, attn_local, kv_all, rpos, rlab, cpos, clab, row_max, total, ctx_size)
+    query_grad, reduced, attn_spread = bwd_scatter(
+        query_rows, grad_rows, attn_local, kv_all, rpos, rlab, cpos, clab, row_max, total,
+        ctx_size, tp_size)
     key_grad = reduced[:, :HEAD_DIM].astype(jnp.bfloat16)
     value_grad = reduced[:, HEAD_DIM:].astype(jnp.bfloat16)
-    attn_spread = spread_output(attn_local)
     return (attn_spread, query_grad, key_grad, value_grad)
 
 

time: 137 us -> 131 us (0.956)
  starting transfers between devices: 12.4 us -> 0 us
  Pallas kernels: 106 us -> 113 us
    all_to_all x2 -> x0, starting transfers between devices: 12.4 us -> none  [the longest x1 8.47 us: fetch_grad(): lax.all_to_all(out_grad, 'tp', split_axis=1, concat_axis=0, tiled=True)]
    pallas_call x2, Pallas kernels: 86.3 us -> 93 us  [the longest x1 47.6 us: bwd_scatter(): pl.pallas_call(functools.partial(bwd_scatter_kernel, n, t), out_shape=(ja...]
    all_to_all x2 -> x0, local copies, waits for them, and re-layouts: 2.4 us -> none  [the longest x1 1.68 us: fetch_grad(): lax.all_to_all(out_grad, 'tp', split_axis=1, concat_axis=0, tiled=True)]
    unnamed x9 -> x4, local copies, waits for them, and re-layouts: 1.69 us -> 3.34 us
  transfers between devices with their start and end apart: 2 -> 0, of which waited for: 0 -> 0; matrix products, arithmetic and copies ran while one was open for 8% -> 0% of each run, Pallas kernels for 79% -> 0%
where the time goes in v8:
time: 131 us; the launch traced here: 130 us
  Pallas kernels  113 us (86%)
  other arithmetic  9.64 us (7%)
  local copies, waits for them, and re-layouts  6.56 us (5%)
    pallas_call x1, Pallas kernels, bwd_scatter(): pl.pallas_call(functools.partial(bwd_scatter_kernel, n, t), out_shape=(ja...  47.6 us
    pallas_call x1, Pallas kernels, ctx_gather(): pl.pallas_call(functools.partial(gather_kernel, n, t), out_shape=(jax.Sha...  45.3 us
    pallas_call x1, Pallas kernels, attention_fwd(): pl.pallas_call(fwd_kernel, out_shape=(jax.ShapeDtypeStruct(q.shape, jnp.b...  19.7 us
    add x3, other arithmetic, on_device(): (positions >= prompt_end).astype(jnp.int32)  5.16 us
    unnamed x4, local copies, waits for them, and re-layouts  3.34 us

profile of v8, /device:TPU:16, one launch (start us, length us, event | category | flops | bytes accessed | tf_op | source)
XLA Modules:
  0.0 129.6 jit_solution(10782064312807994518)
XLA Ops:
  0.6 0.7 broadcast_multiply_fusion
  1.3 0.1 add.78
  1.4 1.4 %convert_reduce_fusion.1 = (s32[]{:T(128)}, s32[]{:T(128)}) fusion(s32[4096]{0:T(1024)} %param.10), kind=kLoop, calls=%fused_computation.7 | loop fusion | flops 24574 | bytes 16392 | tf_op jit(solution)/shard_map/reduce_sum | solution.py:324
  2.8 0.1 add.74
  2.9 0.1 add.75
  3.0 0.1 add.76
  3.1 1.9 %convert_add_fusion = (s32[32,128]{1,0:T(8,128)}, s32[32,128]{1,0:T(8,128)}) fusion(s32[]{:T(128)} %get-tuple-element.21, s32[]{:T(128)} %get-tuple-element.20, s32[32,128]{1,0:T(8,128)S(1)} %add.76, s32[128]{0:T(128)S(1)} %add.78), kind=kLoop, calls=%fused_computation.5 | loop fusion | flops 24576 | bytes 49672 | tf_op jit(solution)/shard_map/add | solution.py:326
  5.0 0.1 iota_add_fusion
  5.1 0.1 add.72.cpos_ref
  5.2 0.0 copy-start
  5.2 0.1 add.69
  5.2 1.4 %fusion.1 = (s32[128]{0:T(128)S(1)}, s32[128]{0:T(128)S(1)}) fusion(s32[]{:T(128)} %get-tuple-element.21, s32[]{:T(128)} %get-tuple-element.20, s32[4096]{0:T(1024)S(1)} %add.69, s32[]{:T(128)S(6)} %select_n.4), kind=kLoop, calls=%fused_computation.11 | loop fusion | flops 640 | bytes 1548 | tf_op jit(solution)/shard_map/add | solution.py:326
  6.6 1.9 %fusion.clab_ref = s32[1,4096]{1,0:T(1,128)} fusion(s32[1,4096]{1,0:T(1,128)S(1)} %add.72.cpos_ref, s32[]{:T(128)} %get-tuple-element.21, s32[]{:T(128)} %get-tuple-element.20), kind=kLoop, calls=%fused_computation.4 | loop fusion | flops 20480 | bytes 32776 | tf_op jit(solution)/shard_map/add | solution.py:326
  8.5 1.4 %pad_maximum_fusion.src_ref = bf16[128,256]{1,0:T(8,128)(2,1)} fusion(bf16[128,128]{1,0:T(8,128)(2,1)} %param.8, bf16[128,128]{1,0:T(8,128)(2,1)} %param.7), kind=kLoop, calls=%fused_computation | loop fusion | flops 131072 | bytes 131072 | tf_op jit(solution)/shard_map/concatenate | solution.py:333
  9.9 1.0 copy.10.rpos_ref
  11.0 1.0 copy.11.rlab_ref
  12.0 45.3 %shard_map.93 = (bf16[32,128,256]{2,1,0:T(8,128)(2,1)}, bf16[128,1024]{1,0:T(8,128)(2,1)}) custom-call(bf16[128,256]{1,0:T(8,128)(2,1)} %pad_maximum_fusion.src_ref, bf16[16,8192]{1,0:T(8,128)(2,1)} %og_ref.1), custom_call_target="tpu_custom_call" | custom-call | tf_op jit(solution)/shard_map/pallas_call | solution.py:111
  57.3 0.0 copy-done
  57.3 19.7 %shard_map.94 = (bf16[128,1024]{1,0:T(8,128)(2,1)}, f32[1024,1]{1,0:T(8,128)}, f32[1024,1]{1,0:T(8,128)}) custom-call(bf16[128,1024]{1,0:T(8,128)(2,1)} %q_ref.3, bf16[4096,256]{1,0:T(8,128)(2,1)} %bitcast.3, s32[1024,1]{1,0:T(8,128)} %copy.10.rpos_ref, s32[1024,1]{1,0:T(8,128)} %copy.11.rlab_ref, s32[1,4096]{1,0:T(1,128)} %copy-done, s32[1,4096]{1,0:T(1,128)} %fusion.clab_ref), custom_call_target="tpu_custom_call" | custom-call | tf_op jit(solution)/shard_map/pallas_call | solution.py:185
  77.0 47.6 %shard_map.95 = (bf16[128,1024]{1,0:T(8,128)(2,1)}, f32[128,256]{1,0:T(8,128)}, bf16[16,8192]{1,0:T(8,128)(2,1)}) custom-call(bf16[128,1024]{1,0:T(8,128)(2,1)} %q_ref.3, bf16[128,1024]{1,0:T(8,128)(2,1)} %get-tuple-element.12.g_ref, bf16[128,1024]{1,0:T(8,128)(2,1)} %get-tuple-element.14.o_ref, bf16[32,128,256]{2,1,0:T(8,128)(2,1)} %get-tuple-element.13.kv_ref, ...), custom_call_target="tpu_custom_call" | custom-call | tf_op jit(solution)/shard_map/pallas_call | solution.py:294
  124.7 0.9 convert.4
  125.6 0.6 fusion.2
  126.2 1.7 %copy.16 = bf16[16,8192]{1,0:T(8,128)(2,1)} copy(bf16[16,8192]{1,0:T(8,128)(2,1)} %get-tuple-element.32) | data formatting | bytes 524288
  127.9 1.7 %copy.17 = bf16[128,1024]{1,0:T(8,128)(2,1)} copy(bf16[128,1024]{1,0:T(8,128)(2,1)} %get-tuple-element.33) | data formatting | bytes 524288
  (3 shorter events, 0.0 us)
Async XLA Ops:
  5.2 52.2 %copy-start = (s32[1,4096]{1,0:T(1,128)}, s32[1,4096]{1,0:T(1,128)S(1)}, u32[]{:S(2)}) copy-start(s32[1,4096]{1,0:T(1,128)S(1)} %add.72.cpos_ref) | copy-start | bytes 49156

commit v9 on v8

--- a/solution.py
+++ b/solution.py
@@ -61,7 +61,43 @@
     return start, finish
 
 
-def gather_kernel(n, t, src_ref, og_ref, out_ref, grad_ref, send_sem, recv_sem, gsend_sem, grecv_sem):
+def mask_vectors(me, heads, so_ref, seg_ref, rpos_ref, rlab_ref, cpos_ref, clab_ref, cgrid_ref, lgrid_ref):
+    seg = seg_ref[...]
+    prompt_end = jnp.sum(jnp.sum((seg == 0).astype(jnp.int32), axis=1, keepdims=True), axis=0, keepdims=True)
+    chosen_end = jnp.sum(jnp.sum((seg <= 1).astype(jnp.int32), axis=1, keepdims=True), axis=0, keepdims=True)
+
+    def label_of(pos):
+        return (pos >= prompt_end).astype(jnp.int32) + (pos >= chosen_end).astype(jnp.int32)
+
+    def position_of(rows):
+        block = lax.shift_right_logical(rows, 6)
+        start = jnp.zeros(rows.shape, jnp.int32)
+        for b in range(so_ref.shape[0]):
+            start = jnp.where(block == b, so_ref[b], start)
+        return start * SPAN + jnp.bitwise_and(rows, SPAN - 1)
+
+    lanes = lax.broadcasted_iota(jnp.int32, cpos_ref.shape, 1)
+    cpos = position_of(lanes)
+    cpos_ref[...] = cpos
+    clab_ref[...] = label_of(cpos)
+    grid = (lax.broadcasted_iota(jnp.int32, cgrid_ref.shape, 0) * cgrid_ref.shape[1]
+            + lax.broadcasted_iota(jnp.int32, cgrid_ref.shape, 1))
+    gpos = position_of(grid)
+    cgrid_ref[...] = gpos
+    lgrid_ref[...] = label_of(gpos)
+    local = rpos_ref.shape[0] // heads
+    within = jnp.bitwise_and(lax.broadcasted_iota(jnp.int32, rpos_ref.shape, 0), local - 1)
+    first = so_ref[me * (local // SPAN)]
+    second = so_ref[me * (local // SPAN) + 1]
+    start = jnp.where(within < SPAN, first, second)
+    rpos = start * SPAN + jnp.bitwise_and(within, SPAN - 1)
+    rpos_ref[...] = rpos
+    rlab_ref[...] = label_of(rpos)
+
+
+def gather_kernel(n, t, src_ref, og_ref, so_ref, seg_ref, out_ref, grad_ref,
+                  rpos_ref, rlab_ref, cpos_ref, clab_ref, cgrid_ref, lgrid_ref,
+                  send_sem, recv_sem, gsend_sem, grecv_sem):
     me = lax.axis_index("ctx")
     mt = lax.axis_index("tp")
     greet_all(n, me, t, mt)
@@ -93,6 +129,8 @@
 
     lax.fori_loop(1, n, send, 0)
     out_ref[me] = src_ref[...]
+    mask_vectors(me, grad_ref.shape[1] // HEAD_DIM, so_ref, seg_ref,
+                 rpos_ref, rlab_ref, cpos_ref, clab_ref, cgrid_ref, lgrid_ref)
     grad_ref[pl.ds(pl.multiple_of(mt * rows, rows), rows), :] = og_ref[
         :, pl.ds(pl.multiple_of(mt * cols, cols), cols)]
 
@@ -105,21 +143,28 @@
     grad_finish()
 
 
-def ctx_gather(block, out_grad, n, t):
+def ctx_gather(block, out_grad, span_order, segment_ids, n, t):
     rows, width = block.shape
     grad_shape = (out_grad.shape[0] * t, out_grad.shape[1] // t)
+    stacked = rows * (grad_shape[1] // HEAD_DIM)
+    seg = segment_ids.reshape(n, segment_ids.shape[0] // n)
+    column = jax.ShapeDtypeStruct((1, n * rows), jnp.int32)
+    row = jax.ShapeDtypeStruct((stacked, 1), jnp.int32)
+    grid = jax.ShapeDtypeStruct((n, rows), jnp.int32)
     return pl.pallas_call(
         functools.partial(gather_kernel, n, t),
         out_shape=(
             jax.ShapeDtypeStruct((n, rows, width), block.dtype),
             jax.ShapeDtypeStruct(grad_shape, out_grad.dtype),
+            row, row, column, column, grid, grid,
         ),
-        in_specs=[pl.BlockSpec(memory_space=pltpu.VMEM)] * 2,
-        out_specs=(pl.BlockSpec(memory_space=pltpu.VMEM),) * 2,
+        in_specs=[pl.BlockSpec(memory_space=pltpu.VMEM)] * 2
+        + [pl.BlockSpec(memory_space=pltpu.SMEM), pl.BlockSpec(memory_space=pltpu.VMEM)],
+        out_specs=(pl.BlockSpec(memory_space=pltpu.VMEM),) * 8,
         scratch_shapes=[pltpu.SemaphoreType.DMA((n,)), pltpu.SemaphoreType.DMA((n,)),
                         pltpu.SemaphoreType.DMA((t,)), pltpu.SemaphoreType.DMA((t,))],
         compiler_params=pltpu.CompilerParams(collective_id=0, has_side_effects=True),
-    )(block, out_grad)
+    )(block, out_grad, span_order, seg)
 
 
 KEY_BLOCK = 512
@@ -319,23 +364,12 @@
     local_rows = query_rows.shape[0]
     heads_here = query_rows.shape[1] // HEAD_DIM
     total_rows = local_rows * ctx_size
-    offsets = jnp.arange(SPAN, dtype=jnp.int32)
-    positions = (SPAN * span_order[:, None] + offsets[None, :]).reshape(total_rows)
-    prompt_end = jnp.sum((segment_ids == 0).astype(jnp.int32))
-    chosen_end = jnp.sum((segment_ids <= 1).astype(jnp.int32))
-    labels = (positions >= prompt_end).astype(jnp.int32) + (positions >= chosen_end).astype(jnp.int32)
-    own_pos = lax.dynamic_slice_in_dim(positions, ctx_index * local_rows, local_rows, 0)
-    own_label = lax.dynamic_slice_in_dim(labels, ctx_index * local_rows, local_rows, 0)
-    rpos = jnp.tile(own_pos, heads_here)[:, None]
-    rlab = jnp.tile(own_label, heads_here)[:, None]
-    cpos = positions.reshape(ctx_size, local_rows)
-    clab = labels.reshape(ctx_size, local_rows)
     kv_local = jnp.concatenate([key_rows, value_rows], axis=1)
     tp_size = lax.axis_size("tp")
-    kv_all, grad_rows = ctx_gather(kv_local, out_grad, ctx_size, tp_size)
+    kv_all, grad_rows, rpos, rlab, cpos_row, clab_row, cpos, clab = ctx_gather(
+        kv_local, out_grad, span_order, segment_ids, ctx_size, tp_size)
     attn_local, row_max, total = attention_fwd(
-        query_rows, kv_all.reshape(total_rows, kv_all.shape[2]), rpos, rlab,
-        positions[None, :], labels[None, :])
+        query_rows, kv_all.reshape(total_rows, kv_all.shape[2]), rpos, rlab, cpos_row, clab_row)
     query_grad, reduced, attn_spread = bwd_scatter(
         query_rows, grad_rows, attn_local, kv_all, rpos, rlab, cpos, clab, row_max, total,
         ctx_size, tp_size)

time: 131 us -> 120 us (0.916)
  other arithmetic: 9.64 us -> 2.33 us
  local copies, waits for them, and re-layouts: 6.56 us -> 3.97 us
    add x4 -> x0, other arithmetic: 5.23 us -> none  [the longest x3 5.16 us: on_device(): (positions >= prompt_end).astype(jnp.int32)]
    another operation x4 -> x0, local copies, waits for them, and re-layouts: 2.06 us -> none  [the longest x2 1.04 us: on_device(): rlab = jnp.tile(own_label, heads_here)[:, None]]
    reduce_sum x1 -> x0, other arithmetic: 1.42 us -> none  [on_device(): prompt_end = jnp.sum((segment_ids == 0).astype(jnp.int32))]
    unnamed x4 -> x2, local copies, waits for them, and re-layouts: 3.34 us -> 3.34 us
where the time goes in v9:
time: 120 us; the launch traced here: 119 us
  Pallas kernels  112 us (93%)
  local copies, waits for them, and re-layouts  3.97 us (3%)
  other arithmetic  2.33 us (2%)
    pallas_call x1, Pallas kernels, bwd_scatter(): pl.pallas_call(functools.partial(bwd_scatter_kernel, n, t), out_shape=(ja...  46.5 us
    pallas_call x1, Pallas kernels, ctx_gather(): pl.pallas_call(functools.partial(gather_kernel, n, t), out_shape=(jax.Sha...  46 us
    pallas_call x1, Pallas kernels, attention_fwd(): pl.pallas_call(fwd_kernel, out_shape=(jax.ShapeDtypeStruct(q.shape, jnp.b...  19.7 us
    unnamed x2, local copies, waits for them, and re-layouts  3.34 us

profile of v9, /device:TPU:16, one launch (start us, length us, event | category | flops | bytes accessed | tf_op | source)
XLA Modules:
  0.0 119.1 jit_solution(10699350760682884776)
XLA Ops:
  0.6 1.4 %pad_maximum_fusion.src_ref = bf16[128,256]{1,0:T(8,128)(2,1)} fusion(bf16[128,128]{1,0:T(8,128)(2,1)} %param.8, bf16[128,128]{1,0:T(8,128)(2,1)} %param.7), kind=kLoop, calls=%fused_computation | loop fusion | flops 131072 | bytes 131072 | tf_op jit(solution)/shard_map/concatenate | solution.py:367
  2.0 46.0 %shard_map.93 = (bf16[32,128,256]{2,1,0:T(8,128)(2,1)}, bf16[128,1024]{1,0:T(8,128)(2,1)}, s32[1024,1]{1,0:T(8,128)}, s32[1024,1]{1,0:T(8,128)}, s32[1,4096]{1,0...) custom-call(bf16[128,256]{1,0:T(8,128)(2,1)} %pad_maximum_fusion.src_ref, ...), custom_call_target="tpu_custom_call" | custom-call | tf_op jit(solution)/shard_map/pallas_call | solution.py:154
  48.1 19.7 %shard_map.94 = (bf16[128,1024]{1,0:T(8,128)(2,1)}, f32[1024,1]{1,0:T(8,128)}, f32[1024,1]{1,0:T(8,128)}) custom-call(bf16[128,1024]{1,0:T(8,128)(2,1)} %q_ref.3, bf16[4096,256]{1,0:T(8,128)(2,1)} %bitcast.2, s32[1024,1]{1,0:T(8,128)} %get-tuple-element.20.rpos_ref, s32[1024,1]{1,0:T(8,128)} %get-tuple-element.21.rlab_ref, ...), custom_call_target="tpu_custom_call" | custom-call | tf_op jit(solution)/shard_map/pallas_call | solution.py:230
  67.7 46.5 %shard_map.95 = (bf16[128,1024]{1,0:T(8,128)(2,1)}, f32[128,256]{1,0:T(8,128)}, bf16[16,8192]{1,0:T(8,128)(2,1)}) custom-call(bf16[128,1024]{1,0:T(8,128)(2,1)} %q_ref.3, bf16[128,1024]{1,0:T(8,128)(2,1)} %get-tuple-element.18.g_ref, bf16[128,1024]{1,0:T(8,128)(2,1)} %get-tuple-element.24.o_ref, bf16[32,128,256]{2,1,0:T(8,128)(2,1)} %get-tuple-element.19.kv_ref, ...), custom_call_target="tpu_custom_call" | custom-call | tf_op jit(solution)/shard_map/pallas_call | solution.py:339
  114.2 0.9 convert.4
  115.1 0.6 fusion
  115.7 1.7 %copy.12 = bf16[16,8192]{1,0:T(8,128)(2,1)} copy(bf16[16,8192]{1,0:T(8,128)(2,1)} %get-tuple-element.38) | data formatting | bytes 524288
  117.4 1.7 %copy.13 = bf16[128,1024]{1,0:T(8,128)(2,1)} copy(bf16[128,1024]{1,0:T(8,128)(2,1)} %get-tuple-element.39) | data formatting | bytes 524288

commit v10 on v9

--- a/solution.py
+++ b/solution.py
@@ -11,6 +11,25 @@
 HEAD_DIM = 128
 SPAN = 64
 MESH = pl.DeviceIdType.MESH
+
+
+CTX_SHAPE = (4, 4, 2)
+
+
+def ctx_peer(me, i, n, sign):
+    if n != math.prod(CTX_SHAPE):
+        return lax.rem(me + sign * i + n, n)
+    sx, sy, sz = CTX_SHAPE
+    dz = lax.rem(i, sz)
+    dx = lax.rem(i // sz, sx)
+    dy = i // (sz * sx)
+    x = me // (sy * sz)
+    y = lax.rem(me // sz, sy)
+    z = lax.rem(me, sz)
+    x = lax.rem(x + sign * dx + sx, sx)
+    y = lax.rem(y + sign * dy + sy, sy)
+    z = lax.rem(z + sign * dz + sz, sz)
+    return (x * sy + y) * sz + z
 
 
 def greet_all(n, me, t=1, mt=None):
@@ -124,7 +143,7 @@
             device_id={"ctx": src}, device_id_type=MESH)
 
     def send(i, c):
-        copy_to(lax.rem(me + i, n)).start()
+        copy_to(ctx_peer(me, i, n, 1)).start()
         return c
 
     lax.fori_loop(1, n, send, 0)
@@ -135,8 +154,8 @@
         :, pl.ds(pl.multiple_of(mt * cols, cols), cols)]
 
     def wait(i, c):
-        copy_to(lax.rem(me + i, n)).wait_send()
-        copy_from(lax.rem(me + n - i, n)).wait_recv()
+        copy_to(ctx_peer(me, i, n, 1)).wait_send()
+        copy_from(ctx_peer(me, i, n, -1)).wait_recv()
         return c
 
     lax.fori_loop(1, n, wait, 0)
@@ -304,21 +323,21 @@
     red_ref[...] = block_terms(me)
 
     def step(i, c):
-        peer = lax.rem(me + i, n)
+        peer = ctx_peer(me, i, n, 1)
         terms_sc[peer] = block_terms(peer).astype(terms_sc.dtype)
 
         @pl.when(i >= 2)
         def _():
-            copy_to(lax.rem(me + i - 1, n)).start()
+            copy_to(ctx_peer(me, i - 1, n, 1)).start()
 
         return c
 
     lax.fori_loop(1, n, step, 0)
-    copy_to(lax.rem(me + n - 1, n)).start()
+    copy_to(ctx_peer(me, n - 1, n, 1)).start()
     unstack_heads(dq_ref, (dq_sc[...] * scale).astype(dq_ref.dtype))
 
     def arrive(i, c):
-        src = lax.rem(me + n - i, n)
+        src = ctx_peer(me, i, n, -1)
         copy_from(src).wait_recv()
         red_ref[...] += held[src].astype(jnp.float32)
         return c
@@ -326,7 +345,7 @@
     lax.fori_loop(1, n, arrive, 0)
 
     def drain(i, c):
-        copy_to(lax.rem(me + i, n)).wait_send()
+        copy_to(ctx_peer(me, i, n, 1)).wait_send()
         return c
 
     lax.fori_loop(1, n, drain, 0)

time: 120 us -> 120 us (level)
    pallas_call x1, Pallas kernels: 46.5 us -> 48.6 us  [bwd_scatter(): pl.pallas_call(functools.partial(bwd_scatter_kernel, n, t), out_shape=(ja...]
    pallas_call x1, Pallas kernels: 46 us -> 44.5 us  [ctx_gather(): pl.pallas_call(functools.partial(gather_kernel, n, t), out_shape=(jax.Sha...]
where the time goes in v10:
time: 120 us
  Pallas kernels  113 us (94%)
  local copies, waits for them, and re-layouts  3.97 us (3%)
  other arithmetic  2.33 us (2%)
    pallas_call x1, Pallas kernels, bwd_scatter(): pl.pallas_call(functools.partial(bwd_scatter_kernel, n, t), out_shape=(ja...  48.6 us
    pallas_call x1, Pallas kernels, ctx_gather(): pl.pallas_call(functools.partial(gather_kernel, n, t), out_shape=(jax.Sha...  44.5 us
    pallas_call x1, Pallas kernels, attention_fwd(): pl.pallas_call(fwd_kernel, out_shape=(jax.ShapeDtypeStruct(q.shape, jnp.b...  19.7 us
    unnamed x2, local copies, waits for them, and re-layouts  3.34 us

profile of v10, /device:TPU:16, one launch (start us, length us, event | category | flops | bytes accessed | tf_op | source)
XLA Modules:
  0.0 119.7 jit_solution(10271861566454243262)
XLA Ops:
  0.6 1.4 %pad_maximum_fusion.src_ref = bf16[128,256]{1,0:T(8,128)(2,1)} fusion(bf16[128,128]{1,0:T(8,128)(2,1)} %param.8, bf16[128,128]{1,0:T(8,128)(2,1)} %param.7), kind=kLoop, calls=%fused_computation | loop fusion | flops 131072 | bytes 131072 | tf_op jit(solution)/shard_map/concatenate | solution.py:386
  2.0 44.5 %shard_map.93 = (bf16[32,128,256]{2,1,0:T(8,128)(2,1)}, bf16[128,1024]{1,0:T(8,128)(2,1)}, s32[1024,1]{1,0:T(8,128)}, s32[1024,1]{1,0:T(8,128)}, s32[1,4096]{1,0...) custom-call(bf16[128,256]{1,0:T(8,128)(2,1)} %pad_maximum_fusion.src_ref, ...), custom_call_target="tpu_custom_call" | custom-call | tf_op jit(solution)/shard_map/pallas_call | solution.py:173
  46.5 19.7 %shard_map.94 = (bf16[128,1024]{1,0:T(8,128)(2,1)}, f32[1024,1]{1,0:T(8,128)}, f32[1024,1]{1,0:T(8,128)}) custom-call(bf16[128,1024]{1,0:T(8,128)(2,1)} %q_ref.3, bf16[4096,256]{1,0:T(8,128)(2,1)} %bitcast.2, s32[1024,1]{1,0:T(8,128)} %get-tuple-element.20.rpos_ref, s32[1024,1]{1,0:T(8,128)} %get-tuple-element.21.rlab_ref, ...), custom_call_target="tpu_custom_call" | custom-call | tf_op jit(solution)/shard_map/pallas_call | solution.py:249
  66.2 48.6 %shard_map.95 = (bf16[128,1024]{1,0:T(8,128)(2,1)}, f32[128,256]{1,0:T(8,128)}, bf16[16,8192]{1,0:T(8,128)(2,1)}) custom-call(bf16[128,1024]{1,0:T(8,128)(2,1)} %q_ref.3, bf16[128,1024]{1,0:T(8,128)(2,1)} %get-tuple-element.18.g_ref, bf16[128,1024]{1,0:T(8,128)(2,1)} %get-tuple-element.24.o_ref, bf16[32,128,256]{2,1,0:T(8,128)(2,1)} %get-tuple-element.19.kv_ref, ...), custom_call_target="tpu_custom_call" | custom-call | tf_op jit(solution)/shard_map/pallas_call | solution.py:358
  114.8 0.9 convert.4
  115.7 0.6 fusion
  116.4 1.7 %copy.12 = bf16[16,8192]{1,0:T(8,128)(2,1)} copy(bf16[16,8192]{1,0:T(8,128)(2,1)} %get-tuple-element.38) | data formatting | bytes 524288
  118.0 1.7 %copy.13 = bf16[128,1024]{1,0:T(8,128)(2,1)} copy(bf16[128,1024]{1,0:T(8,128)(2,1)} %get-tuple-element.39) | data formatting | bytes 524288

commit v11 on v10

--- a/solution.py
+++ b/solution.py
@@ -186,7 +186,7 @@
     )(block, out_grad, span_order, seg)
 
 
-KEY_BLOCK = 512
+KEY_BLOCK = 1024
 NT_DIMS = (((1,), (1,)), ((), ()))
 TN_DIMS = (((0,), (0,)), ((), ()))
 
@@ -203,11 +203,12 @@
 
 
 def key_block(kv_ref, cpos_ref, clab_ref, rpos, rlab, kb):
-    start = pl.multiple_of(kb * KEY_BLOCK, KEY_BLOCK)
-    keys = kv_ref[pl.ds(start, KEY_BLOCK), :HEAD_DIM]
-    values = kv_ref[pl.ds(start, KEY_BLOCK), HEAD_DIM:]
-    cpos = cpos_ref[:, pl.ds(start, KEY_BLOCK)]
-    clab = clab_ref[:, pl.ds(start, KEY_BLOCK)]
+    size = min(KEY_BLOCK, kv_ref.shape[0])
+    start = pl.multiple_of(kb * size, size)
+    keys = kv_ref[pl.ds(start, size), :HEAD_DIM]
+    values = kv_ref[pl.ds(start, size), HEAD_DIM:]
+    cpos = cpos_ref[:, pl.ds(start, size)]
+    clab = clab_ref[:, pl.ds(start, size)]
     visible = (cpos <= rpos) & ((clab == 0) | (clab == rlab))
     return start, keys, values, visible
 
@@ -229,14 +230,14 @@
         new_max = jnp.maximum(running, jnp.max(scores, axis=-1, keepdims=True))
         shift = jnp.where(new_max == -jnp.inf, 0.0, new_max)
         factor = jnp.exp(running - shift)
-        weights = jnp.where(visible, jnp.exp(scores - shift), 0.0)
+        weights = jnp.exp(scores - shift)
         l_ref[...] = l_ref[...] * factor + jnp.sum(weights, axis=-1, keepdims=True)
         acc_sc[...] = acc_sc[...] * factor + jnp.dot(
             weights.astype(jnp.bfloat16), values, preferred_element_type=jnp.float32)
         m_ref[...] = new_max
         return c
 
-    lax.fori_loop(0, kv_ref.shape[0] // KEY_BLOCK, body, 0)
+    lax.fori_loop(0, kv_ref.shape[0] // min(KEY_BLOCK, kv_ref.shape[0]), body, 0)
     unstack_heads(o_ref, (acc_sc[...] / l_ref[...]).astype(o_ref.dtype))
 
 

time: 120 us -> 120 us (level)
  no operation moved by 1% of the time
where the time goes in v11:
time: 120 us; the launch traced here: 119 us
  Pallas kernels  112 us (93%)
  local copies, waits for them, and re-layouts  3.97 us (3%)
  other arithmetic  2.33 us (2%)
    pallas_call x1, Pallas kernels, bwd_scatter(): pl.pallas_call(functools.partial(bwd_scatter_kernel, n, t), out_shape=(ja...  49 us
    pallas_call x1, Pallas kernels, ctx_gather(): pl.pallas_call(functools.partial(gather_kernel, n, t), out_shape=(jax.Sha...  44.5 us
    pallas_call x1, Pallas kernels, attention_fwd(): pl.pallas_call(fwd_kernel, out_shape=(jax.ShapeDtypeStruct(q.shape, jnp.b...  18.8 us
    unnamed x2, local copies, waits for them, and re-layouts  3.34 us

profile of v11, /device:TPU:16, one launch (start us, length us, event | category | flops | bytes accessed | tf_op | source)
XLA Modules:
  0.0 119.2 jit_solution(8971971598210788254)
XLA Ops:
  0.6 1.4 %pad_maximum_fusion.src_ref = bf16[128,256]{1,0:T(8,128)(2,1)} fusion(bf16[128,128]{1,0:T(8,128)(2,1)} %param.8, bf16[128,128]{1,0:T(8,128)(2,1)} %param.7), kind=kLoop, calls=%fused_computation | loop fusion | flops 131072 | bytes 131072 | tf_op jit(solution)/shard_map/concatenate | solution.py:387
  2.0 44.5 %shard_map.93 = (bf16[32,128,256]{2,1,0:T(8,128)(2,1)}, bf16[128,1024]{1,0:T(8,128)(2,1)}, s32[1024,1]{1,0:T(8,128)}, s32[1024,1]{1,0:T(8,128)}, s32[1,4096]{1,0...) custom-call(bf16[128,256]{1,0:T(8,128)(2,1)} %pad_maximum_fusion.src_ref, ...), custom_call_target="tpu_custom_call" | custom-call | tf_op jit(solution)/shard_map/pallas_call | solution.py:173
  46.5 18.8 %shard_map.94 = (bf16[128,1024]{1,0:T(8,128)(2,1)}, f32[1024,1]{1,0:T(8,128)}, f32[1024,1]{1,0:T(8,128)}) custom-call(bf16[128,1024]{1,0:T(8,128)(2,1)} %q_ref.3, bf16[4096,256]{1,0:T(8,128)(2,1)} %bitcast.2, s32[1024,1]{1,0:T(8,128)} %get-tuple-element.20.rpos_ref, s32[1024,1]{1,0:T(8,128)} %get-tuple-element.21.rlab_ref, ...), custom_call_target="tpu_custom_call" | custom-call | tf_op jit(solution)/shard_map/pallas_call | solution.py:250
  65.4 49.0 %shard_map.95 = (bf16[128,1024]{1,0:T(8,128)(2,1)}, f32[128,256]{1,0:T(8,128)}, bf16[16,8192]{1,0:T(8,128)(2,1)}) custom-call(bf16[128,1024]{1,0:T(8,128)(2,1)} %q_ref.3, bf16[128,1024]{1,0:T(8,128)(2,1)} %get-tuple-element.18.g_ref, bf16[128,1024]{1,0:T(8,128)(2,1)} %get-tuple-element.24.o_ref, bf16[32,128,256]{2,1,0:T(8,128)(2,1)} %get-tuple-element.19.kv_ref, ...), custom_call_target="tpu_custom_call" | custom-call | tf_op jit(solution)/shard_map/pallas_call | solution.py:359
  114.4 0.9 convert.4
  115.3 0.6 fusion
  115.9 1.7 %copy.12 = bf16[16,8192]{1,0:T(8,128)(2,1)} copy(bf16[16,8192]{1,0:T(8,128)(2,1)} %get-tuple-element.38) | data formatting | bytes 524288
  117.6 1.7 %copy.13 = bf16[128,1024]{1,0:T(8,128)(2,1)} copy(bf16[128,1024]{1,0:T(8,128)(2,1)} %get-tuple-element.39) | data formatting | bytes 524288

commit v12 on v11

--- a/solution.py
+++ b/solution.py
@@ -114,9 +114,9 @@
     rlab_ref[...] = label_of(rpos)
 
 
-def gather_kernel(n, t, src_ref, og_ref, so_ref, seg_ref, out_ref, grad_ref,
+def gather_kernel(n, t, k_ref, v_ref, og_ref, so_ref, seg_ref, out_ref, grad_ref,
                   rpos_ref, rlab_ref, cpos_ref, clab_ref, cgrid_ref, lgrid_ref,
-                  send_sem, recv_sem, gsend_sem, grecv_sem):
+                  send_sem, recv_sem, vsend_sem, vrecv_sem, gsend_sem, grecv_sem):
     me = lax.axis_index("ctx")
     mt = lax.axis_index("tp")
     greet_all(n, me, t, mt)
@@ -132,38 +132,48 @@
     grad_start, grad_finish = tp_exchange(t, mt, grad_src, grad_dst, gsend_sem, grecv_sem)
     grad_start()
 
-    def copy_to(peer):
-        return pltpu.make_async_remote_copy(
-            src_ref, out_ref.at[me], send_sem.at[peer], recv_sem.at[me],
-            device_id={"ctx": peer}, device_id_type=MESH)
-
-    def copy_from(src):
-        return pltpu.make_async_remote_copy(
-            src_ref, out_ref.at[src], send_sem.at[src], recv_sem.at[src],
-            device_id={"ctx": src}, device_id_type=MESH)
+    width = k_ref.shape[1]
+
+    def copies(dst, peer, slot):
+        return (
+            pltpu.make_async_remote_copy(
+                k_ref, out_ref.at[dst, :, :width], send_sem.at[slot], recv_sem.at[dst],
+                device_id={"ctx": peer}, device_id_type=MESH),
+            pltpu.make_async_remote_copy(
+                v_ref, out_ref.at[dst, :, width:], vsend_sem.at[slot], vrecv_sem.at[dst],
+                device_id={"ctx": peer}, device_id_type=MESH),
+        )
 
     def send(i, c):
-        copy_to(ctx_peer(me, i, n, 1)).start()
+        peer = ctx_peer(me, i, n, 1)
+        for copy in copies(me, peer, peer):
+            copy.start()
         return c
 
     lax.fori_loop(1, n, send, 0)
-    out_ref[me] = src_ref[...]
+    out_ref[me, :, :width] = k_ref[...]
+    out_ref[me, :, width:] = v_ref[...]
     mask_vectors(me, grad_ref.shape[1] // HEAD_DIM, so_ref, seg_ref,
                  rpos_ref, rlab_ref, cpos_ref, clab_ref, cgrid_ref, lgrid_ref)
     grad_ref[pl.ds(pl.multiple_of(mt * rows, rows), rows), :] = og_ref[
         :, pl.ds(pl.multiple_of(mt * cols, cols), cols)]
 
     def wait(i, c):
-        copy_to(ctx_peer(me, i, n, 1)).wait_send()
-        copy_from(ctx_peer(me, i, n, -1)).wait_recv()
+        peer = ctx_peer(me, i, n, 1)
+        for copy in copies(me, peer, peer):
+            copy.wait_send()
+        src = ctx_peer(me, i, n, -1)
+        for copy in copies(src, src, src):
+            copy.wait_recv()
         return c
 
     lax.fori_loop(1, n, wait, 0)
     grad_finish()
 
 
-def ctx_gather(block, out_grad, span_order, segment_ids, n, t):
-    rows, width = block.shape
+def ctx_gather(key_rows, value_rows, out_grad, span_order, segment_ids, n, t):
+    rows = key_rows.shape[0]
+    width = key_rows.shape[1] + value_rows.shape[1]
     grad_shape = (out_grad.shape[0] * t, out_grad.shape[1] // t)
     stacked = rows * (grad_shape[1] // HEAD_DIM)
     seg = segment_ids.reshape(n, segment_ids.shape[0] // n)
@@ -173,17 +183,16 @@
     return pl.pallas_call(
         functools.partial(gather_kernel, n, t),
         out_shape=(
-            jax.ShapeDtypeStruct((n, rows, width), block.dtype),
+            jax.ShapeDtypeStruct((n, rows, width), key_rows.dtype),
             jax.ShapeDtypeStruct(grad_shape, out_grad.dtype),
             row, row, column, column, grid, grid,
         ),
-        in_specs=[pl.BlockSpec(memory_space=pltpu.VMEM)] * 2
+        in_specs=[pl.BlockSpec(memory_space=pltpu.VMEM)] * 3
         + [pl.BlockSpec(memory_space=pltpu.SMEM), pl.BlockSpec(memory_space=pltpu.VMEM)],
         out_specs=(pl.BlockSpec(memory_space=pltpu.VMEM),) * 8,
-        scratch_shapes=[pltpu.SemaphoreType.DMA((n,)), pltpu.SemaphoreType.DMA((n,)),
-                        pltpu.SemaphoreType.DMA((t,)), pltpu.SemaphoreType.DMA((t,))],
+        scratch_shapes=[pltpu.SemaphoreType.DMA((n,))] * 4 + [pltpu.SemaphoreType.DMA((t,))] * 2,
         compiler_params=pltpu.CompilerParams(collective_id=0, has_side_effects=True),
-    )(block, out_grad, span_order, seg)
+    )(key_rows, value_rows, out_grad, span_order, seg)
 
 
 KEY_BLOCK = 1024
@@ -384,10 +393,9 @@
     local_rows = query_rows.shape[0]
     heads_here = query_rows.shape[1] // HEAD_DIM
     total_rows = local_rows * ctx_size
-    kv_local = jnp.concatenate([key_rows, value_rows], axis=1)
     tp_size = lax.axis_size("tp")
     kv_all, grad_rows, rpos, rlab, cpos_row, clab_row, cpos, clab = ctx_gather(
-        kv_local, out_grad, span_order, segment_ids, ctx_size, tp_size)
+        key_rows, value_rows, out_grad, span_order, segment_ids, ctx_size, tp_size)
     attn_local, row_max, total = attention_fwd(
         query_rows, kv_all.reshape(total_rows, kv_all.shape[2]), rpos, rlab, cpos_row, clab_row)
     query_grad, reduced, attn_spread = bwd_scatter(

time: 120 us -> 119 us (level)
  other arithmetic: 2.33 us -> 0.91 us
    concatenate x1 -> x0, other arithmetic: 1.41 us -> none  [on_device(): kv_local = jnp.concatenate([key_rows, value_rows], axis=1)]
where the time goes in v12:
time: 119 us
  Pallas kernels  113 us (95%)
  local copies, waits for them, and re-layouts  3.97 us (3%)
    pallas_call x1, Pallas kernels, bwd_scatter(): pl.pallas_call(functools.partial(bwd_scatter_kernel, n, t), out_shape=(ja...  49 us
    pallas_call x1, Pallas kernels, ctx_gather(): pl.pallas_call(functools.partial(gather_kernel, n, t), out_shape=(jax.Sha...  45.3 us
    pallas_call x1, Pallas kernels, attention_fwd(): pl.pallas_call(fwd_kernel, out_shape=(jax.ShapeDtypeStruct(q.shape, jnp.b...  18.8 us
    unnamed x2, local copies, waits for them, and re-layouts  3.34 us

profile of v12, /device:TPU:16, one launch (start us, length us, event | category | flops | bytes accessed | tf_op | source)
XLA Modules:
  0.0 118.6 jit_solution(5050902942498609115)
XLA Ops:
  0.6 45.3 %shard_map.93 = (bf16[32,128,256]{2,1,0:T(8,128)(2,1)}, bf16[128,1024]{1,0:T(8,128)(2,1)}, s32[1024,1]{1,0:T(8,128)}, s32[1024,1]{1,0:T(8,128)}, s32[1,4096]{1,0...) custom-call(bf16[128,128]{1,0:T(8,128)(2,1)} %k_ref.1, bf16[128,128]{1,0:T(8,128)(2,1)} %v_ref.1, ...), custom_call_target="tpu_custom_call" | custom-call | tf_op jit(solution)/shard_map/pallas_call | solution.py:183
  45.9 18.8 %shard_map.94 = (bf16[128,1024]{1,0:T(8,128)(2,1)}, f32[1024,1]{1,0:T(8,128)}, f32[1024,1]{1,0:T(8,128)}) custom-call(bf16[128,1024]{1,0:T(8,128)(2,1)} %q_ref.3, bf16[4096,256]{1,0:T(8,128)(2,1)} %bitcast.2, s32[1024,1]{1,0:T(8,128)} %get-tuple-element.20.rpos_ref, s32[1024,1]{1,0:T(8,128)} %get-tuple-element.21.rlab_ref, ...), custom_call_target="tpu_custom_call" | custom-call | tf_op jit(solution)/shard_map/pallas_call | solution.py:259
  64.7 49.0 %shard_map.95 = (bf16[128,1024]{1,0:T(8,128)(2,1)}, f32[128,256]{1,0:T(8,128)}, bf16[16,8192]{1,0:T(8,128)(2,1)}) custom-call(bf16[128,1024]{1,0:T(8,128)(2,1)} %q_ref.3, bf16[128,1024]{1,0:T(8,128)(2,1)} %get-tuple-element.18.g_ref, bf16[128,1024]{1,0:T(8,128)(2,1)} %get-tuple-element.24.o_ref, bf16[32,128,256]{2,1,0:T(8,128)(2,1)} %get-tuple-element.19.kv_ref, ...), custom_call_target="tpu_custom_call" | custom-call | tf_op jit(solution)/shard_map/pallas_call | solution.py:368
  113.8 0.9 convert.4
  114.7 0.6 fusion
  115.3 1.7 %copy.12 = bf16[16,8192]{1,0:T(8,128)(2,1)} copy(bf16[16,8192]{1,0:T(8,128)(2,1)} %get-tuple-element.38) | data formatting | bytes 524288
  117.0 1.7 %copy.13 = bf16[128,1024]{1,0:T(8,128)(2,1)} copy(bf16[128,1024]{1,0:T(8,128)(2,1)} %get-tuple-element.39) | data formatting | bytes 524288

commit v13 on v12

--- a/solution.py
+++ b/solution.py
@@ -196,6 +196,7 @@
 
 
 KEY_BLOCK = 1024
+FWD_GROUP = 8
 NT_DIMS = (((1,), (1,)), ((), ()))
 TN_DIMS = (((0,), (0,)), ((), ()))
 
@@ -275,12 +276,46 @@
     return (cpos <= rpos) & ((clab == 0) | (clab == rlab))
 
 
-def bwd_scatter_kernel(n, t, q_ref, g_ref, o_ref, kv_ref, rpos_ref, rlab_ref, cpos_ref, clab_ref,
-                       m_ref, l_ref, dq_ref, red_ref, spread_ref, terms_sc, held, dq_sc, send_sem, recv_sem,
-                       osend_sem, orecv_sem):
+def fwd_groups(n, queries, kv_ref, cpos_ref, clab_ref, rpos, rlab, m_ref, l_ref, acc_sc, o_ref):
+    scale = 1.0 / math.sqrt(HEAD_DIM)
+    group = math.gcd(n, FWD_GROUP)
+    m_ref[...] = jnp.full(m_ref.shape, -jnp.inf, jnp.float32)
+    l_ref[...] = jnp.zeros(l_ref.shape, jnp.float32)
+    acc_sc[...] = jnp.zeros(acc_sc.shape, jnp.float32)
+
+    def body(j, c):
+        first = j * group
+        block = jnp.concatenate([kv_ref[first + b] for b in range(group)], axis=0)
+        cpos = jnp.concatenate([cpos_ref[pl.ds(first + b, 1), :] for b in range(group)], axis=1)
+        clab = jnp.concatenate([clab_ref[pl.ds(first + b, 1), :] for b in range(group)], axis=1)
+        visible = (cpos <= rpos) & ((clab == 0) | (clab == rlab))
+        keys = block[:, :HEAD_DIM]
+        values = block[:, HEAD_DIM:]
+        scores = lax.dot_general(queries, keys, NT_DIMS, preferred_element_type=jnp.float32) * scale
+        scores = jnp.where(visible, scores, -jnp.inf)
+        running = m_ref[...]
+        new_max = jnp.maximum(running, jnp.max(scores, axis=-1, keepdims=True))
+        shift = jnp.where(new_max == -jnp.inf, 0.0, new_max)
+        factor = jnp.exp(running - shift)
+        weights = jnp.exp(scores - shift)
+        l_ref[...] = l_ref[...] * factor + jnp.sum(weights, axis=-1, keepdims=True)
+        acc_sc[...] = acc_sc[...] * factor + jnp.dot(
+            weights.astype(jnp.bfloat16), values, preferred_element_type=jnp.float32)
+        m_ref[...] = new_max
+        return c
+
+    lax.fori_loop(0, n // group, body, 0)
+    unstack_heads(o_ref, (acc_sc[...] / l_ref[...]).astype(o_ref.dtype))
+
+
+def bwd_scatter_kernel(n, t, q_ref, g_ref, kv_ref, rpos_ref, rlab_ref, cpos_ref, clab_ref,
+                       dq_ref, red_ref, spread_ref, o_ref, m_ref, l_ref, terms_sc, held, dq_sc,
+                       send_sem, recv_sem, osend_sem, orecv_sem):
     me = lax.axis_index("ctx")
     mt = lax.axis_index("tp")
     greet_all(n, me, t, mt)
+    fwd_groups(n, stack_heads(q_ref), kv_ref, cpos_ref, clab_ref, rpos_ref[...], rlab_ref[...],
+               m_ref, l_ref, dq_sc, o_ref)
     rows = spread_ref.shape[0]
     cols = o_ref.shape[1]
 
@@ -362,7 +397,7 @@
     out_finish()
 
 
-def bwd_scatter(q, g, o, kv, rpos, rlab, cpos, clab, m, l, n, t):
+def bwd_scatter(q, g, kv, rpos, rlab, cpos, clab, n, t):
     _, rows, width = kv.shape
     stacked = rpos.shape[0]
     return pl.pallas_call(
@@ -370,11 +405,14 @@
         out_shape=(
             jax.ShapeDtypeStruct(q.shape, jnp.bfloat16),
             jax.ShapeDtypeStruct((rows, width), jnp.float32),
-            jax.ShapeDtypeStruct((o.shape[0] // t, o.shape[1] * t), o.dtype),
+            jax.ShapeDtypeStruct((q.shape[0] // t, q.shape[1] * t), jnp.bfloat16),
         ),
-        in_specs=vmem_specs(10),
+        in_specs=vmem_specs(7),
         out_specs=tuple(vmem_specs(3)),
         scratch_shapes=[
+            pltpu.VMEM(q.shape, jnp.bfloat16),
+            pltpu.VMEM((stacked, 1), jnp.float32),
+            pltpu.VMEM((stacked, 1), jnp.float32),
             pltpu.VMEM(kv.shape, jnp.bfloat16),
             pltpu.VMEM(kv.shape, jnp.bfloat16),
             pltpu.VMEM((stacked, HEAD_DIM), jnp.float32),
@@ -384,7 +422,7 @@
             pltpu.SemaphoreType.DMA((t,)),
         ],
         compiler_params=pltpu.CompilerParams(collective_id=1, has_side_effects=True),
-    )(q, g, o, kv, rpos, rlab, cpos, clab, m, l)
+    )(q, g, kv, rpos, rlab, cpos, clab)
 
 
 def on_device(query_rows, key_rows, value_rows, out_grad, segment_ids, span_order):
@@ -396,11 +434,8 @@
     tp_size = lax.axis_size("tp")
     kv_all, grad_rows, rpos, rlab, cpos_row, clab_row, cpos, clab = ctx_gather(
         key_rows, value_rows, out_grad, span_order, segment_ids, ctx_size, tp_size)
-    attn_local, row_max, total = attention_fwd(
-        query_rows, kv_all.reshape(total_rows, kv_all.shape[2]), rpos, rlab, cpos_row, clab_row)
     query_grad, reduced, attn_spread = bwd_scatter(
-        query_rows, grad_rows, attn_local, kv_all, rpos, rlab, cpos, clab, row_max, total,
-        ctx_size, tp_size)
+        query_rows, grad_rows, kv_all, rpos, rlab, cpos, clab, ctx_size, tp_size)
     key_grad = reduced[:, :HEAD_DIM].astype(jnp.bfloat16)
     value_grad = reduced[:, HEAD_DIM:].astype(jnp.bfloat16)
     return (attn_spread, query_grad, key_grad, value_grad)

time: 119 us -> 116 us (0.975)
  Pallas kernels: 113 us -> 110 us
    pallas_call x1 -> x0, Pallas kernels: 18.8 us -> none  [attention_fwd(): pl.pallas_call(fwd_kernel, out_shape=(jax.ShapeDtypeStruct(q.shape, jnp.b...]
    pallas_call x1, Pallas kernels: 49 us -> 64.9 us  [bwd_scatter(): pl.pallas_call(functools.partial(bwd_scatter_kernel, n, t), out_shape=(ja...]
where the time goes in v13:
time: 116 us
  Pallas kernels  110 us (95%)
  local copies, waits for them, and re-layouts  3.97 us (3%)
    pallas_call x1, Pallas kernels, bwd_scatter(): pl.pallas_call(functools.partial(bwd_scatter_kernel, n, t), out_shape=(ja...  64.9 us
    pallas_call x1, Pallas kernels, ctx_gather(): pl.pallas_call(functools.partial(gather_kernel, n, t), out_shape=(jax.Sha...  45.3 us
    unnamed x2, local copies, waits for them, and re-layouts  3.34 us

profile of v13, /device:TPU:16, one launch (start us, length us, event | category | flops | bytes accessed | tf_op | source)
XLA Modules:
  0.0 115.7 jit_solution(11253582646445209208)
XLA Ops:
  0.6 45.3 %shard_map.93 = (bf16[32,128,256]{2,1,0:T(8,128)(2,1)}, bf16[128,1024]{1,0:T(8,128)(2,1)}, s32[1024,1]{1,0:T(8,128)}, s32[1024,1]{1,0:T(8,128)}, s32[1,4096]{1,0...) custom-call(bf16[128,128]{1,0:T(8,128)(2,1)} %k_ref.1, bf16[128,128]{1,0:T(8,128)(2,1)} %v_ref.1, ...), custom_call_target="tpu_custom_call" | custom-call | tf_op jit(solution)/shard_map/pallas_call | solution.py:183
  45.9 64.9 %shard_map.94 = (bf16[128,1024]{1,0:T(8,128)(2,1)}, f32[128,256]{1,0:T(8,128)}, bf16[16,8192]{1,0:T(8,128)(2,1)}) custom-call(bf16[128,1024]{1,0:T(8,128)(2,1)} %q_ref.1, bf16[128,1024]{1,0:T(8,128)(2,1)} %get-tuple-element.13.g_ref, bf16[32,128,256]{2,1,0:T(8,128)(2,1)} %get-tuple-element.14.kv_ref, s32[1024,1]{1,0:T(8,128)} %get-tuple-element.15.rpos_ref, ...), custom_call_target="tpu_custom_call" | custom-call | tf_op jit(solution)/shard_map/pallas_call | solution.py:403
  110.8 0.9 convert.4
  111.7 0.6 fusion
  112.3 1.7 %copy.12 = bf16[16,8192]{1,0:T(8,128)(2,1)} copy(bf16[16,8192]{1,0:T(8,128)(2,1)} %get-tuple-element.28) | data formatting | bytes 524288
  114.0 1.7 %copy.13 = bf16[128,1024]{1,0:T(8,128)(2,1)} copy(bf16[128,1024]{1,0:T(8,128)(2,1)} %get-tuple-element.29) | data formatting | bytes 524288

commit v14 on v13

--- a/solution.py
+++ b/solution.py
@@ -309,7 +309,7 @@
 
 
 def bwd_scatter_kernel(n, t, q_ref, g_ref, kv_ref, rpos_ref, rlab_ref, cpos_ref, clab_ref,
-                       dq_ref, red_ref, spread_ref, o_ref, m_ref, l_ref, terms_sc, held, dq_sc,
+                       dq_ref, kg_ref, vg_ref, spread_ref, o_ref, m_ref, l_ref, red_ref, terms_sc, held, dq_sc,
                        send_sem, recv_sem, osend_sem, orecv_sem):
     me = lax.axis_index("ctx")
     mt = lax.axis_index("tp")
@@ -388,6 +388,8 @@
         return c
 
     lax.fori_loop(1, n, arrive, 0)
+    kg_ref[...] = red_ref[:, :HEAD_DIM].astype(kg_ref.dtype)
+    vg_ref[...] = red_ref[:, HEAD_DIM:].astype(vg_ref.dtype)
 
     def drain(i, c):
         copy_to(ctx_peer(me, i, n, 1)).wait_send()
@@ -404,15 +406,17 @@
         functools.partial(bwd_scatter_kernel, n, t),
         out_shape=(
             jax.ShapeDtypeStruct(q.shape, jnp.bfloat16),
-            jax.ShapeDtypeStruct((rows, width), jnp.float32),
+            jax.ShapeDtypeStruct((rows, HEAD_DIM), jnp.bfloat16),
+            jax.ShapeDtypeStruct((rows, width - HEAD_DIM), jnp.bfloat16),
             jax.ShapeDtypeStruct((q.shape[0] // t, q.shape[1] * t), jnp.bfloat16),
         ),
         in_specs=vmem_specs(7),
-        out_specs=tuple(vmem_specs(3)),
+        out_specs=tuple(vmem_specs(4)),
         scratch_shapes=[
             pltpu.VMEM(q.shape, jnp.bfloat16),
             pltpu.VMEM((stacked, 1), jnp.float32),
             pltpu.VMEM((stacked, 1), jnp.float32),
+            pltpu.VMEM((rows, width), jnp.float32),
             pltpu.VMEM(kv.shape, jnp.bfloat16),
             pltpu.VMEM(kv.shape, jnp.bfloat16),
             pltpu.VMEM((stacked, HEAD_DIM), jnp.float32),
@@ -434,10 +438,8 @@
     tp_size = lax.axis_size("tp")
     kv_all, grad_rows, rpos, rlab, cpos_row, clab_row, cpos, clab = ctx_gather(
         key_rows, value_rows, out_grad, span_order, segment_ids, ctx_size, tp_size)
-    query_grad, reduced, attn_spread = bwd_scatter(
+    query_grad, key_grad, value_grad, attn_spread = bwd_scatter(
         query_rows, grad_rows, kv_all, rpos, rlab, cpos, clab, ctx_size, tp_size)
-    key_grad = reduced[:, :HEAD_DIM].astype(jnp.bfloat16)
-    value_grad = reduced[:, HEAD_DIM:].astype(jnp.bfloat16)
     return (attn_spread, query_grad, key_grad, value_grad)
 
 

time: 116 us -> 117 us (level)
  local copies, waits for them, and re-layouts: 3.97 us -> 6.09 us
    unnamed x2 -> x4, local copies, waits for them, and re-layouts: 3.34 us -> 6.09 us
where the time goes in v14:
time: 117 us
  Pallas kernels  110 us (94%)
  local copies, waits for them, and re-layouts  6.09 us (5%)
    pallas_call x1, Pallas kernels, bwd_scatter(): pl.pallas_call(functools.partial(bwd_scatter_kernel, n, t), out_shape=(ja...  64.5 us
    pallas_call x1, Pallas kernels, ctx_gather(): pl.pallas_call(functools.partial(gather_kernel, n, t), out_shape=(jax.Sha...  45.3 us
    unnamed x4, local copies, waits for them, and re-layouts  6.09 us

profile of v14, /device:TPU:16, one launch (start us, length us, event | category | flops | bytes accessed | tf_op | source)
XLA Modules:
  0.0 116.6 jit_solution(10144957852089708174)
XLA Ops:
  0.6 45.3 %shard_map.93 = (bf16[32,128,256]{2,1,0:T(8,128)(2,1)}, bf16[128,1024]{1,0:T(8,128)(2,1)}, s32[1024,1]{1,0:T(8,128)}, s32[1024,1]{1,0:T(8,128)}, s32[1,4096]{1,0...) custom-call(bf16[128,128]{1,0:T(8,128)(2,1)} %k_ref.1, bf16[128,128]{1,0:T(8,128)(2,1)} %v_ref.1, ...), custom_call_target="tpu_custom_call" | custom-call | tf_op jit(solution)/shard_map/pallas_call | solution.py:183
  45.9 64.5 %shard_map.94 = (bf16[128,1024]{1,0:T(8,128)(2,1)}, bf16[128,128]{1,0:T(8,128)(2,1)}, bf16[128,128]{1,0:T(8,128)(2,1)}, bf16[16,8192]{1,0:T(8,128)(2,1)}) custom-call(bf16[128,1024]{1,0:T(8,128)(2,1)} %q_ref.1, bf16[128,1024]{1,0:T(8,128)(2,1)} %get-tuple-element.14.g_ref, bf16[32,128,256]{2,1,0:T(8,128)(2,1)} %get-tuple-element.15.kv_ref, ...), custom_call_target="tpu_custom_call" | custom-call | tf_op jit(solution)/shard_map/pallas_call | solution.py:405
  110.5 1.7 %copy.14 = bf16[16,8192]{1,0:T(8,128)(2,1)} copy(bf16[16,8192]{1,0:T(8,128)(2,1)} %get-tuple-element.28) | data formatting | bytes 524288
  112.1 1.7 %copy.15 = bf16[128,1024]{1,0:T(8,128)(2,1)} copy(bf16[128,1024]{1,0:T(8,128)(2,1)} %get-tuple-element.29) | data formatting | bytes 524288
  113.8 1.4 %copy.16 = bf16[128,128]{1,0:T(8,128)(2,1)} copy(bf16[128,128]{1,0:T(8,128)(2,1)} %get-tuple-element.30) | data formatting | bytes 65536
  115.2 1.4 %copy.17 = bf16[128,128]{1,0:T(8,128)(2,1)} copy(bf16[128,128]{1,0:T(8,128)(2,1)} %get-tuple-element.31) | data formatting | bytes 65536

commit v15 on v13

--- a/solution.py
+++ b/solution.py
@@ -379,7 +379,7 @@
 
     lax.fori_loop(1, n, step, 0)
     copy_to(ctx_peer(me, n - 1, n, 1)).start()
-    unstack_heads(dq_ref, (dq_sc[...] * scale).astype(dq_ref.dtype))
+    dq_ref[...] = dq_sc[...] * scale
 
     def arrive(i, c):
         src = ctx_peer(me, i, n, -1)
@@ -403,7 +403,7 @@
     return pl.pallas_call(
         functools.partial(bwd_scatter_kernel, n, t),
         out_shape=(
-            jax.ShapeDtypeStruct(q.shape, jnp.bfloat16),
+            jax.ShapeDtypeStruct((stacked, HEAD_DIM), jnp.float32),
             jax.ShapeDtypeStruct((rows, width), jnp.float32),
             jax.ShapeDtypeStruct((q.shape[0] // t, q.shape[1] * t), jnp.bfloat16),
         ),
@@ -434,10 +434,13 @@
     tp_size = lax.axis_size("tp")
     kv_all, grad_rows, rpos, rlab, cpos_row, clab_row, cpos, clab = ctx_gather(
         key_rows, value_rows, out_grad, span_order, segment_ids, ctx_size, tp_size)
-    query_grad, reduced, attn_spread = bwd_scatter(
+    stacked_grad, reduced, attn_spread = bwd_scatter(
         query_rows, grad_rows, kv_all, rpos, rlab, cpos, clab, ctx_size, tp_size)
     key_grad = reduced[:, :HEAD_DIM].astype(jnp.bfloat16)
     value_grad = reduced[:, HEAD_DIM:].astype(jnp.bfloat16)
+    query_grad = jnp.transpose(
+        stacked_grad.astype(jnp.bfloat16).reshape(heads_here, local_rows, HEAD_DIM), (1, 0, 2)
+    ).reshape(local_rows, heads_here * HEAD_DIM)
     return (attn_spread, query_grad, key_grad, value_grad)
 
 

time: 116 us -> 116 us (level)
    unnamed x2 -> x1, local copies, waits for them, and re-layouts: 3.34 us -> 1.67 us
where the time goes in v15:
time: 116 us
  Pallas kernels  110 us (95%)
  local copies, waits for them, and re-layouts  3.07 us (3%)
  other arithmetic  1.98 us (2%)
    pallas_call x1, Pallas kernels, bwd_scatter(): pl.pallas_call(functools.partial(bwd_scatter_kernel, n, t), out_shape=(ja...  64.9 us
    pallas_call x1, Pallas kernels, ctx_gather(): pl.pallas_call(functools.partial(gather_kernel, n, t), out_shape=(jax.Sha...  45.3 us

profile of v15, /device:TPU:16, one launch (start us, length us, event | category | flops | bytes accessed | tf_op | source)
XLA Modules:
  0.0 115.8 jit_solution(13673187373406053917)
XLA Ops:
  0.6 45.3 %shard_map.93 = (bf16[32,128,256]{2,1,0:T(8,128)(2,1)}, bf16[128,1024]{1,0:T(8,128)(2,1)}, s32[1024,1]{1,0:T(8,128)}, s32[1024,1]{1,0:T(8,128)}, s32[1,4096]{1,0...) custom-call(bf16[128,128]{1,0:T(8,128)(2,1)} %k_ref.1, bf16[128,128]{1,0:T(8,128)(2,1)} %v_ref.1, ...), custom_call_target="tpu_custom_call" | custom-call | tf_op jit(solution)/shard_map/pallas_call | solution.py:183
  45.9 64.9 %shard_map.94 = (f32[1024,128]{1,0:T(8,128)}, f32[128,256]{1,0:T(8,128)}, bf16[16,8192]{1,0:T(8,128)(2,1)}) custom-call(bf16[128,1024]{1,0:T(8,128)(2,1)} %q_ref.1, bf16[128,1024]{1,0:T(8,128)(2,1)} %get-tuple-element.13.g_ref, bf16[32,128,256]{2,1,0:T(8,128)(2,1)} %get-tuple-element.14.kv_ref, s32[1024,1]{1,0:T(8,128)} %get-tuple-element.15.rpos_ref, ...), custom_call_target="tpu_custom_call" | custom-call | tf_op jit(solution)/shard_map/pallas_call | solution.py:403
  110.8 0.9 convert.4
  111.7 0.6 fusion
  112.3 1.1 convert_element_type.2
  113.4 0.8 copy.13
  114.1 1.7 %copy.15 = bf16[16,8192]{1,0:T(8,128)(2,1)} copy(bf16[16,8192]{1,0:T(8,128)(2,1)} %get-tuple-element.28) | data formatting | bytes 524288

commit v16 on v13

--- a/solution.py
+++ b/solution.py
@@ -196,7 +196,7 @@
 
 
 KEY_BLOCK = 1024
-FWD_GROUP = 8
+FWD_GROUP = 16
 NT_DIMS = (((1,), (1,)), ((), ()))
 TN_DIMS = (((0,), (0,)), ((), ()))
 

time: 116 us -> 110 us (0.948)
  Pallas kernels: 110 us -> 104 us
    pallas_call x1, Pallas kernels: 64.9 us -> 58.7 us  [bwd_scatter(): pl.pallas_call(functools.partial(bwd_scatter_kernel, n, t), out_shape=(ja...]
where the time goes in v16:
time: 110 us
  Pallas kernels  104 us (95%)
  local copies, waits for them, and re-layouts  3.97 us (4%)
    pallas_call x1, Pallas kernels, bwd_scatter(): pl.pallas_call(functools.partial(bwd_scatter_kernel, n, t), out_shape=(ja...  58.7 us
    pallas_call x1, Pallas kernels, ctx_gather(): pl.pallas_call(functools.partial(gather_kernel, n, t), out_shape=(jax.Sha...  45.3 us
    unnamed x2, local copies, waits for them, and re-layouts  3.34 us

profile of v16, /device:TPU:16, one launch (start us, length us, event | category | flops | bytes accessed | tf_op | source)
XLA Modules:
  0.0 109.5 jit_solution(6938697424959511540)
XLA Ops:
  0.6 45.3 %shard_map.93 = (bf16[32,128,256]{2,1,0:T(8,128)(2,1)}, bf16[128,1024]{1,0:T(8,128)(2,1)}, s32[1024,1]{1,0:T(8,128)}, s32[1024,1]{1,0:T(8,128)}, s32[1,4096]{1,0...) custom-call(bf16[128,128]{1,0:T(8,128)(2,1)} %k_ref.1, bf16[128,128]{1,0:T(8,128)(2,1)} %v_ref.1, ...), custom_call_target="tpu_custom_call" | custom-call | tf_op jit(solution)/shard_map/pallas_call | solution.py:183
  45.9 58.7 %shard_map.94 = (bf16[128,1024]{1,0:T(8,128)(2,1)}, f32[128,256]{1,0:T(8,128)}, bf16[16,8192]{1,0:T(8,128)(2,1)}) custom-call(bf16[128,1024]{1,0:T(8,128)(2,1)} %q_ref.1, bf16[128,1024]{1,0:T(8,128)(2,1)} %get-tuple-element.13.g_ref, bf16[32,128,256]{2,1,0:T(8,128)(2,1)} %get-tuple-element.14.kv_ref, s32[1024,1]{1,0:T(8,128)} %get-tuple-element.15.rpos_ref, ...), custom_call_target="tpu_custom_call" | custom-call | tf_op jit(solution)/shard_map/pallas_call | solution.py:403
  104.6 0.9 convert.4
  105.5 0.6 fusion
  106.2 1.7 %copy.12 = bf16[16,8192]{1,0:T(8,128)(2,1)} copy(bf16[16,8192]{1,0:T(8,128)(2,1)} %get-tuple-element.28) | data formatting | bytes 524288
  107.8 1.7 %copy.13 = bf16[128,1024]{1,0:T(8,128)(2,1)} copy(bf16[128,1024]{1,0:T(8,128)(2,1)} %get-tuple-element.29) | data formatting | bytes 524288
